TPU v7x, 256 devices: a whole 4x4x8 slice. The times are simulated.
256 devices in a mesh: section: 2 (over y_hi), sx: 16 (over z, core), sy: 8 (over y_lo, x).
Axes of the slice: x: 4, y: 4 (y_hi: 2, y_lo: 2; y = y_hi * 2 + y_lo), z: 8, core: 2. Of those that a mesh axis runs over, the one named last changes fastest.
Arguments:
- previous: float32 [16, 256, 1024], P(None, 'sx', 'sy'), may hold values from -3 to 3
- sections: float32 [4, 16, 256, 1024], P('section', None, 'sx', 'sy'), may hold values from -3 to 3
- diffusivity: float32 [16, 256, 1024], P(None, 'sx', 'sy'), may hold values from 0.3 to 3
- reaction: float32 [16, 256, 1024], P(None, 'sx', 'sy'), may hold values from 0.2 to 2
Outputs:
- updated: float32 [4, 16, 256, 1024], P('section', None, 'sx', 'sy')
All inputs are finite; a program needn't handle non-finite values.
Results may differ from a plain program's by a relative error of at most 0.0003.
Values sent between devices are 32-bit elements; how exact they have to be, the bound alone decides.
No kernel may reach another device: no remote copies, remote signals or barrier semaphores. Data moves between devices by JAX's collectives and lax.ppermute only.
A program may use at most 64 MiB of HBM per device.

v0:
```python
import jax
import jax.numpy as jnp
from jax import lax
from jax.sharding import PartitionSpec as P

ITERS = 4


step_size = 1.0
tiny_value = 1e-06


def extended(cells, sides, width):
    for axis, dim in sides:
        count = lax.axis_size(axis)
        ends = count - 1
        head = lax.slice_in_dim(cells, 0, width, axis=dim)
        tail = lax.slice_in_dim(cells, cells.shape[dim] - width, cells.shape[dim], axis=dim)
        cells = jnp.concatenate(
            [
                lax.ppermute(tail, axis, [(i, (i + 1) % count) for i in range(ends)]),
                cells,
                lax.ppermute(head, axis, [((i + 1) % count, i) for i in range(ends)]),
            ],
            axis=dim,
        )
    return cells


def invert_table(matrix):
    order_n = len(matrix)
    augmented = [
        list(matrix[r]) + [1.0 if c == r else 0.0 for c in range(order_n)] for r in range(order_n)
    ]
    for col in range(order_n):
        pivot_row = max(range(col, order_n), key=lambda r: abs(augmented[r][col]))
        augmented[col], augmented[pivot_row] = (augmented[pivot_row], augmented[col])
        leading = augmented[col][col]
        augmented[col] = [v / leading for v in augmented[col]]
        for r in range(order_n):
            if r != col:
                factor = augmented[r][col]
                augmented[r] = [a - factor * b for a, b in zip(augmented[r], augmented[col])]
    return [row_values[order_n:] for row_values in augmented]


def table_product(left, right):
    return [
        [sum((left[i][k] * right[k][j] for k in range(len(right)))) for j in range(len(right[0]))]
        for i in range(len(left))
    ]


def pair_add(first, second):
    return (first[0] + second[0], first[1] + second[1])


def pair_sub(first, second):
    return (first[0] - second[0], first[1] - second[1])


def pair_mul(first, second):
    return (
        first[0] * second[0] - first[1] * second[1],
        first[0] * second[1] + first[1] * second[0],
    )


def pair_div(first, second):
    scale_sq = second[0] * second[0] + second[1] * second[1]
    return (
        (first[0] * second[0] + first[1] * second[1]) / scale_sq,
        (first[1] * second[0] - first[0] * second[1]) / scale_sq,
    )


def quartic_value(point):
    return (((210.0 * point - 480.0) * point + 360.0) * point - 96.0) * point + 6.0


def bisect_root(lower, upper):
    for count in range(200):
        middle = 0.5 * (lower + upper)
        if (quartic_value(lower) < 0.0) == (quartic_value(middle) < 0.0):
            lower = middle
        else:
            upper = middle
    return 0.5 * (lower + upper)


def radau_tables():
    abscissae = []
    grid_steps = 4000
    for m in range(grid_steps):
        lower = 0.999 * m / grid_steps
        upper = 0.999 * (m + 1) / grid_steps
        if (quartic_value(lower) < 0.0) != (quartic_value(upper) < 0.0):
            abscissae.append(bisect_root(lower, upper))
    abscissae.append(1.0)
    vander = [[abscissae[j] ** k for k in range(4)] for j in range(4)]
    moments = [[abscissae[i] ** (k + 1) / (k + 1) for k in range(4)] for i in range(4)]
    tableau = table_product(moments, invert_table(vander))
    inverse = invert_table(tableau)
    running = [list(row_values) for row_values in inverse]
    coeffs = []
    for k in range(1, 5):
        trace_value = sum((running[i][i] for i in range(4)))
        coeffs.append(-trace_value / k)
        shifted_table = [
            [running[i][j] + (coeffs[-1] if i == j else 0.0) for j in range(4)] for i in range(4)
        ]
        running = table_product(inverse, shifted_table)
    start_point = (0.4, 0.9)
    estimates = [(1.0, 0.0)]
    for k in range(3):
        estimates.append(pair_mul(estimates[-1], start_point))
    for count in range(500):
        for i in range(4):
            value = (1.0, 0.0)
            for coef_value in coeffs:
                value = pair_add(pair_mul(value, estimates[i]), (coef_value, 0.0))
            denom = (1.0, 0.0)
            for j in range(4):
                if j != i:
                    denom = pair_mul(denom, pair_sub(estimates[i], estimates[j]))
            estimates[i] = pair_sub(estimates[i], pair_div(value, denom))
    chosen = [m for m in range(4) if estimates[m][1] > 0.0]
    ranking = sorted(chosen, key=lambda m: -estimates[m][1])
    columns = []
    pairs = []
    for m in ranking:
        eigen_pair = estimates[m]
        system = [
            [
                (
                    inverse[i][j] - (eigen_pair[0] if i == j else 0.0),
                    -(eigen_pair[1] if i == j else 0.0),
                )
                for j in range(4)
            ]
            for i in range(3)
        ]
        rows_left = [
            [system[i][j] for j in range(3)] + [(-system[i][3][0], -system[i][3][1])]
            for i in range(3)
        ]
        for col in range(3):
            pivot_row = max(
                range(col, 3), key=lambda r: rows_left[r][col][0] ** 2 + rows_left[r][col][1] ** 2
            )
            rows_left[col], rows_left[pivot_row] = (rows_left[pivot_row], rows_left[col])
            leading = rows_left[col][col]
            rows_left[col] = [pair_div(v, leading) for v in rows_left[col]]
            for r in range(3):
                if r != col:
                    factor = rows_left[r][col]
                    rows_left[r] = [
                        pair_sub(a, pair_mul(factor, b))
                        for a, b in zip(rows_left[r], rows_left[col])
                    ]
        vector = [rows_left[i][3] for i in range(3)] + [(1.0, 0.0)]
        columns.append([v[0] for v in vector])
        columns.append([v[1] for v in vector])
        pairs.append((eigen_pair[0], eigen_pair[1]))
    eigen_basis = [[columns[j][i] for j in range(4)] for i in range(4)]
    basis_inverse = invert_table(eigen_basis)
    return (tableau, inverse, eigen_basis, basis_inverse, pairs)


def center(padded):
    return padded[..., 1:-1, 1:-1, 1:-1]


def shifted(padded, member):
    if member == 0:
        return padded[..., 2:, 1:-1, 1:-1]
    if member == 1:
        return padded[..., :-2, 1:-1, 1:-1]
    if member == 2:
        return padded[..., 1:-1, 2:, 1:-1]
    if member == 3:
        return padded[..., 1:-1, :-2, 1:-1]
    if member == 4:
        return padded[..., 1:-1, 1:-1, 2:]
    return padded[..., 1:-1, 1:-1, :-2]


def face_terms(padded):
    middle = center(padded)
    return [0.5 * (middle + shifted(padded, m)) for m in range(6)]


def face_total(faces):
    total = faces[0]
    for m in range(1, 6):
        total = total + faces[m]
    return total


def neighbour_sum(faces, padded):
    total = faces[0] * shifted(padded, 0)
    for m in range(1, 6):
        total = total + faces[m] * shifted(padded, m)
    return total


def pad_depth(field, width):
    return jnp.pad(field, [(0, 0)] * (field.ndim - 3) + [(width, width), (0, 0), (0, 0)])


def trim_cells(field, width):
    if width == 0:
        return field
    return field[..., width:-width, width:-width, width:-width]


def apply_inverse(diag_real, coupling, determinant, vector):
    first = (diag_real * vector[0] - coupling * vector[1]) / determinant
    second = (coupling * vector[0] + diag_real * vector[1]) / determinant
    return jnp.stack([first, second])


def apply_block(diag_real, coupling, vector):
    return jnp.stack(
        [diag_real * vector[0] + coupling * vector[1], diag_real * vector[1] - coupling * vector[0]]
    )


def combine(coef, fields):
    total = coef[:, 0][:, None, None, None] * fields[0][None]
    for column in range(1, fields.shape[0]):
        total = total + coef[:, column][:, None, None, None] * fields[column][None]
    return total


def body(previous, sections, diffusivity, reaction):
    tableau, inverse, eigen_basis, basis_inverse, pairs = radau_tables()
    flux_rows = jnp.asarray(basis_inverse, jnp.float32)
    shift_table = table_product(basis_inverse, inverse)
    shift_rows = jnp.asarray(
        [[v / step_size for v in row_values] for row_values in shift_table], jnp.float32
    )
    basis_rows = jnp.asarray(eigen_basis, jnp.float32)
    pair_table = jnp.asarray([list(p) for p in pairs], jnp.float32)
    eigen_block = lax.axis_index("section")
    section_coef = diffusivity * (1.0 + 0.5 * jnp.tanh(sections))
    frozen_coef = diffusivity * (1.0 + 0.5 * jnp.tanh(previous))
    react_slope = reaction * (1.0 - 3.0 * previous * previous)
    coefs = jnp.concatenate([section_coef, frozen_coef[None], react_slope[None]], 0)
    halo_width = 1
    section_pad, coef_pad = (
        extended(sections, (("sx", 2), ("sy", 3)), halo_width),
        extended(coefs, (("sx", 2), ("sy", 3)), halo_width),
    )
    section_pad = pad_depth(section_pad, halo_width)
    coef_pad = pad_depth(coef_pad, halo_width)
    section_near = trim_cells(section_pad, halo_width - 1)
    coef_near = trim_cells(coef_pad, halo_width - 1)
    section_faces = face_terms(coef_near[:2])
    section_flux = neighbour_sum(section_faces, section_near) - face_total(section_faces) * sections
    section_flux = section_flux + reaction * sections * (1.0 - sections * sections)
    increment = sections - previous
    all_flux, all_increment = (
        lax.all_gather(section_flux, "section", axis=0, tiled=True),
        lax.all_gather(increment, "section", axis=0, tiled=True),
    )
    own_flux = lax.dynamic_slice(flux_rows, (2 * eigen_block, 0), (2, 4))
    own_shift = lax.dynamic_slice(shift_rows, (2 * eigen_block, 0), (2, 4))
    rhs = combine(own_flux, all_flux) - combine(own_shift, all_increment)
    faces_region = face_terms(coef_pad[2])
    slope_region = trim_cells(coef_pad[3], 1)
    real_part = pair_table[eigen_block, 0] / step_size
    coupling = pair_table[eigen_block, 1] / step_size
    diag_region = real_part + face_total(faces_region) - slope_region
    det_region = diag_region * diag_region + coupling * coupling
    inner_cut = halo_width - 1
    faces_inner = [trim_cells(face, inner_cut) for face in faces_region]
    diag_inner = trim_cells(diag_region, inner_cut)
    det_inner = trim_cells(det_region, inner_cut)
    residue = rhs
    correction = jnp.zeros_like(residue)
    for sweep in range(ITERS):
        scaled = apply_inverse(diag_inner, coupling, det_inner, residue)
        scaled_pad = extended(scaled, (("sx", 2), ("sy", 3)), halo_width)
        scaled_pad = pad_depth(scaled_pad, halo_width)
        search = scaled + apply_inverse(
            diag_inner, coupling, det_inner, neighbour_sum(faces_inner, scaled_pad)
        )
        search_pad = extended(search, (("sx", 2), ("sy", 3)), 1)
        search_pad = pad_depth(search_pad, 1)
        image = apply_block(diag_inner, coupling, search) - neighbour_sum(faces_inner, search_pad)
        numerator, denominator = lax.psum(
            (jnp.sum(image * residue), jnp.sum(image * image)), ("sx", "sy")
        )
        step_length = numerator / (denominator + tiny_value)
        correction = correction + step_length * search
        residue = residue - step_length * image
    gathered = lax.all_gather(correction, "section", axis=0, tiled=True)
    own_basis = lax.dynamic_slice(basis_rows, (2 * eigen_block, 0), (2, 4))
    return sections + combine(own_basis, gathered)


def solution(mesh):
    in_specs = (
        P(None, "sx", "sy"),
        P("section", None, "sx", "sy"),
        P(None, "sx", "sy"),
        P(None, "sx", "sy"),
    )
    out_specs = P("section", None, "sx", "sy")
    return jax.shard_map(body, mesh=mesh, in_specs=in_specs, out_specs=out_specs, check_vma=False)
```

profile of v0, /device:TPU:1, one launch (start us, length us, event | category | flops | bytes accessed | tf_op | source)
XLA Modules:
  0.0 1346.9 jit_solution(1758878238142489170)
XLA Ops:
  1.8 4.9 collective-permute-start.4
  10.5 9.8 all_gather.10
  25.4 4.7 collective-permute-start
  38.1 4.0 collective-permute-start.2
  52.4 8.5 all_gather.9
  63.8 6.6 collective-permute-start.8
  79.4 4.0 collective-permute-done.10
  83.4 4.4 collective-permute-done.11
  98.1 5.5 collective-permute-start.14
  108.8 4.4 collective-permute-done.15
  115.6 266.2 %all-reduce.13 = (f32[]{:T(128)}, f32[]{:T(128)}) all-reduce(f32[]{:T(128)} %get-tuple-element.12, f32[]{:T(128)} %get-tuple-element.11), channel_id=1, replica_groups=mesh['section'=2,'sx'=16,'sy'=8] {'sx','sy'}, use_global_device_ids=true, to_apply=%region_1.2 | all-reduce | flops 2 | bytes 16 | tf_op jit(solution)/shard_map/psum | solution.py:292
  386.9 13.3 collective-permute-start.17
  403.8 5.0 collective-permute-done.18
  428.9 4.1 collective-permute-done.23
  434.5 264.3 %all-reduce.12 = (f32[]{:T(128)}, f32[]{:T(128)}) all-reduce(f32[]{:T(128)} %get-tuple-element.10, f32[]{:T(128)} %get-tuple-element.9), channel_id=1, replica_groups=mesh['section'=2,'sx'=16,'sy'=8] {'sx','sy'}, use_global_device_ids=true, to_apply=%region_5.6 | all-reduce | flops 2 | bytes 16 | tf_op jit(solution)/shard_map/psum | solution.py:292
  702.9 13.3 collective-permute-start.25
  722.4 4.7 collective-permute-done.26
  747.8 4.1 collective-permute-done.31
  753.4 264.3 %all-reduce.11 = (f32[]{:T(128)}, f32[]{:T(128)}) all-reduce(f32[]{:T(128)} %get-tuple-element.8, f32[]{:T(128)} %get-tuple-element.7), channel_id=1, replica_groups=mesh['section'=2,'sx'=16,'sy'=8] {'sx','sy'}, use_global_device_ids=true, to_apply=%region_9.10 | all-reduce | flops 2 | bytes 16 | tf_op jit(solution)/shard_map/psum | solution.py:292
  1021.8 13.3 collective-permute-start.33
  1041.4 4.6 collective-permute-done.34
  1066.7 4.1 collective-permute-done.39
  1072.3 264.4 %all-reduce.10 = (f32[]{:T(128)}, f32[]{:T(128)}) all-reduce(f32[]{:T(128)} %get-tuple-element.6, f32[]{:T(128)} %get-tuple-element.5), channel_id=1, replica_groups=mesh['section'=2,'sx'=16,'sy'=8] {'sx','sy'}, use_global_device_ids=true, to_apply=%region_13.14 | all-reduce | flops 2 | bytes 16 | tf_op jit(solution)/shard_map/psum | solution.py:292
  1338.3 7.7 all_gather.11
  (198 shorter events, 148.9 us)
Async XLA Ops:
  1.8 23.4 %collective-permute-start.4 = (f32[2,16,1,128]{3,1,2,0:T(8,128)S(1)}, f32[2,16,1,128]{3,1,2,0:T(8,128)S(1)}, u32[]{:S(2)}, u32[]{:S(2)}) collective-permute-start(f32[2,16,1,128]{3,1,2,0:T(8,128)S(1)} %get-tuple-element.109), channel_id=1, source_target_pairs={{0,8},{8,16},{16,24},{24,32},{32,40},{40,48},{48,56},{56,64},{64,7... | collective-permute-start | bytes 49160 | tf_op jit(solution)/shard_map/ppermute | solution.py:21
  6.7 25.3 %collective-permute-start.5 = (f32[2,16,1,128]{3,1,2,0:T(8,128)S(1)}, f32[2,16,1,128]{3,1,2,0:T(8,128)S(1)}, u32[]{:S(2)}, u32[]{:S(2)}) collective-permute-start(f32[2,16,1,128]{3,1,2,0:T(8,128)S(1)} %get-tuple-element.108), channel_id=1, source_target_pairs={{8,0},{16,8},{24,16},{32,24},{40,32},{48,40},{56,48},{64,56},{72,6... | collective-permute-start | bytes 49160 | tf_op jit(solution)/shard_map/ppermute | solution.py:23
  25.4 11.9 collective-permute-start
  32.2 11.7 collective-permute-start.6
  63.8 8.6 collective-permute-start.8
  78.1 9.7 collective-permute-start.11
  98.1 10.8 collective-permute-start.14
  103.5 9.7 collective-permute-start.15
  385.0 15.2 %collective-permute-start.16 = (f32[2,16,1,128]{3,1,2,0:T(8,128)S(1)}, f32[2,16,1,128]{3,1,2,0:T(8,128)S(1)}, u32[]{:S(2)}, u32[]{:S(2)}) collective-permute-start(f32[2,16,1,128]{3,1,2,0:T(8,128)S(1)} %get-tuple-element.100), channel_id=1, source_target_pairs={{0,8},{8,16},{16,24},{24,32},{32,40},{40,48},{48,56},{56,64},{64,7... | collective-permute-start | bytes 49160 | tf_op jit(solution)/shard_map/ppermute | solution.py:21
  386.9 14.1 %collective-permute-start.17 = (f32[2,16,1,128]{3,1,2,0:T(8,128)S(1)}, f32[2,16,1,128]{3,1,2,0:T(8,128)S(1)}, u32[]{:S(2)}, u32[]{:S(2)}) collective-permute-start(f32[2,16,1,128]{3,1,2,0:T(8,128)S(1)} %get-tuple-element.101), channel_id=1, source_target_pairs={{8,0},{16,8},{24,16},{32,24},{40,32},{48,40},{56,48},{64,56},{72,6... | collective-permute-start | bytes 49160 | tf_op jit(solution)/shard_map/ppermute | solution.py:23
  402.5 10.1 collective-permute-start.19
  423.0 9.9 collective-permute-start.23
  700.9 15.2 %collective-permute-start.24 = (f32[2,16,1,128]{3,1,2,0:T(8,128)S(1)}, f32[2,16,1,128]{3,1,2,0:T(8,128)S(1)}, u32[]{:S(2)}, u32[]{:S(2)}) collective-permute-start(f32[2,16,1,128]{3,1,2,0:T(8,128)S(1)} %get-tuple-element.96), channel_id=1, source_target_pairs={{0,8},{8,16},{16,24},{24,32},{32,40},{40,48},{48,56},{56,64},{64,7... | collective-permute-start | bytes 49160 | tf_op jit(solution)/shard_map/ppermute | solution.py:21
  702.9 14.1 %collective-permute-start.25 = (f32[2,16,1,128]{3,1,2,0:T(8,128)S(1)}, f32[2,16,1,128]{3,1,2,0:T(8,128)S(1)}, u32[]{:S(2)}, u32[]{:S(2)}) collective-permute-start(f32[2,16,1,128]{3,1,2,0:T(8,128)S(1)} %get-tuple-element.97), channel_id=1, source_target_pairs={{8,0},{16,8},{24,16},{32,24},{40,32},{48,40},{56,48},{64,56},{72,6... | collective-permute-start | bytes 49160 | tf_op jit(solution)/shard_map/ppermute | solution.py:23
  717.2 9.9 collective-permute-start.26
  721.1 9.8 collective-permute-start.27
  739.7 8.1 collective-permute-start.30
  742.0 9.9 collective-permute-start.31
  1019.9 15.2 %collective-permute-start.32 = (f32[2,16,1,128]{3,1,2,0:T(8,128)S(1)}, f32[2,16,1,128]{3,1,2,0:T(8,128)S(1)}, u32[]{:S(2)}, u32[]{:S(2)}) collective-permute-start(f32[2,16,1,128]{3,1,2,0:T(8,128)S(1)} %get-tuple-element.92), channel_id=1, source_target_pairs={{0,8},{8,16},{16,24},{24,32},{32,40},{40,48},{48,56},{56,64},{64,7... | collective-permute-start | bytes 49160 | tf_op jit(solution)/shard_map/ppermute | solution.py:21
  1021.8 14.1 %collective-permute-start.33 = (f32[2,16,1,128]{3,1,2,0:T(8,128)S(1)}, f32[2,16,1,128]{3,1,2,0:T(8,128)S(1)}, u32[]{:S(2)}, u32[]{:S(2)}) collective-permute-start(f32[2,16,1,128]{3,1,2,0:T(8,128)S(1)} %get-tuple-element.93), channel_id=1, source_target_pairs={{8,0},{16,8},{24,16},{32,24},{40,32},{48,40},{56,48},{64,56},{72,6... | collective-permute-start | bytes 49160 | tf_op jit(solution)/shard_map/ppermute | solution.py:23
  1036.1 9.9 collective-permute-start.34
  1040.0 9.8 collective-permute-start.35
  1058.7 8.1 collective-permute-start.38
  1060.9 9.9 collective-permute-start.39
  (33 other events, 801.9 us)
where the time goes:
time: 1370 us; the launch traced here: 1350 us
  blocking collectives  1090 us (80%)
  starting transfers between devices  131 us (10%)
  waiting for transfers between devices  82.7 us (6%)
  other arithmetic  29.6 us (2%)
    psum x4, blocking collectives, body(): lax.psum((jnp.sum(image * residue), jnp.sum(image * image)), ('sx', 'sy'))  1060 us
    ppermute x20, starting transfers between devices, extended(): lax.ppermute(head, axis, [((i + 1) % count, i) for i in range(ends)])  68.6 us
    ppermute x20, starting transfers between devices, extended(): lax.ppermute(tail, axis, [(i, (i + 1) % count) for i in range(ends)])  62 us
    ppermute x20, waiting for transfers between devices, extended(): lax.ppermute(head, axis, [((i + 1) % count, i) for i in range(ends)])  49.8 us
    ppermute x20, waiting for transfers between devices, extended(): lax.ppermute(tail, axis, [(i, (i + 1) % count) for i in range(ends)])  32.9 us
  transfers between devices with their start and end apart: 40, of which 25 were waited for; matrix products, arithmetic and copies ran while one was open for 1% of the time, Pallas kernels for 0%

commit v1 on v0

v1 whole, which is shorter than its diff:
```python
import functools

import jax
import jax.numpy as jnp
from jax import lax
from jax.experimental import pallas as pl
from jax.experimental.pallas import tpu as pltpu
from jax.sharding import PartitionSpec as P

ITERS = 4
SHIFTS = (0.0, 0.9, 0.45, 0.7)
EDGE = 9
LANES = 128
SIZE = ITERS + 1
PAIRS = [(i, j) for i in range(SIZE) for j in range(i, SIZE)]
VMEM_LIMIT = 58 * 1024 * 1024


step_size = 1.0
tiny_value = 1e-06


def invert_table(matrix):
    order_n = len(matrix)
    augmented = [
        list(matrix[r]) + [1.0 if c == r else 0.0 for c in range(order_n)] for r in range(order_n)
    ]
    for col in range(order_n):
        pivot_row = max(range(col, order_n), key=lambda r: abs(augmented[r][col]))
        augmented[col], augmented[pivot_row] = (augmented[pivot_row], augmented[col])
        leading = augmented[col][col]
        augmented[col] = [v / leading for v in augmented[col]]
        for r in range(order_n):
            if r != col:
                factor = augmented[r][col]
                augmented[r] = [a - factor * b for a, b in zip(augmented[r], augmented[col])]
    return [row_values[order_n:] for row_values in augmented]


def table_product(left, right):
    return [
        [sum((left[i][k] * right[k][j] for k in range(len(right)))) for j in range(len(right[0]))]
        for i in range(len(left))
    ]


def pair_add(first, second):
    return (first[0] + second[0], first[1] + second[1])


def pair_sub(first, second):
    return (first[0] - second[0], first[1] - second[1])


def pair_mul(first, second):
    return (
        first[0] * second[0] - first[1] * second[1],
        first[0] * second[1] + first[1] * second[0],
    )


def pair_div(first, second):
    scale_sq = second[0] * second[0] + second[1] * second[1]
    return (
        (first[0] * second[0] + first[1] * second[1]) / scale_sq,
        (first[1] * second[0] - first[0] * second[1]) / scale_sq,
    )


def quartic_value(point):
    return (((210.0 * point - 480.0) * point + 360.0) * point - 96.0) * point + 6.0


def bisect_root(lower, upper):
    for count in range(200):
        middle = 0.5 * (lower + upper)
        if (quartic_value(lower) < 0.0) == (quartic_value(middle) < 0.0):
            lower = middle
        else:
            upper = middle
    return 0.5 * (lower + upper)


def radau_tables():
    abscissae = []
    grid_steps = 4000
    for m in range(grid_steps):
        lower = 0.999 * m / grid_steps
        upper = 0.999 * (m + 1) / grid_steps
        if (quartic_value(lower) < 0.0) != (quartic_value(upper) < 0.0):
            abscissae.append(bisect_root(lower, upper))
    abscissae.append(1.0)
    vander = [[abscissae[j] ** k for k in range(4)] for j in range(4)]
    moments = [[abscissae[i] ** (k + 1) / (k + 1) for k in range(4)] for i in range(4)]
    tableau = table_product(moments, invert_table(vander))
    inverse = invert_table(tableau)
    running = [list(row_values) for row_values in inverse]
    coeffs = []
    for k in range(1, 5):
        trace_value = sum((running[i][i] for i in range(4)))
        coeffs.append(-trace_value / k)
        shifted_table = [
            [running[i][j] + (coeffs[-1] if i == j else 0.0) for j in range(4)] for i in range(4)
        ]
        running = table_product(inverse, shifted_table)
    start_point = (0.4, 0.9)
    estimates = [(1.0, 0.0)]
    for k in range(3):
        estimates.append(pair_mul(estimates[-1], start_point))
    for count in range(500):
        for i in range(4):
            value = (1.0, 0.0)
            for coef_value in coeffs:
                value = pair_add(pair_mul(value, estimates[i]), (coef_value, 0.0))
            denom = (1.0, 0.0)
            for j in range(4):
                if j != i:
                    denom = pair_mul(denom, pair_sub(estimates[i], estimates[j]))
            estimates[i] = pair_sub(estimates[i], pair_div(value, denom))
    chosen = [m for m in range(4) if estimates[m][1] > 0.0]
    ranking = sorted(chosen, key=lambda m: -estimates[m][1])
    columns = []
    pairs = []
    for m in ranking:
        eigen_pair = estimates[m]
        system = [
            [
                (
                    inverse[i][j] - (eigen_pair[0] if i == j else 0.0),
                    -(eigen_pair[1] if i == j else 0.0),
                )
                for j in range(4)
            ]
            for i in range(3)
        ]
        rows_left = [
            [system[i][j] for j in range(3)] + [(-system[i][3][0], -system[i][3][1])]
            for i in range(3)
        ]
        for col in range(3):
            pivot_row = max(
                range(col, 3), key=lambda r: rows_left[r][col][0] ** 2 + rows_left[r][col][1] ** 2
            )
            rows_left[col], rows_left[pivot_row] = (rows_left[pivot_row], rows_left[col])
            leading = rows_left[col][col]
            rows_left[col] = [pair_div(v, leading) for v in rows_left[col]]
            for r in range(3):
                if r != col:
                    factor = rows_left[r][col]
                    rows_left[r] = [
                        pair_sub(a, pair_mul(factor, b))
                        for a, b in zip(rows_left[r], rows_left[col])
                    ]
        vector = [rows_left[i][3] for i in range(3)] + [(1.0, 0.0)]
        columns.append([v[0] for v in vector])
        columns.append([v[1] for v in vector])
        pairs.append((eigen_pair[0], eigen_pair[1]))
    eigen_basis = [[columns[j][i] for j in range(4)] for i in range(4)]
    basis_inverse = invert_table(eigen_basis)
    return (tableau, inverse, eigen_basis, basis_inverse, pairs)


def constants():
    tableau, inverse, eigen_basis, basis_inverse, pairs = radau_tables()
    shift_table = table_product(basis_inverse, inverse)
    shift_rows = [[v / step_size for v in row_values] for row_values in shift_table]
    pairs = [(p[0] / step_size, p[1] / step_size) for p in pairs]
    return eigen_basis, basis_inverse, shift_rows, pairs


def lane_ids(rows):
    return lax.broadcasted_iota(jnp.int32, (rows, LANES), 1)


def turn(cells, amount):
    return pltpu.roll(cells, amount % LANES, cells.ndim - 1)


def edges_kernel(own_ref, prev_ref, diff_ref, react_ref, low_ref, high_ref):
    nz, nx = prev_ref.shape[0], prev_ref.shape[1]
    lanes = lane_ids(nx)
    for z in range(nz // 2):
        low = jnp.zeros((nx, LANES), jnp.float32)
        high = low
        for part in range(2):
            plane = z + part * (nz // 2)
            cells = [own_ref[0, plane], own_ref[1, plane], prev_ref[plane], diff_ref[plane], react_ref[plane]]
            for f, cell in enumerate(cells):
                at = part * 64 + f * EDGE
                here = (lanes >= at) & (lanes < at + EDGE)
                low = jnp.where(here, turn(cell, at), low)
                high = jnp.where(here, turn(cell, at + EDGE), high)
        low_ref[z] = low
        high_ref[z] = high


def rows_kernel(own_ref, other_ref, prev_ref, diff_ref, react_ref, own_left_ref, own_right_ref, other_left_ref, other_right_ref, side_ref, low_ref, high_ref):
    nz, nx = prev_ref.shape[0], prev_ref.shape[1]
    lanes = lane_ids(nx)
    half = nz // 2
    for z in range(nz):
        part, plane = divmod(z, half)
        side = jnp.zeros((nx, LANES), jnp.float32)
        for f in range(7):
            source = (0, 1, 0, 1, 2, 3, 4)[f]
            refs = (other_left_ref, other_right_ref) if f in (2, 3) else (own_left_ref, own_right_ref)
            for right in range(2):
                at = f * 2 * EDGE + right * EDGE
                here = (lanes >= at) & (lanes < at + EDGE)
                side = jnp.where(here, turn(refs[right][plane], at - part * 64 - source * EDGE), side)
        side_ref[z] = side
        cells = [own_ref[0, z], own_ref[1, z], other_ref[0, z], other_ref[1, z], prev_ref[z], diff_ref[z], react_ref[z], side]
        for f, cell in enumerate(cells):
            low_ref[z, 8 * f : 8 * f + 8] = cell[0:8]
            low_ref[z, 64 + f : 65 + f] = cell[8:9]
            high_ref[z, 8 * f : 8 * f + 8] = cell[nx - 8 : nx]
            high_ref[z, 64 + f : 65 + f] = cell[nx - 9 : nx - 8]


ROWS = 48
FIRST, LAST = 8, 40
OWN = slice(16, 32)
WORK = slice(FIRST, LAST)
BEFORE = slice(FIRST - 1, LAST - 1)
AFTER = slice(FIRST + 1, LAST + 1)


def main_kernel(consts, own_ref, other_ref, prev_ref, diff_ref, react_ref, side_ref, from_low_ref, from_high_ref,
                part_ref, sums_ref, val, kap, frozen, slope, rea, prv, fx, fym, fyp, fz, alpha, beta, vec, ya, yb, keep, table):
    eigen_basis, basis_inverse, shift_rows, pairs = consts
    nz, nx = prev_ref.shape[0], prev_ref.shape[1]
    section = lax.axis_index("section")
    lanes = lane_ids(ROWS)
    zero_plane = jnp.zeros((ROWS, LANES), jnp.float32)

    def merged(pair):
        keep_left = lane_ids(pair[0].shape[0]) < 64
        return jnp.where(keep_left, turn(pair[0], -EDGE), turn(pair[1], EDGE))

    for a in range(2):
        for edge in (0, nz + 1):
            frozen[a, edge] = zero_plane
            for f in range(4):
                val[f, a, edge] = zero_plane
                kap[f, a, edge] = zero_plane
                ya[f, a, edge] = zero_plane
                yb[f, a, edge] = zero_plane

    def assemble(z, carry):
        side = side_ref[z]
        low, high = from_low_ref[z], from_high_ref[z]

        def column(main, f):
            tile = lambda t: jnp.broadcast_to(t, (8, LANES))
            if f == 7:
                body = main
            else:
                body = main
            return jnp.concatenate(
                [tile(low[64 + f : 65 + f]), low[8 * f : 8 * f + 8], body, high[8 * f : 8 * f + 8], tile(high[64 + f : 65 + f])], 0
            )

        sides = column(side, 7)

        def split(main, f):
            cells = column(main, f)
            at = 2 * EDGE * f
            left = jnp.where(lanes < EDGE, turn(sides, -at), turn(cells, EDGE))
            right = jnp.where(lanes >= LANES - EDGE, turn(sides, LANES - 2 * EDGE - at), turn(cells, -EDGE))
            return left, right

        diffs = split(diff_ref[z], 5)
        prevs = split(prev_ref[z], 4)
        reacts = split(react_ref[z], 6)
        for a in range(2):
            frozen[a, z + 1] = diffs[a] * (0.5 + 0.25 * jnp.tanh(prevs[a]))
            slope[a, z] = (reacts[a] * (1.0 - 3.0 * prevs[a] * prevs[a]))[WORK]
            rea[a, z] = reacts[a][WORK]
            prv[a, z] = prevs[a][WORK]
            inside = jnp.where(diffs[a] > 0.0, 1.0, 0.0)
            alpha[0, a, z] = inside[WORK]
        for f in range(4):
            main = own_ref[f, z] if f < 2 else other_ref[f - 2, z]
            values = split(main, f)
            for a in range(2):
                val[f, a, z + 1] = values[a]
                kap[f, a, z + 1] = diffs[a] * (0.5 + 0.25 * jnp.tanh(values[a]))
        return carry

    lax.fori_loop(0, nz, assemble, 0)

    def pick(matrix, m, j):
        first, second = matrix[m][j], matrix[m][(j + 2) % 4]
        return jnp.where(section == 0, jnp.float32(first), jnp.float32(second))

    q_rows = [[pick(basis_inverse, m, j) for j in range(4)] for m in range(4)]
    c_rows = [[pick(shift_rows, m, j) for j in range(4)] for m in range(4)]

    def prepare(z, carry):
        starts = []
        for a in range(2):
            mid = frozen[a, z + 1, WORK]
            f_xm = mid + frozen[a, z + 1, BEFORE]
            f_xp = mid + frozen[a, z + 1, AFTER]
            f_ym = mid + turn(mid, 1)
            f_yp = mid + turn(mid, -1)
            f_zm = mid + frozen[a, z, WORK]
            f_zp = mid + frozen[a, z + 2, WORK]
            fx[0, a, z] = f_xm
            fx[1, a, z] = f_xp
            fym[a, z] = f_ym
            fyp[a, z] = f_yp
            fz[0, a, z] = f_zm
            fz[1, a, z] = f_zp
            base = ((f_xm + f_xp) + (f_ym + f_yp)) + (f_zm + f_zp) - slope[a, z]
            inside = alpha[0, a, z]
            for b in range(2):
                real, imag = pairs[b]
                diag = base + real
                scale = inside / (diag * diag + imag * imag)
                alpha[b, a, z] = diag * scale
                beta[b, a, z] = imag * scale
            prev = prv[a, z]
            react = rea[a, z]
            rhs = [None] * 4
            for j in range(4):
                v = val[j, a, z + 1, WORK]
                k = kap[j, a, z + 1, WORK]
                flux = react * v * (1.0 - v * v)
                flux = flux + (k + kap[j, a, z + 1, BEFORE]) * (val[j, a, z + 1, BEFORE] - v)
                flux = flux + (k + kap[j, a, z + 1, AFTER]) * (val[j, a, z + 1, AFTER] - v)
                flux = flux + (k + turn(k, 1)) * (turn(v, 1) - v)
                flux = flux + (k + turn(k, -1)) * (turn(v, -1) - v)
                flux = flux + (k + kap[j, a, z, WORK]) * (val[j, a, z, WORK] - v)
                flux = flux + (k + kap[j, a, z + 2, WORK]) * (val[j, a, z + 2, WORK] - v)
                grown = v - prev
                for m in range(4):
                    term = q_rows[m][j] * flux - c_rows[m][j] * grown
                    rhs[m] = term if j == 0 else rhs[m] + term
            for m in range(4):
                vec[m, a, z] = rhs[m]
            for b in range(2):
                al, be = alpha[b, a, z], beta[b, a, z]
                ya[2 * b, a, z + 1, WORK] = al * rhs[2 * b] - be * rhs[2 * b + 1]
                ya[2 * b + 1, a, z + 1, WORK] = be * rhs[2 * b] + al * rhs[2 * b + 1]
            starts.append([r[8:24] for r in rhs])
        for m in range(4):
            keep[0, m, z] = merged([starts[0][m], starts[1][m]])
        for a in range(2):
            for m in range(4):
                for ref in (ya, yb):
                    ref[m, a, z + 1, 0:FIRST] = jnp.zeros((FIRST, LANES), jnp.float32)
                    ref[m, a, z + 1, LAST:ROWS] = jnp.zeros((ROWS - LAST, LANES), jnp.float32)
        return carry

    lax.fori_loop(0, nz, prepare, 0)

    def spread(ref, m, a, z, rows=WORK):
        lo, hi = rows.start, rows.stop
        cut = slice(lo - FIRST, hi - FIRST)
        mid = ref[m, a, z + 1, lo:hi]
        total = fx[0, a, z, cut] * ref[m, a, z + 1, lo - 1 : hi - 1]
        total = total + fx[1, a, z, cut] * ref[m, a, z + 1, lo + 1 : hi + 1]
        total = total + fym[a, z, cut] * turn(mid, 1)
        total = total + fyp[a, z, cut] * turn(mid, -1)
        total = total + fz[0, a, z, cut] * ref[m, a, z, lo:hi]
        return total + fz[1, a, z, cut] * ref[m, a, z + 2, lo:hi]

    for j in range(ITERS):

        def odd(z, carry, j=j):
            done = [[None] * 4, [None] * 4]
            for a in range(2):
                for b in range(2):
                    t0 = spread(ya, 2 * b, a, z)
                    t1 = spread(ya, 2 * b + 1, a, z)
                    al, be = alpha[b, a, z], beta[b, a, z]
                    y0 = al * t0 - be * t1
                    y1 = be * t0 + al * t1
                    yb[2 * b, a, z + 1, WORK] = y0
                    yb[2 * b + 1, a, z + 1, WORK] = y1
                    done[a][2 * b] = ya[2 * b, a, z + 1, OWN] + y0[8:24]
                    done[a][2 * b + 1] = ya[2 * b + 1, a, z + 1, OWN] + y1[8:24]
            for m in range(4):
                sums_ref[j, m, z] = merged([done[0][m], done[1][m]])
            return carry

        def even(z, carry, j=j):
            last = j == ITERS - 1
            done = [[None] * 4, [None] * 4]
            rows = OWN if last else WORK
            cut = slice(rows.start - FIRST, rows.stop - FIRST)
            for a in range(2):
                for b in range(2):
                    new = []
                    for m in (2 * b, 2 * b + 1):
                        v = spread(yb, m, a, z, rows)
                        if SHIFTS[j]:
                            v = v - SHIFTS[j] * vec[m, a, z, cut]
                        new.append(v)
                        done[a][m] = v if last else v[8:24]
                    if not last:
                        al, be = alpha[b, a, z], beta[b, a, z]
                        vec[2 * b, a, z] = new[0]
                        vec[2 * b + 1, a, z] = new[1]
                        ya[2 * b, a, z + 1, WORK] = al * new[0] - be * new[1]
                        ya[2 * b + 1, a, z + 1, WORK] = be * new[0] + al * new[1]
            for m in range(4):
                keep[j + 1, m, z] = merged([done[0][m], done[1][m]])
            return carry

        lax.fori_loop(0, nz, odd, 0)
        lax.fori_loop(0, nz, even, 0)

    table[...] = jnp.zeros((LANES, LANES), jnp.float32)
    for b in range(2):

        def dots(z, carry):
            out = list(carry)
            for m in (2 * b, 2 * b + 1):
                for r in range(0, nx, 8):
                    cells = [keep[i, m, z, r : r + 8] for i in range(SIZE)]
                    for at, (i, j) in enumerate(PAIRS):
                        out[at] = out[at] + cells[i] * cells[j]
            return tuple(out)

        zero = jnp.zeros((8, LANES), jnp.float32)
        out = lax.fori_loop(0, nz, dots, tuple(zero for _ in PAIRS))
        for at in range(len(PAIRS)):
            table[b * len(PAIRS) + at : b * len(PAIRS) + at + 1] = jnp.sum(out[at], axis=0, keepdims=True)
    total = jnp.sum(table[...].T, axis=0, keepdims=True)
    part_ref[...] = jnp.broadcast_to(total, part_ref.shape)


def step_weights(gram):
    table = {}
    for at, (i, j) in enumerate(PAIRS):
        table[i, j] = table[j, i] = gram[at]
    coef = [jnp.ones_like(gram[0])]
    weight = []
    step = coef[0]
    for k in range(ITERS):
        moved = [SHIFTS[j] * coef[j] for j in range(k + 1)] + [jnp.zeros_like(step)]
        for j in range(k + 1):
            moved[j + 1] = moved[j + 1] + coef[j]
        coef = coef + [jnp.zeros_like(step)]
        image = [coef[j] - moved[j] for j in range(k + 2)]
        num, den, bound = 0.0, 0.0, 0.0
        for i in range(k + 2):
            row, size = 0.0, 0.0
            for j in range(k + 2):
                term = table[i, j] * image[j]
                row = row + term
                size = size + jnp.abs(term)
            num = num + row * coef[i]
            den = den + row * image[i]
            bound = bound + size * jnp.abs(image[i])
        step = jnp.where(den > bound * 6e-8, num / (jnp.maximum(den, 0.0) + tiny_value), step)
        weight = weight + [jnp.zeros_like(step)]
        for j in range(k + 1):
            weight[j] = weight[j] + step * coef[j]
        coef = [coef[j] - step * image[j] for j in range(k + 2)]
    return weight


def finish_kernel(consts, total_ref, sums_ref, own_ref, out_ref):
    eigen_basis = consts[0]
    nz, nx = own_ref.shape[1], own_ref.shape[2]
    section = lax.axis_index("section")
    total = jnp.sum(total_ref[...], axis=0, keepdims=True)
    count = len(PAIRS)
    weights = []
    for b in range(2):
        gram = [jnp.broadcast_to(total[:, b * count + at : b * count + at + 1], (1, LANES)) for at in range(count)]
        weights.append(step_weights(gram))
    basis = [
        [jnp.where(section == 0, jnp.float32(eigen_basis[r][m]), jnp.float32(eigen_basis[2 + r][m])) for m in range(4)]
        for r in range(2)
    ]

    def combine(z, carry):
        outs = [own_ref[0, z], own_ref[1, z]]
        for m in range(4):
            field = 0.0
            for j in range(ITERS):
                field = field + weights[m // 2][j] * sums_ref[j, m, z]
            outs = [outs[r] + basis[r][m] * field for r in range(2)]
        out_ref[0, z] = outs[0]
        out_ref[1, z] = outs[1]
        return carry

    lax.fori_loop(0, nz, combine, 0)


def call(kernel, outs, scratch=(), flops=1_000_000, name=None):
    many = isinstance(outs, list)
    shapes = [jax.ShapeDtypeStruct(o, jnp.float32) for o in (outs if many else [outs])]

    def run(*args):
        moved = 4 * sum(int(a.size) for a in args) + 4 * sum(int(functools.reduce(lambda p, q: p * q, s.shape, 1)) for s in shapes)
        return pl.pallas_call(
            kernel,
            out_shape=shapes if many else shapes[0],
            in_specs=[pl.BlockSpec(memory_space=pltpu.VMEM)] * len(args),
            out_specs=[pl.BlockSpec(memory_space=pltpu.VMEM)] * len(shapes) if many else pl.BlockSpec(memory_space=pltpu.VMEM),
            scratch_shapes=[pltpu.VMEM(s, jnp.float32) for s in scratch],
            compiler_params=pltpu.CompilerParams(vmem_limit_bytes=VMEM_LIMIT),
            cost_estimate=pl.CostEstimate(flops=flops, bytes_accessed=moved, transcendentals=0),
            name=name,
        )(*args)

    return run


def neighbours(count, step):
    return [(i, i + step) for i in range(count) if 0 <= i + step < count]


def crossed(count, step):
    return [
        (s * count + i, (1 - s) * count + i + step) for s in range(2) for i in range(count) if 0 <= i + step < count
    ]


def body(previous, sections, diffusivity, reaction):
    consts = constants()
    nz, nx, ny = previous.shape
    columns, rows = lax.axis_size("sy"), lax.axis_size("sx")
    other = lax.ppermute(sections, "section", [(0, 1), (1, 0)])
    edge = (nz // 2, nx, ny)
    low, high = call(edges_kernel, [edge, edge], name="edges")(sections, previous, diffusivity, reaction)
    own_left = lax.ppermute(high, "sy", neighbours(columns, 1))
    own_right = lax.ppermute(low, "sy", neighbours(columns, -1))
    other_left = lax.ppermute(high, ("section", "sy"), crossed(columns, 1))
    other_right = lax.ppermute(low, ("section", "sy"), crossed(columns, -1))
    side, low_rows, high_rows = call(rows_kernel, [(nz, nx, ny), (nz, 72, ny), (nz, 72, ny)], name="rows")(
        sections, other, previous, diffusivity, reaction, own_left, own_right, other_left, other_right
    )
    from_low = lax.ppermute(high_rows, "sx", neighbours(rows, 1))
    from_high = lax.ppermute(low_rows, "sx", neighbours(rows, -1))
    peers = columns * rows
    padded, work = (2, nz + 2, ROWS, ny), (2, nz, LAST - FIRST, ny)
    scratch = [
        (4,) + padded, (4,) + padded, padded, work, work, work,
        (2,) + work, work, work, (2,) + work, (2,) + work, (2,) + work,
        (4,) + work, (4,) + padded, (4,) + padded, (SIZE, 4, nz, nx, ny), (LANES, LANES),
    ]
    part, sums = call(
        functools.partial(main_kernel, consts), [(peers, LANES), (ITERS, 4, nz, nx, ny)], scratch, 50_000_000, name="main"
    )(sections, other, previous, diffusivity, reaction, side, from_low, from_high)
    total = lax.all_to_all(part.reshape(peers, 1, LANES), ("sx", "sy"), 0, 0).reshape(peers, LANES)
    return call(functools.partial(finish_kernel, consts), sections.shape, name="finish")(total, sums, sections)


def solution(mesh):
    in_specs = (
        P(None, "sx", "sy"),
        P("section", None, "sx", "sy"),
        P(None, "sx", "sy"),
        P(None, "sx", "sy"),
    )
    out_specs = P("section", None, "sx", "sy")
    return jax.shard_map(body, mesh=mesh, in_specs=in_specs, out_specs=out_specs, check_vma=False)
```

time: 1370 us -> 108 us (0.08); the launches traced: 1350 us -> 108 us
  blocking collectives: 1090 us -> 24 us
  starting transfers between devices: 131 us -> 19.6 us
  waiting for transfers between devices: 82.7 us -> 17.4 us
  Pallas kernels: 0 us -> 44.9 us
  other arithmetic: 29.6 us -> 0 us
    psum x4 -> x0, blocking collectives: 1060 us -> none  [body(): lax.psum((jnp.sum(image * residue), jnp.sum(image * image)), ('sx', 'sy'))]
    ppermute x40 -> x7, starting transfers between devices: 131 us -> 19.6 us  [the longest x1 5.31 us: body(): from_low = lax.ppermute(high_rows, 'sx', neighbours(rows, 1))]
    ppermute x40 -> x7, waiting for transfers between devices: 82.7 us -> 17.4 us  [the longest x1 5.19 us: body(): from_low = lax.ppermute(high_rows, 'sx', neighbours(rows, 1))]
    pallas_call x0 -> x4, Pallas kernels: none -> 44.9 us  [run(): pl.pallas_call(kernel, out_shape=shapes if many else shapes[0], in_specs=...]
    all_gather x3 -> x0, blocking collectives: 25.9 us -> none  [the longest x1 9.77 us: body(): lax.all_gather(increment, 'section', axis=0, tiled=True)]
    all_to_all x0 -> x1, blocking collectives: none -> 24 us  [body(): lax.all_to_all(part.reshape(peers, 1, LANES), ('sx', 'sy'), 0, 0)]
  transfers between devices with their start and end apart: 40 -> 7, of which waited for: 25 -> 4; matrix products, arithmetic and copies ran while one was open for 1% -> 0% of each run, Pallas kernels for 0% -> 2%
where the time goes in v1:
time: 108 us
  Pallas kernels  44.9 us (42%)
  blocking collectives  24 us (22%)
  starting transfers between devices  19.6 us (18%)
  waiting for transfers between devices  17.4 us (16%)
  local copies, waits for them, and re-layouts  2.13 us (2%)
    pallas_call x4, Pallas kernels, run(): pl.pallas_call(kernel, out_shape=shapes if many else shapes[0], in_specs=...  44.9 us
    all_to_all x1, blocking collectives, body(): lax.all_to_all(part.reshape(peers, 1, LANES), ('sx', 'sy'), 0, 0)  24 us
    ppermute x1, starting transfers between devices, body(): from_low = lax.ppermute(high_rows, 'sx', neighbours(rows, 1))  5.31 us
    ppermute x1, waiting for transfers between devices, body(): from_low = lax.ppermute(high_rows, 'sx', neighbours(rows, 1))  5.19 us
    ppermute x1, waiting for transfers between devices, body(): other_right = lax.ppermute(low, ('section', 'sy'), crossed(columns, -1))  4.98 us
    ppermute x1, waiting for transfers between devices, body(): from_high = lax.ppermute(low_rows, 'sx', neighbours(rows, -1))  4.29 us
    ppermute x1, starting transfers between devices, body(): other = lax.ppermute(sections, 'section', [(0, 1), (1, 0)])  3.74 us
    ppermute x1, starting transfers between devices, body(): own_left = lax.ppermute(high, 'sy', neighbours(columns, 1))  3.12 us
  transfers between devices with their start and end apart: 7, of which 4 were waited for; matrix products, arithmetic and copies ran while one was open for 0% of the time, Pallas kernels for 2%

profile of v1, /device:TPU:1, one launch (start us, length us, event | category | flops | bytes accessed | tf_op | source)
XLA Modules:
  0.0 108.1 jit_solution(6712220082667540043)
XLA Ops:
  0.0 3.7 %collective-permute-start = (f32[2,16,16,128]{3,2,1,0:T(8,128)}, f32[2,16,16,128]{3,2,1,0:T(8,128)S(1)}, u32[]{:S(2)}, u32[]{:S(2)}) collective-permute-start(f32[2,16,16,128]{3,2,1,0:T(8,128)} %own_ref.7), channel_id=1, source_target_pairs={{0,128},{128,0},{1,129},{129,1},{2,130},{130,2},{3,131},{131,3},{4... | collective-permute-start | bytes 786440 | tf_op jit(solution)/shard_map/ppermute | solution.py:529
  3.7 2.1 %edges.1 = (f32[8,16,128]{2,1,0:T(8,128)}, f32[8,16,128]{2,1,0:T(8,128)}) custom-call(f32[2,16,16,128]{3,2,1,0:T(8,128)} %own_ref.7, f32[16,16,128]{2,1,0:T(8,128)} %prev_ref.5, f32[16,16,128]{2,1,0:T(8,128)} %diff_ref.5, f32[16,16,128]{2,1,0:T(8,128)} %react_ref.5), custom_call_target="tpu_custom_call" | custom-call | flops 1000000 | bytes 786432 | tf_op jit(solution)/shard_map/edges/pallas_call | solution.py:501
  5.9 2.9 %collective-permute-start.3 = (f32[8,16,128]{2,1,0:T(8,128)}, f32[8,16,128]{2,1,0:T(8,128)S(1)}, u32[]{:S(2)}, u32[]{:S(2)}) collective-permute-start(f32[8,16,128]{2,1,0:T(8,128)} %get-tuple-element.12), channel_id=1, source_target_pairs={{0,129},{1,130},{2,131},{3,132},{4,133},{5,134},{6,135},{128,1},{1... | collective-permute-start | bytes 196616 | tf_op jit(solution)/shard_map/ppermute | solution.py:534
  8.8 3.1 %collective-permute-start.1 = (f32[8,16,128]{2,1,0:T(8,128)}, f32[8,16,128]{2,1,0:T(8,128)S(1)}, u32[]{:S(2)}, u32[]{:S(2)}) collective-permute-start(f32[8,16,128]{2,1,0:T(8,128)} %get-tuple-element.12), channel_id=1, source_target_pairs={{0,1},{1,2},{2,3},{3,4},{4,5},{5,6},{6,7},{8,9},{9,10},{10,11},{11... | collective-permute-start | bytes 196616 | tf_op jit(solution)/shard_map/ppermute | solution.py:532
  11.9 1.3 %collective-permute-start.4 = (f32[8,16,128]{2,1,0:T(8,128)}, f32[8,16,128]{2,1,0:T(8,128)S(1)}, u32[]{:S(2)}, u32[]{:S(2)}) collective-permute-start(f32[8,16,128]{2,1,0:T(8,128)} %get-tuple-element.13), channel_id=1, source_target_pairs={{1,128},{2,129},{3,130},{4,131},{5,132},{6,133},{7,134},{129,0},{1... | collective-permute-start | bytes 196616 | tf_op jit(solution)/shard_map/ppermute | solution.py:535
  13.2 1.3 %collective-permute-start.2 = (f32[8,16,128]{2,1,0:T(8,128)}, f32[8,16,128]{2,1,0:T(8,128)S(1)}, u32[]{:S(2)}, u32[]{:S(2)}) collective-permute-start(f32[8,16,128]{2,1,0:T(8,128)} %get-tuple-element.13), channel_id=1, source_target_pairs={{1,0},{2,1},{3,2},{4,3},{5,4},{6,5},{7,6},{9,8},{10,9},{11,10},{12... | collective-permute-start | bytes 196616 | tf_op jit(solution)/shard_map/ppermute | solution.py:533
  14.5 0.0 collective-permute-done.3.other_left_ref
  14.5 0.0 copy-start.3
  14.5 0.0 collective-permute-done.1.own_left_ref
  14.5 0.0 copy-start.4
  14.5 5.0 %collective-permute-done.4.other_right_ref = f32[8,16,128]{2,1,0:T(8,128)S(1)} collective-permute-done((f32[8,16,128]{2,1,0:T(8,128)}, f32[8,16,128]{2,1,0:T(8,128)S(1)}, u32[]{:S(2)}, u32[]{:S(2)}) %collective-permute-start.4) | collective-permute-done | bytes 65568 | tf_op jit(solution)/shard_map/ppermute | solution.py:535
  19.5 2.9 %collective-permute-done.2.own_right_ref = f32[8,16,128]{2,1,0:T(8,128)S(1)} collective-permute-done((f32[8,16,128]{2,1,0:T(8,128)}, f32[8,16,128]{2,1,0:T(8,128)S(1)}, u32[]{:S(2)}, u32[]{:S(2)}) %collective-permute-start.2) | collective-permute-done | bytes 65568 | tf_op jit(solution)/shard_map/ppermute | solution.py:533
  22.5 0.0 collective-permute-done.other_ref
  22.5 0.6 copy-done.6
  23.1 0.7 copy-done
  23.8 2.9 %rows.1 = (f32[16,16,128]{2,1,0:T(8,128)}, f32[16,72,128]{2,1,0:T(8,128)}, f32[16,72,128]{2,1,0:T(8,128)}) custom-call(f32[2,16,16,128]{3,2,1,0:T(8,128)} %own_ref.7, f32[2,16,16,128]{3,2,1,0:T(8,128)} %copy-done, f32[16,16,128]{2,1,0:T(8,128)} %prev_ref.5, f32[16,16,128]{2,1,0:T(8,128)} %diff_ref.5, f32[16,16,128]{2,1,0:T(8,128)} %react_ref.5, ...), custom_call_target="tpu_custom_call" | custom-call | flops 1000000 | bytes 2490368 | tf_op jit(solution)/shard_map/rows/pallas_call | solution.py:501
  26.6 5.3 %collective-permute-start.5 = (f32[16,72,128]{2,1,0:T(8,128)}, f32[16,72,128]{2,1,0:T(8,128)S(1)}, u32[]{:S(2)}, u32[]{:S(2)}) collective-permute-start(f32[16,72,128]{2,1,0:T(8,128)} %get-tuple-element.15), channel_id=1, source_target_pairs={{0,8},{8,16},{16,24},{24,32},{32,40},{40,48},{48,56},{56,64},{64,7... | collective-permute-start | bytes 1769480 | tf_op jit(solution)/shard_map/ppermute | solution.py:539
  32.0 1.9 %collective-permute-start.6 = (f32[16,72,128]{2,1,0:T(8,128)}, f32[16,72,128]{2,1,0:T(8,128)S(1)}, u32[]{:S(2)}, u32[]{:S(2)}) collective-permute-start(f32[16,72,128]{2,1,0:T(8,128)} %get-tuple-element.16), channel_id=1, source_target_pairs={{8,0},{16,8},{24,16},{32,24},{40,32},{48,40},{56,48},{64,56},{72,6... | collective-permute-start | bytes 1769480 | tf_op jit(solution)/shard_map/ppermute | solution.py:540
  33.9 5.2 %collective-permute-done.5.from_low_ref = f32[16,72,128]{2,1,0:T(8,128)S(1)} collective-permute-done((f32[16,72,128]{2,1,0:T(8,128)}, f32[16,72,128]{2,1,0:T(8,128)S(1)}, u32[]{:S(2)}, u32[]{:S(2)}) %collective-permute-start.5) | collective-permute-done | bytes 589856 | tf_op jit(solution)/shard_map/ppermute | solution.py:539
  39.1 4.3 %collective-permute-done.6.from_high_ref = f32[16,72,128]{2,1,0:T(8,128)S(1)} collective-permute-done((f32[16,72,128]{2,1,0:T(8,128)}, f32[16,72,128]{2,1,0:T(8,128)S(1)}, u32[]{:S(2)}, u32[]{:S(2)}) %collective-permute-start.6) | collective-permute-done | bytes 589856 | tf_op jit(solution)/shard_map/ppermute | solution.py:540
  43.4 0.8 copy-done.2
  44.2 37.1 %main.1 = (f32[128,128]{1,0:T(8,128)}, f32[4,4,16,16,128]{4,3,2,1,0:T(8,128)}) custom-call(f32[2,16,16,128]{3,2,1,0:T(8,128)} %own_ref.7, f32[2,16,16,128]{3,2,1,0:T(8,128)} %copy-done, f32[16,16,128]{2,1,0:T(8,128)} %prev_ref.5, f32[16,16,128]{2,1,0:T(8,128)} %diff_ref.5, f32[16,16,128]{2,1,0:T(8,128)} %react_ref.5, ...), custom_call_target="tpu_custom_call" | custom-call | flops 50000000 | bytes 4390912 | tf_op jit(solution)/shard_map/main/pallas_call | solution.py:501
  81.3 24.0 %all_to_all.5 = f32[128,1,128]{2,1,0:T(1,128)} all-to-all(f32[128,1,128]{2,1,0:T(1,128)} %bitcast.5), channel_id=1, replica_groups=mesh['section'=2,'sx'=16,'sy'=8] {'sx','sy'}, dimensions={0} | all-to-all | bytes 131072 | tf_op jit(solution)/shard_map/all_to_all | solution.py:551
  105.3 2.8 %finish.1 = f32[2,16,16,128]{3,2,1,0:T(8,128)} custom-call(f32[128,128]{1,0:T(8,128)} %bitcast.4, f32[4,4,16,16,128]{4,3,2,1,0:T(8,128)} %get-tuple-element.18.sums_ref, f32[2,16,16,128]{3,2,1,0:T(8,128)} %own_ref.7), custom_call_target="tpu_custom_call" | custom-call | flops 1000000 | bytes 2686976 | tf_op jit(solution)/shard_map/finish/pallas_call | solution.py:501
  (9 shorter events, 0.0 us)
Async XLA Ops:
  0.0 22.5 %collective-permute-start = (f32[2,16,16,128]{3,2,1,0:T(8,128)}, f32[2,16,16,128]{3,2,1,0:T(8,128)S(1)}, u32[]{:S(2)}, u32[]{:S(2)}) collective-permute-start(f32[2,16,16,128]{3,2,1,0:T(8,128)} %own_ref.7), channel_id=1, source_target_pairs={{0,128},{128,0},{1,129},{129,1},{2,130},{130,2},{3,131},{131,3},{4... | collective-permute-start | bytes 786440 | tf_op jit(solution)/shard_map/ppermute | solution.py:529
  5.9 8.6 %collective-permute-start.3 = (f32[8,16,128]{2,1,0:T(8,128)}, f32[8,16,128]{2,1,0:T(8,128)S(1)}, u32[]{:S(2)}, u32[]{:S(2)}) collective-permute-start(f32[8,16,128]{2,1,0:T(8,128)} %get-tuple-element.12), channel_id=1, source_target_pairs={{0,129},{1,130},{2,131},{3,132},{4,133},{5,134},{6,135},{128,1},{1... | collective-permute-start | bytes 196616 | tf_op jit(solution)/shard_map/ppermute | solution.py:534
  8.8 5.8 %collective-permute-start.1 = (f32[8,16,128]{2,1,0:T(8,128)}, f32[8,16,128]{2,1,0:T(8,128)S(1)}, u32[]{:S(2)}, u32[]{:S(2)}) collective-permute-start(f32[8,16,128]{2,1,0:T(8,128)} %get-tuple-element.12), channel_id=1, source_target_pairs={{0,1},{1,2},{2,3},{3,4},{4,5},{5,6},{6,7},{8,9},{9,10},{10,11},{11... | collective-permute-start | bytes 196616 | tf_op jit(solution)/shard_map/ppermute | solution.py:532
  11.9 7.6 %collective-permute-start.4 = (f32[8,16,128]{2,1,0:T(8,128)}, f32[8,16,128]{2,1,0:T(8,128)S(1)}, u32[]{:S(2)}, u32[]{:S(2)}) collective-permute-start(f32[8,16,128]{2,1,0:T(8,128)} %get-tuple-element.13), channel_id=1, source_target_pairs={{1,128},{2,129},{3,130},{4,131},{5,132},{6,133},{7,134},{129,0},{1... | collective-permute-start | bytes 196616 | tf_op jit(solution)/shard_map/ppermute | solution.py:535
  13.2 9.2 %collective-permute-start.2 = (f32[8,16,128]{2,1,0:T(8,128)}, f32[8,16,128]{2,1,0:T(8,128)S(1)}, u32[]{:S(2)}, u32[]{:S(2)}) collective-permute-start(f32[8,16,128]{2,1,0:T(8,128)} %get-tuple-element.13), channel_id=1, source_target_pairs={{1,0},{2,1},{3,2},{4,3},{5,4},{6,5},{7,6},{9,8},{10,9},{11,10},{12... | collective-permute-start | bytes 196616 | tf_op jit(solution)/shard_map/ppermute | solution.py:533
  14.5 7.9 %copy-start.3 = (f32[8,16,128]{2,1,0:T(8,128)}, f32[8,16,128]{2,1,0:T(8,128)S(1)}, u32[]{:S(2)}) copy-start(f32[8,16,128]{2,1,0:T(8,128)S(1)} %collective-permute-done.3.other_left_ref) | copy-start | bytes 196612
  14.5 7.9 %copy-start.4 = (f32[8,16,128]{2,1,0:T(8,128)}, f32[8,16,128]{2,1,0:T(8,128)S(1)}, u32[]{:S(2)}) copy-start(f32[8,16,128]{2,1,0:T(8,128)S(1)} %collective-permute-done.1.own_left_ref) | copy-start | bytes 196612
  19.5 2.9 %copy-start.5 = (f32[8,16,128]{2,1,0:T(8,128)}, f32[8,16,128]{2,1,0:T(8,128)S(1)}, u32[]{:S(2)}) copy-start(f32[8,16,128]{2,1,0:T(8,128)S(1)} %collective-permute-done.4.other_right_ref) | copy-start | bytes 196612
  22.5 0.6 copy-start.6
  23.1 0.7 copy-start
  26.6 12.4 %collective-permute-start.5 = (f32[16,72,128]{2,1,0:T(8,128)}, f32[16,72,128]{2,1,0:T(8,128)S(1)}, u32[]{:S(2)}, u32[]{:S(2)}) collective-permute-start(f32[16,72,128]{2,1,0:T(8,128)} %get-tuple-element.15), channel_id=1, source_target_pairs={{0,8},{8,16},{16,24},{24,32},{32,40},{40,48},{48,56},{56,64},{64,7... | collective-permute-start | bytes 1769480 | tf_op jit(solution)/shard_map/ppermute | solution.py:539
  32.0 11.4 %collective-permute-start.6 = (f32[16,72,128]{2,1,0:T(8,128)}, f32[16,72,128]{2,1,0:T(8,128)S(1)}, u32[]{:S(2)}, u32[]{:S(2)}) collective-permute-start(f32[16,72,128]{2,1,0:T(8,128)} %get-tuple-element.16), channel_id=1, source_target_pairs={{8,0},{16,8},{24,16},{32,24},{40,32},{48,40},{56,48},{64,56},{72,6... | collective-permute-start | bytes 1769480 | tf_op jit(solution)/shard_map/ppermute | solution.py:540
  39.1 4.3 %copy-start.1 = (f32[16,72,128]{2,1,0:T(8,128)}, f32[16,72,128]{2,1,0:T(8,128)S(1)}, u32[]{:S(2)}) copy-start(f32[16,72,128]{2,1,0:T(8,128)S(1)} %collective-permute-done.5.from_low_ref) | copy-start | bytes 1769476
  43.4 0.8 copy-start.2

commit v2 on v1

v2 whole, which is shorter than its diff:
```python
import functools

import jax
import jax.numpy as jnp
from jax import lax
from jax.experimental import pallas as pl
from jax.experimental.pallas import tpu as pltpu
from jax.sharding import PartitionSpec as P

ITERS = 4
SHIFTS = (0.0, 0.9, 0.45, 0.7)
EDGE = 9
LANES = 128
SIZE = ITERS + 1
PAIRS = [(i, j) for i in range(SIZE) for j in range(i, SIZE)]
PREPARE_UNROLL = 1
STEP_UNROLL = 2
VMEM_LIMIT = 58 * 1024 * 1024


step_size = 1.0
tiny_value = 1e-06


def invert_table(matrix):
    order_n = len(matrix)
    augmented = [
        list(matrix[r]) + [1.0 if c == r else 0.0 for c in range(order_n)] for r in range(order_n)
    ]
    for col in range(order_n):
        pivot_row = max(range(col, order_n), key=lambda r: abs(augmented[r][col]))
        augmented[col], augmented[pivot_row] = (augmented[pivot_row], augmented[col])
        leading = augmented[col][col]
        augmented[col] = [v / leading for v in augmented[col]]
        for r in range(order_n):
            if r != col:
                factor = augmented[r][col]
                augmented[r] = [a - factor * b for a, b in zip(augmented[r], augmented[col])]
    return [row_values[order_n:] for row_values in augmented]


def table_product(left, right):
    return [
        [sum((left[i][k] * right[k][j] for k in range(len(right)))) for j in range(len(right[0]))]
        for i in range(len(left))
    ]


def pair_add(first, second):
    return (first[0] + second[0], first[1] + second[1])


def pair_sub(first, second):
    return (first[0] - second[0], first[1] - second[1])


def pair_mul(first, second):
    return (
        first[0] * second[0] - first[1] * second[1],
        first[0] * second[1] + first[1] * second[0],
    )


def pair_div(first, second):
    scale_sq = second[0] * second[0] + second[1] * second[1]
    return (
        (first[0] * second[0] + first[1] * second[1]) / scale_sq,
        (first[1] * second[0] - first[0] * second[1]) / scale_sq,
    )


def quartic_value(point):
    return (((210.0 * point - 480.0) * point + 360.0) * point - 96.0) * point + 6.0


def bisect_root(lower, upper):
    for count in range(200):
        middle = 0.5 * (lower + upper)
        if (quartic_value(lower) < 0.0) == (quartic_value(middle) < 0.0):
            lower = middle
        else:
            upper = middle
    return 0.5 * (lower + upper)


def radau_tables():
    abscissae = []
    grid_steps = 4000
    for m in range(grid_steps):
        lower = 0.999 * m / grid_steps
        upper = 0.999 * (m + 1) / grid_steps
        if (quartic_value(lower) < 0.0) != (quartic_value(upper) < 0.0):
            abscissae.append(bisect_root(lower, upper))
    abscissae.append(1.0)
    vander = [[abscissae[j] ** k for k in range(4)] for j in range(4)]
    moments = [[abscissae[i] ** (k + 1) / (k + 1) for k in range(4)] for i in range(4)]
    tableau = table_product(moments, invert_table(vander))
    inverse = invert_table(tableau)
    running = [list(row_values) for row_values in inverse]
    coeffs = []
    for k in range(1, 5):
        trace_value = sum((running[i][i] for i in range(4)))
        coeffs.append(-trace_value / k)
        shifted_table = [
            [running[i][j] + (coeffs[-1] if i == j else 0.0) for j in range(4)] for i in range(4)
        ]
        running = table_product(inverse, shifted_table)
    start_point = (0.4, 0.9)
    estimates = [(1.0, 0.0)]
    for k in range(3):
        estimates.append(pair_mul(estimates[-1], start_point))
    for count in range(500):
        for i in range(4):
            value = (1.0, 0.0)
            for coef_value in coeffs:
                value = pair_add(pair_mul(value, estimates[i]), (coef_value, 0.0))
            denom = (1.0, 0.0)
            for j in range(4):
                if j != i:
                    denom = pair_mul(denom, pair_sub(estimates[i], estimates[j]))
            estimates[i] = pair_sub(estimates[i], pair_div(value, denom))
    chosen = [m for m in range(4) if estimates[m][1] > 0.0]
    ranking = sorted(chosen, key=lambda m: -estimates[m][1])
    columns = []
    pairs = []
    for m in ranking:
        eigen_pair = estimates[m]
        system = [
            [
                (
                    inverse[i][j] - (eigen_pair[0] if i == j else 0.0),
                    -(eigen_pair[1] if i == j else 0.0),
                )
                for j in range(4)
            ]
            for i in range(3)
        ]
        rows_left = [
            [system[i][j] for j in range(3)] + [(-system[i][3][0], -system[i][3][1])]
            for i in range(3)
        ]
        for col in range(3):
            pivot_row = max(
                range(col, 3), key=lambda r: rows_left[r][col][0] ** 2 + rows_left[r][col][1] ** 2
            )
            rows_left[col], rows_left[pivot_row] = (rows_left[pivot_row], rows_left[col])
            leading = rows_left[col][col]
            rows_left[col] = [pair_div(v, leading) for v in rows_left[col]]
            for r in range(3):
                if r != col:
                    factor = rows_left[r][col]
                    rows_left[r] = [
                        pair_sub(a, pair_mul(factor, b))
                        for a, b in zip(rows_left[r], rows_left[col])
                    ]
        vector = [rows_left[i][3] for i in range(3)] + [(1.0, 0.0)]
        columns.append([v[0] for v in vector])
        columns.append([v[1] for v in vector])
        pairs.append((eigen_pair[0], eigen_pair[1]))
    eigen_basis = [[columns[j][i] for j in range(4)] for i in range(4)]
    basis_inverse = invert_table(eigen_basis)
    return (tableau, inverse, eigen_basis, basis_inverse, pairs)


def constants():
    tableau, inverse, eigen_basis, basis_inverse, pairs = radau_tables()
    shift_table = table_product(basis_inverse, inverse)
    shift_rows = [[v / step_size for v in row_values] for row_values in shift_table]
    pairs = [(p[0] / step_size, p[1] / step_size) for p in pairs]
    return eigen_basis, basis_inverse, shift_rows, pairs


def lane_ids(rows):
    return lax.broadcasted_iota(jnp.int32, (rows, LANES), 1)


def turn(cells, amount):
    return pltpu.roll(cells, amount % LANES, cells.ndim - 1)


def half_mask(rows, section):
    return (lane_ids(rows) < LANES // 2) == (section == 0)


def edges_kernel(own_ref, prev_ref, diff_ref, react_ref, same_ref, cross_ref):
    nz, nx = prev_ref.shape[0], prev_ref.shape[1]
    lanes = lane_ids(nx)
    first = lax.axis_index("section") == 0
    high, low = LANES - EDGE, 0
    same_from = jnp.where(first, high, low)
    cross_from = jnp.where(first, low, high)

    def pack(ref, start, slot, fields):
        parts = LANES // slot
        planes = nz // parts
        for z in range(planes):
            tile = jnp.zeros((nx, LANES), jnp.float32)
            for part in range(parts):
                for f, load in enumerate(fields):
                    at = part * slot + f * EDGE
                    moved = pltpu.roll(load(part * planes + z), lax.rem(at + LANES - start, LANES), 1)
                    tile = jnp.where((lanes >= at) & (lanes < at + EDGE), moved, tile)
            ref[z] = tile

    sections = [lambda z: own_ref[0, z], lambda z: own_ref[1, z]]
    others = [lambda z: prev_ref[z], lambda z: diff_ref[z], lambda z: react_ref[z]]
    pack(same_ref, same_from, 64, sections + others)
    pack(cross_ref, cross_from, 32, sections)


def rows_kernel(own_ref, other_ref, prev_ref, diff_ref, react_ref, same_ref, cross_ref, ring_ref, low_ref, high_ref):
    nz, nx = prev_ref.shape[0], prev_ref.shape[1]
    lanes = lane_ids(nx)
    first = lax.axis_index("section") == 0
    to = jnp.where(first, LANES - EDGE, 0)
    border = (lanes >= to) & (lanes < to + EDGE)

    def unpack(ref, slot, f, z):
        planes = nz // (LANES // slot)
        part, plane = divmod(z, planes)
        at = part * slot + f * EDGE
        return pltpu.roll(ref[plane], lax.rem(to + LANES - at, LANES), 1)

    for z in range(nz):
        cells = [own_ref[0, z], own_ref[1, z], other_ref[0, z], other_ref[1, z], prev_ref[z], diff_ref[z], react_ref[z]]
        for f, cell in enumerate(cells):
            side = unpack(cross_ref, 32, f - 2, z) if f in (2, 3) else unpack(same_ref, 64, (0, 1, 0, 0, 2, 3, 4)[f], z)
            cell = jnp.where(border, side, cell)
            ring_ref[f, z] = cell
            low_ref[z, 8 * f : 8 * f + 8] = cell[0:8]
            low_ref[z, 56 + f : 57 + f] = cell[8:9]
            high_ref[z, 8 * f : 8 * f + 8] = cell[nx - 8 : nx]
            high_ref[z, 56 + f : 57 + f] = cell[nx - 9 : nx - 8]
        low_ref[z, 63:64] = jnp.zeros((1, LANES), jnp.float32)
        high_ref[z, 63:64] = jnp.zeros((1, LANES), jnp.float32)


ROWS = 48
FIRST, LAST = 8, 40
OWN = slice(16, 32)
WORK = slice(FIRST, LAST)
BEFORE = slice(FIRST - 1, LAST - 1)
AFTER = slice(FIRST + 1, LAST + 1)


def each_plane(count, unroll, work):
    def group(i, carry):
        for u in range(unroll):
            work(i * unroll + u)
        return carry

    lax.fori_loop(0, count // unroll, group, 0)


def main_kernel(consts, ring_ref, from_low_ref, from_high_ref, part_ref, sums_ref,
                val, kap, frozen, fx, fy, fz, alpha, beta, vec, ya, yb, table):
    eigen_basis, basis_inverse, shift_rows, pairs = consts
    nz = ring_ref.shape[1]
    section = lax.axis_index("section")
    zero_plane = jnp.zeros((ROWS, LANES), jnp.float32)
    zero_rows = jnp.zeros((FIRST, LANES), jnp.float32)

    for edge in (0, nz + 1):
        frozen[edge] = zero_plane
        for f in range(4):
            for ref in (val, kap, ya, yb):
                ref[f, edge] = zero_plane

    def column(f, z):
        tile = lambda t: jnp.broadcast_to(t, (8, LANES))
        low, high = from_low_ref, from_high_ref
        return jnp.concatenate(
            [tile(low[z, 56 + f : 57 + f]), low[z, 8 * f : 8 * f + 8], ring_ref[f, z], high[z, 8 * f : 8 * f + 8], tile(high[z, 56 + f : 57 + f])], 0
        )

    def assemble(z):
        diff = column(5, z)
        frozen[z + 1] = diff * (0.5 + 0.25 * jnp.tanh(column(4, z)))
        for f in range(4):
            value = column(f, z)
            val[f, z + 1] = value
            kap[f, z + 1] = diff * (0.5 + 0.25 * jnp.tanh(value))
            for ref in (ya, yb):
                ref[f, z + 1, 0:FIRST] = zero_rows
                ref[f, z + 1, LAST:ROWS] = zero_rows

    each_plane(nz, 1, assemble)

    def pick(matrix, m, j):
        return jnp.where(section == 0, jnp.float32(matrix[m][j]), jnp.float32(matrix[m][(j + 2) % 4]))

    q_rows = [[pick(basis_inverse, m, j) for j in range(4)] for m in range(4)]
    c_rows = [[pick(shift_rows, m, j) for j in range(4)] for m in range(4)]

    def prepare(z):
        def middle(f):
            return jnp.concatenate([from_low_ref[z, 8 * f : 8 * f + 8], ring_ref[f, z], from_high_ref[z, 8 * f : 8 * f + 8]], 0)

        mid = frozen[z + 1, WORK]
        faces = [
            mid + frozen[z + 1, BEFORE], mid + frozen[z + 1, AFTER], mid + turn(mid, 1), mid + turn(mid, -1),
            mid + frozen[z, WORK], mid + frozen[z + 2, WORK],
        ]
        for at, ref in enumerate((fx, fy, fz)):
            ref[0, z] = faces[2 * at]
            ref[1, z] = faces[2 * at + 1]
        prev, react = middle(4), middle(6)
        base = ((faces[0] + faces[1]) + (faces[2] + faces[3])) + (faces[4] + faces[5]) - react * (1.0 - 3.0 * prev * prev)
        inside = jnp.where(middle(5) > 0.0, 1.0, 0.0)
        scaled = []
        for b in range(2):
            real, imag = pairs[b]
            diag = base + real
            scale = inside / (diag * diag + imag * imag)
            scaled.append((diag * scale, imag * scale))
            alpha[b, z], beta[b, z] = scaled[b]
        rhs = [None] * 4
        for j in range(4):
            v = val[j, z + 1, WORK]
            k = kap[j, z + 1, WORK]
            flux = react * v * (1.0 - v * v)
            flux = flux + (k + kap[j, z + 1, BEFORE]) * (val[j, z + 1, BEFORE] - v)
            flux = flux + (k + kap[j, z + 1, AFTER]) * (val[j, z + 1, AFTER] - v)
            flux = flux + (k + turn(k, 1)) * (turn(v, 1) - v)
            flux = flux + (k + turn(k, -1)) * (turn(v, -1) - v)
            flux = flux + (k + kap[j, z, WORK]) * (val[j, z, WORK] - v)
            flux = flux + (k + kap[j, z + 2, WORK]) * (val[j, z + 2, WORK] - v)
            grown = v - prev
            for m in range(4):
                term = q_rows[m][j] * flux - c_rows[m][j] * grown
                rhs[m] = term if j == 0 else rhs[m] + term
        for m in range(4):
            vec[0, m, z] = rhs[m]
        for b in range(2):
            al, be = scaled[b]
            ya[2 * b, z + 1, WORK] = al * rhs[2 * b] - be * rhs[2 * b + 1]
            ya[2 * b + 1, z + 1, WORK] = be * rhs[2 * b] + al * rhs[2 * b + 1]

    each_plane(nz, PREPARE_UNROLL, prepare)

    def spread(ref, m, z, rows=WORK):
        lo, hi = rows.start, rows.stop
        cut = slice(lo - FIRST, hi - FIRST)
        mid = ref[m, z + 1, lo:hi]
        in_y = fy[0, z, cut] * turn(mid, 1) + fy[1, z, cut] * turn(mid, -1)
        in_x = fx[0, z, cut] * ref[m, z + 1, lo - 1 : hi - 1] + fx[1, z, cut] * ref[m, z + 1, lo + 1 : hi + 1]
        in_z = fz[0, z, cut] * ref[m, z, lo:hi] + fz[1, z, cut] * ref[m, z + 2, lo:hi]
        return (in_x + in_z) + in_y

    for j in range(ITERS):

        def odd(z, j=j):
            for b in range(2):
                t0 = spread(ya, 2 * b, z)
                t1 = spread(ya, 2 * b + 1, z)
                al, be = alpha[b, z], beta[b, z]
                y0 = al * t0 - be * t1
                y1 = be * t0 + al * t1
                yb[2 * b, z + 1, WORK] = y0
                yb[2 * b + 1, z + 1, WORK] = y1
                sums_ref[j, 2 * b, z] = ya[2 * b, z + 1, OWN] + y0[8:24]
                sums_ref[j, 2 * b + 1, z] = ya[2 * b + 1, z + 1, OWN] + y1[8:24]

        def even(z, j=j):
            last = j == ITERS - 1
            rows = OWN if last else WORK
            cut = slice(rows.start - FIRST, rows.stop - FIRST)
            for b in range(2):
                new = []
                for m in (2 * b, 2 * b + 1):
                    v = spread(yb, m, z, rows)
                    if SHIFTS[j]:
                        v = v - SHIFTS[j] * vec[j, m, z, cut]
                    vec[j + 1, m, z, cut] = v
                    new.append(v)
                if not last:
                    al, be = alpha[b, z], beta[b, z]
                    ya[2 * b, z + 1, WORK] = al * new[0] - be * new[1]
                    ya[2 * b + 1, z + 1, WORK] = be * new[0] + al * new[1]

        each_plane(nz, STEP_UNROLL, odd)
        each_plane(nz, STEP_UNROLL, even)

    table[...] = jnp.zeros((LANES, LANES), jnp.float32)
    mine = half_mask(8, section)
    for b in range(2):

        def dots(z, carry):
            out = list(carry)
            for m in (2 * b, 2 * b + 1):
                for r in (8, 16):
                    cells = [vec[i, m, z, r : r + 8] for i in range(SIZE)]
                    for at, (i, j) in enumerate(PAIRS):
                        out[at] = out[at] + cells[i] * cells[j]
            return tuple(out)

        zero = jnp.zeros((8, LANES), jnp.float32)
        out = lax.fori_loop(0, nz, dots, tuple(zero for _ in PAIRS))
        for at in range(len(PAIRS)):
            row = jnp.sum(jnp.where(mine, out[at], 0.0), axis=0, keepdims=True)
            table[b * len(PAIRS) + at : b * len(PAIRS) + at + 1] = row
    total = jnp.sum(table[...].T, axis=0, keepdims=True)
    part_ref[...] = jnp.broadcast_to(total, part_ref.shape)


def step_weights(gram):
    table = {}
    for at, (i, j) in enumerate(PAIRS):
        table[i, j] = table[j, i] = gram[at]
    coef = [jnp.ones_like(gram[0])]
    weight = []
    step = coef[0]
    for k in range(ITERS):
        moved = [SHIFTS[j] * coef[j] for j in range(k + 1)] + [jnp.zeros_like(step)]
        for j in range(k + 1):
            moved[j + 1] = moved[j + 1] + coef[j]
        coef = coef + [jnp.zeros_like(step)]
        image = [coef[j] - moved[j] for j in range(k + 2)]
        num, den, bound = 0.0, 0.0, 0.0
        for i in range(k + 2):
            row, size = 0.0, 0.0
            for j in range(k + 2):
                term = table[i, j] * image[j]
                row = row + term
                size = size + jnp.abs(term)
            num = num + row * coef[i]
            den = den + row * image[i]
            bound = bound + size * jnp.abs(image[i])
        step = jnp.where(den > bound * 6e-8, num / (jnp.maximum(den, 0.0) + tiny_value), step)
        weight = weight + [jnp.zeros_like(step)]
        for j in range(k + 1):
            weight[j] = weight[j] + step * coef[j]
        coef = [coef[j] - step * image[j] for j in range(k + 2)]
    return weight


def finish_kernel(consts, total_ref, sums_ref, ring_ref, mine_ref, send_ref):
    eigen_basis = consts[0]
    nz, nx = mine_ref.shape[1], mine_ref.shape[2]
    section = lax.axis_index("section")
    total = jnp.sum(total_ref[...], axis=0, keepdims=True)
    count = len(PAIRS)
    weights = []
    for b in range(2):
        gram = [jnp.broadcast_to(total[:, b * count + at : b * count + at + 1], (1, LANES)) for at in range(count)]
        weights.append(step_weights(gram))
    basis = [
        [jnp.where(section == 0, jnp.float32(eigen_basis[r][m]), jnp.float32(eigen_basis[(r + 2) % 4][m])) for m in range(4)]
        for r in range(4)
    ]
    mine = half_mask(nx, section)

    def combine(z):
        outs = [ring_ref[r, z] for r in range(4)]
        for m in range(4):
            field = weights[m // 2][0] * sums_ref[0, m, z]
            for j in range(1, ITERS):
                field = field + weights[m // 2][j] * sums_ref[j, m, z]
            outs = [outs[r] + basis[r][m] * field for r in range(4)]
        mine_ref[0, z] = outs[0]
        mine_ref[1, z] = outs[1]
        send_ref[z] = jnp.where(mine, outs[2], turn(outs[3], LANES // 2))

    each_plane(nz, 2, combine)


def join_kernel(mine_ref, other_ref, out_ref):
    nz, nx = mine_ref.shape[1], mine_ref.shape[2]
    mine = half_mask(nx, lax.axis_index("section"))
    for z in range(nz):
        other = other_ref[z]
        out_ref[0, z] = jnp.where(mine, mine_ref[0, z], other)
        out_ref[1, z] = jnp.where(mine, mine_ref[1, z], turn(other, LANES // 2))


def call(kernel, outs, scratch=(), flops=1_000_000, name=None):
    many = isinstance(outs, list)
    shapes = [jax.ShapeDtypeStruct(o, jnp.float32) for o in (outs if many else [outs])]

    def run(*args):
        moved = 4 * sum(int(a.size) for a in args) + 4 * sum(int(functools.reduce(lambda p, q: p * q, s.shape, 1)) for s in shapes)
        return pl.pallas_call(
            kernel,
            out_shape=shapes if many else shapes[0],
            in_specs=[pl.BlockSpec(memory_space=pltpu.VMEM)] * len(args),
            out_specs=[pl.BlockSpec(memory_space=pltpu.VMEM)] * len(shapes) if many else pl.BlockSpec(memory_space=pltpu.VMEM),
            scratch_shapes=[pltpu.VMEM(s, jnp.float32) for s in scratch],
            compiler_params=pltpu.CompilerParams(vmem_limit_bytes=VMEM_LIMIT),
            cost_estimate=pl.CostEstimate(flops=flops, bytes_accessed=moved, transcendentals=0),
            name=name,
        )(*args)

    return run


def beside(count, cross):
    pairs = []
    for s in range(2):
        to = 1 - s if cross else s
        step = 1 if to == 0 else -1
        for i in range(count):
            if 0 <= i + step < count:
                pairs.append((s * count + i, to * count + i + step))
    return pairs


def neighbours(count, step):
    return [(i, i + step) for i in range(count) if 0 <= i + step < count]


def body(previous, sections, diffusivity, reaction):
    consts = constants()
    nz, nx, ny = previous.shape
    columns, rows = lax.axis_size("sy"), lax.axis_size("sx")
    swap = [(0, 1), (1, 0)]
    other = lax.ppermute(sections, "section", swap)
    same, cross = call(edges_kernel, [(nz // 2, nx, ny), (nz // 4, nx, ny)], name="edges")(sections, previous, diffusivity, reaction)
    same = lax.ppermute(same, ("section", "sy"), beside(columns, False))
    cross = lax.ppermute(cross, ("section", "sy"), beside(columns, True))
    ring, low_rows, high_rows = call(rows_kernel, [(7, nz, nx, ny), (nz, 64, ny), (nz, 64, ny)], name="rows")(
        sections, other, previous, diffusivity, reaction, same, cross
    )
    from_low = lax.ppermute(high_rows, "sx", neighbours(rows, 1))
    from_high = lax.ppermute(low_rows, "sx", neighbours(rows, -1))
    peers = 2 * columns * rows
    padded, work = (nz + 2, ROWS, ny), (nz, LAST - FIRST, ny)
    scratch = [
        (4,) + padded, (4,) + padded, padded, (2,) + work, (2,) + work, (2,) + work, (2,) + work, (2,) + work,
        (SIZE, 4) + work, (4,) + padded, (4,) + padded, (LANES, LANES),
    ]
    part, sums = call(
        functools.partial(main_kernel, consts), [(peers, LANES), (ITERS, 4, nz, nx, ny)], scratch, 50_000_000, name="main"
    )(ring, from_low, from_high)
    total = lax.all_to_all(part.reshape(peers, 1, LANES), ("section", "sx", "sy"), 0, 0).reshape(peers, LANES)
    mine, send = call(functools.partial(finish_kernel, consts), [sections.shape, previous.shape], name="finish")(total, sums, ring)
    got = lax.ppermute(send, "section", swap)
    return call(join_kernel, sections.shape, name="join")(mine, got)


def solution(mesh):
    in_specs = (
        P(None, "sx", "sy"),
        P("section", None, "sx", "sy"),
        P(None, "sx", "sy"),
        P(None, "sx", "sy"),
    )
    out_specs = P("section", None, "sx", "sy")
    return jax.shard_map(body, mesh=mesh, in_specs=in_specs, out_specs=out_specs, check_vma=False)
```

time: 108 us -> 89.4 us (0.83)
  Pallas kernels: 44.9 us -> 25.8 us
  blocking collectives: 24 us -> 30.2 us
  starting transfers between devices: 19.6 us -> 15.6 us
  waiting for transfers between devices: 17.4 us -> 14.7 us
    pallas_call x4 -> x5, Pallas kernels: 44.9 us -> 25.8 us  [run(): pl.pallas_call(kernel, out_shape=shapes if many else shapes[0], in_specs=...]
    all_to_all x1, blocking collectives: 24 us -> 30.2 us  [body(): lax.all_to_all(part.reshape(peers, 1, LANES), ('section', 'sx', 'sy'), 0, 0)]
    ppermute x5 -> x4, starting transfers between devices: 12.3 us -> 8.49 us  [the longest x1 3.74 us: body(): other = lax.ppermute(sections, 'section', swap)]
    ppermute x5 -> x4, waiting for transfers between devices: 7.91 us -> 5.88 us  [the longest x1 4.94 us: body(): got = lax.ppermute(send, 'section', swap)]
    unnamed x14 -> x12, local copies, waits for them, and re-layouts: 2.13 us -> 2.75 us
  transfers between devices with their start and end apart: 7 -> 6, of which waited for: 4 -> 4; matrix products, arithmetic and copies ran while one was open for 0% -> 0% of each run, Pallas kernels for 2% -> 2%
where the time goes in v2:
time: 89.4 us; the launch traced here: 89.1 us
  blocking collectives  30.2 us (34%)
  Pallas kernels  25.8 us (29%)
  starting transfers between devices  15.6 us (17%)
  waiting for transfers between devices  14.7 us (16%)
  local copies, waits for them, and re-layouts  2.75 us (3%)
    all_to_all x1, blocking collectives, body(): lax.all_to_all(part.reshape(peers, 1, LANES), ('section', 'sx', 'sy'), 0, 0)  30.2 us
    pallas_call x5, Pallas kernels, run(): pl.pallas_call(kernel, out_shape=shapes if many else shapes[0], in_specs=...  25.8 us
    ppermute x1, starting transfers between devices, body(): from_low = lax.ppermute(high_rows, 'sx', neighbours(rows, 1))  5.23 us
    ppermute x1, waiting for transfers between devices, body(): got = lax.ppermute(send, 'section', swap)  4.94 us
    ppermute x1, waiting for transfers between devices, body(): from_low = lax.ppermute(high_rows, 'sx', neighbours(rows, 1))  4.49 us
    ppermute x1, waiting for transfers between devices, body(): from_high = lax.ppermute(low_rows, 'sx', neighbours(rows, -1))  4.29 us
    ppermute x1, starting transfers between devices, body(): other = lax.ppermute(sections, 'section', swap)  3.74 us
    ppermute x1, starting transfers between devices, body(): same = lax.ppermute(same, ('section', 'sy'), beside(columns, False))  3.11 us
  transfers between devices with their start and end apart: 6, of which 4 were waited for; matrix products, arithmetic and copies ran while one was open for 0% of the time, Pallas kernels for 2%

profile of v2, /device:TPU:1, one launch (start us, length us, event | category | flops | bytes accessed | tf_op | source)
XLA Modules:
  0.0 89.1 jit_solution(791467007243446334)
XLA Ops:
  0.0 3.7 %collective-permute-start = (f32[2,16,16,128]{3,2,1,0:T(8,128)}, f32[2,16,16,128]{3,2,1,0:T(8,128)S(1)}, u32[]{:S(2)}, u32[]{:S(2)}) collective-permute-start(f32[2,16,16,128]{3,2,1,0:T(8,128)} %own_ref.3), channel_id=1, source_target_pairs={{0,128},{128,0},{1,129},{129,1},{2,130},{130,2},{3,131},{131,3},{4... | collective-permute-start | bytes 786440 | tf_op jit(solution)/shard_map/ppermute | solution.py:516
  3.7 2.0 %edges.1 = (f32[8,16,128]{2,1,0:T(8,128)}, f32[4,16,128]{2,1,0:T(8,128)}) custom-call(f32[2,16,16,128]{3,2,1,0:T(8,128)} %own_ref.3, f32[16,16,128]{2,1,0:T(8,128)} %prev_ref.3, f32[16,16,128]{2,1,0:T(8,128)} %diff_ref.3, f32[16,16,128]{2,1,0:T(8,128)} %react_ref.3), custom_call_target="tpu_custom_call" | custom-call | flops 1000000 | bytes 753664 | tf_op jit(solution)/shard_map/edges/pallas_call | solution.py:482
  5.8 3.1 %collective-permute-start.1 = (f32[8,16,128]{2,1,0:T(8,128)}, f32[8,16,128]{2,1,0:T(8,128)S(1)}, u32[]{:S(2)}, u32[]{:S(2)}) collective-permute-start(f32[8,16,128]{2,1,0:T(8,128)} %get-tuple-element.14), channel_id=1, source_target_pairs={{0,1},{1,2},{2,3},{3,4},{4,5},{5,6},{6,7},{129,128},{130,129},{131... | collective-permute-start | bytes 196616 | tf_op jit(solution)/shard_map/ppermute | solution.py:518
  8.9 0.7 collective-permute-start.2
  9.6 0.0 collective-permute-done.2.cross_ref
  9.6 0.9 %collective-permute-done.1.same_ref = f32[8,16,128]{2,1,0:T(8,128)S(1)} collective-permute-done((f32[8,16,128]{2,1,0:T(8,128)}, f32[8,16,128]{2,1,0:T(8,128)S(1)}, u32[]{:S(2)}, u32[]{:S(2)}) %collective-permute-start.1) | collective-permute-done | bytes 65568 | tf_op jit(solution)/shard_map/ppermute | solution.py:518
  10.5 0.0 collective-permute-done.other_ref
  10.5 0.0 copy-done.5
  10.5 0.6 copy-done.4
  11.1 0.7 copy-done.2
  11.8 2.8 %rows.1 = (f32[7,16,16,128]{3,2,1,0:T(8,128)}, f32[16,64,128]{2,1,0:T(8,128)}, f32[16,64,128]{2,1,0:T(8,128)}) custom-call(f32[2,16,16,128]{3,2,1,0:T(8,128)} %own_ref.3, f32[2,16,16,128]{3,2,1,0:T(8,128)} %copy-done.2, f32[16,16,128]{2,1,0:T(8,128)} %prev_ref.3, f32[16,16,128]{2,1,0:T(8,128)} %diff_ref.3, f32[16,16,128]{2,1,0:T(8,128)} %react_ref.3, ...), custom_call_target="tpu_custom_call" | custom-call | flops 1000000 | bytes 2981888 | tf_op jit(solution)/shard_map/rows/pallas_call | solution.py:482
  14.6 5.2 %collective-permute-start.3 = (f32[16,64,128]{2,1,0:T(8,128)}, f32[16,64,128]{2,1,0:T(8,128)S(1)}, u32[]{:S(2)}, u32[]{:S(2)}) collective-permute-start(f32[16,64,128]{2,1,0:T(8,128)} %get-tuple-element.17), channel_id=1, source_target_pairs={{0,8},{8,16},{16,24},{24,32},{32,40},{40,48},{48,56},{56,64},{64,7... | collective-permute-start | bytes 1572872 | tf_op jit(solution)/shard_map/ppermute | solution.py:523
  19.9 1.9 %collective-permute-start.4 = (f32[16,64,128]{2,1,0:T(8,128)}, f32[16,64,128]{2,1,0:T(8,128)S(1)}, u32[]{:S(2)}, u32[]{:S(2)}) collective-permute-start(f32[16,64,128]{2,1,0:T(8,128)} %get-tuple-element.18), channel_id=1, source_target_pairs={{8,0},{16,8},{24,16},{32,24},{40,32},{48,40},{56,48},{64,56},{72,6... | collective-permute-start | bytes 1572872 | tf_op jit(solution)/shard_map/ppermute | solution.py:524
  21.8 4.5 %collective-permute-done.3.from_low_ref = f32[16,64,128]{2,1,0:T(8,128)S(1)} collective-permute-done((f32[16,64,128]{2,1,0:T(8,128)}, f32[16,64,128]{2,1,0:T(8,128)S(1)}, u32[]{:S(2)}, u32[]{:S(2)}) %collective-permute-start.3) | collective-permute-done | bytes 524320 | tf_op jit(solution)/shard_map/ppermute | solution.py:523
  26.3 4.3 %collective-permute-done.4.from_high_ref = f32[16,64,128]{2,1,0:T(8,128)S(1)} collective-permute-done((f32[16,64,128]{2,1,0:T(8,128)}, f32[16,64,128]{2,1,0:T(8,128)S(1)}, u32[]{:S(2)}, u32[]{:S(2)}) %collective-permute-start.4) | collective-permute-done | bytes 524320 | tf_op jit(solution)/shard_map/ppermute | solution.py:524
  30.6 0.0 copy-done
  30.6 0.8 copy-done.1
  31.4 15.6 %main.1 = (f32[256,128]{1,0:T(8,128)}, f32[4,4,16,16,128]{4,3,2,1,0:T(8,128)}) custom-call(f32[7,16,16,128]{3,2,1,0:T(8,128)} %get-tuple-element.16.ring_ref, f32[16,64,128]{2,1,0:T(8,128)} %copy-done, f32[16,64,128]{2,1,0:T(8,128)} %copy-done.1), custom_call_target="tpu_custom_call" | custom-call | flops 50000000 | bytes 4194304 | tf_op jit(solution)/shard_map/main/pallas_call | solution.py:482
  46.9 30.2 %all_to_all.5 = f32[256,1,128]{2,1,0:T(1,128)} all-to-all(f32[256,1,128]{2,1,0:T(1,128)} %bitcast.5), channel_id=1, replica_groups=mesh['section'=2,'sx'=16,'sy'=8] {'section','sx','sy'}, dimensions={0} | all-to-all | bytes 262144 | tf_op jit(solution)/shard_map/all_to_all | solution.py:534
  77.1 3.6 %finish.1 = (f32[2,16,16,128]{3,2,1,0:T(8,128)}, f32[16,16,128]{2,1,0:T(8,128)}) custom-call(f32[256,128]{1,0:T(8,128)} %bitcast.4, f32[4,4,16,16,128]{4,3,2,1,0:T(8,128)} %get-tuple-element.20.sums_ref, f32[7,16,16,128]{3,2,1,0:T(8,128)} %get-tuple-element.16.ring_ref), custom_call_target="tpu_custom_call" | custom-call | flops 1000000 | bytes 3538944 | tf_op jit(solution)/shard_map/finish/pallas_call | solution.py:482
  80.7 1.0 %collective-permute-start.5 = (f32[16,16,128]{2,1,0:T(8,128)}, f32[16,16,128]{2,1,0:T(8,128)S(1)}, u32[]{:S(2)}, u32[]{:S(2)}) collective-permute-start(f32[16,16,128]{2,1,0:T(8,128)} %get-tuple-element.22), channel_id=1, source_target_pairs={{0,128},{128,0},{1,129},{129,1},{2,130},{130,2},{3,131},{131,3},{4... | collective-permute-start | bytes 393224 | tf_op jit(solution)/shard_map/ppermute | solution.py:536
  81.7 4.9 %collective-permute-done.5.other_ref = f32[16,16,128]{2,1,0:T(8,128)S(1)} collective-permute-done((f32[16,16,128]{2,1,0:T(8,128)}, f32[16,16,128]{2,1,0:T(8,128)S(1)}, u32[]{:S(2)}, u32[]{:S(2)}) %collective-permute-start.5) | collective-permute-done | bytes 131104 | tf_op jit(solution)/shard_map/ppermute | solution.py:536
  86.6 0.7 copy-done.3
  87.3 1.8 %join.1 = f32[2,16,16,128]{3,2,1,0:T(8,128)} custom-call(f32[2,16,16,128]{3,2,1,0:T(8,128)} %get-tuple-element.21.mine_ref, f32[16,16,128]{2,1,0:T(8,128)} %copy-done.3), custom_call_target="tpu_custom_call" | custom-call | flops 1000000 | bytes 655360 | tf_op jit(solution)/shard_map/join/pallas_call | solution.py:482
  (6 shorter events, 0.0 us)
Async XLA Ops:
  0.0 10.5 %collective-permute-start = (f32[2,16,16,128]{3,2,1,0:T(8,128)}, f32[2,16,16,128]{3,2,1,0:T(8,128)S(1)}, u32[]{:S(2)}, u32[]{:S(2)}) collective-permute-start(f32[2,16,16,128]{3,2,1,0:T(8,128)} %own_ref.3), channel_id=1, source_target_pairs={{0,128},{128,0},{1,129},{129,1},{2,130},{130,2},{3,131},{131,3},{4... | collective-permute-start | bytes 786440 | tf_op jit(solution)/shard_map/ppermute | solution.py:516
  5.8 4.7 %collective-permute-start.1 = (f32[8,16,128]{2,1,0:T(8,128)}, f32[8,16,128]{2,1,0:T(8,128)S(1)}, u32[]{:S(2)}, u32[]{:S(2)}) collective-permute-start(f32[8,16,128]{2,1,0:T(8,128)} %get-tuple-element.14), channel_id=1, source_target_pairs={{0,1},{1,2},{2,3},{3,4},{4,5},{5,6},{6,7},{129,128},{130,129},{131... | collective-permute-start | bytes 196616 | tf_op jit(solution)/shard_map/ppermute | solution.py:518
  8.9 0.7 collective-permute-start.2
  9.6 1.0 %copy-start.5 = (f32[4,16,128]{2,1,0:T(8,128)}, f32[4,16,128]{2,1,0:T(8,128)S(1)}, u32[]{:S(2)}) copy-start(f32[4,16,128]{2,1,0:T(8,128)S(1)} %collective-permute-done.2.cross_ref) | copy-start | bytes 98308
  10.5 0.6 copy-start.4
  11.1 0.7 copy-start.2
  14.6 11.7 %collective-permute-start.3 = (f32[16,64,128]{2,1,0:T(8,128)}, f32[16,64,128]{2,1,0:T(8,128)S(1)}, u32[]{:S(2)}, u32[]{:S(2)}) collective-permute-start(f32[16,64,128]{2,1,0:T(8,128)} %get-tuple-element.17), channel_id=1, source_target_pairs={{0,8},{8,16},{16,24},{24,32},{32,40},{40,48},{48,56},{56,64},{64,7... | collective-permute-start | bytes 1572872 | tf_op jit(solution)/shard_map/ppermute | solution.py:523
  19.9 10.7 %collective-permute-start.4 = (f32[16,64,128]{2,1,0:T(8,128)}, f32[16,64,128]{2,1,0:T(8,128)S(1)}, u32[]{:S(2)}, u32[]{:S(2)}) collective-permute-start(f32[16,64,128]{2,1,0:T(8,128)} %get-tuple-element.18), channel_id=1, source_target_pairs={{8,0},{16,8},{24,16},{32,24},{40,32},{48,40},{56,48},{64,56},{72,6... | collective-permute-start | bytes 1572872 | tf_op jit(solution)/shard_map/ppermute | solution.py:524
  26.3 4.3 %copy-start = (f32[16,64,128]{2,1,0:T(8,128)}, f32[16,64,128]{2,1,0:T(8,128)S(1)}, u32[]{:S(2)}) copy-start(f32[16,64,128]{2,1,0:T(8,128)S(1)} %collective-permute-done.3.from_low_ref) | copy-start | bytes 1572868
  30.6 0.8 copy-start.1
  80.7 5.9 %collective-permute-start.5 = (f32[16,16,128]{2,1,0:T(8,128)}, f32[16,16,128]{2,1,0:T(8,128)S(1)}, u32[]{:S(2)}, u32[]{:S(2)}) collective-permute-start(f32[16,16,128]{2,1,0:T(8,128)} %get-tuple-element.22), channel_id=1, source_target_pairs={{0,128},{128,0},{1,129},{129,1},{2,130},{130,2},{3,131},{131,3},{4... | collective-permute-start | bytes 393224 | tf_op jit(solution)/shard_map/ppermute | solution.py:536
  86.6 0.7 copy-start.3

commit v3 on v2

--- a/solution.py
+++ b/solution.py
@@ -13,8 +13,8 @@
 LANES = 128
 SIZE = ITERS + 1
 PAIRS = [(i, j) for i in range(SIZE) for j in range(i, SIZE)]
-PREPARE_UNROLL = 1
-STEP_UNROLL = 2
+PREPARE_UNROLL = 2
+STEP_UNROLL = 8
 VMEM_LIMIT = 58 * 1024 * 1024
 
 
@@ -182,57 +182,63 @@
     return (lane_ids(rows) < LANES // 2) == (section == 0)
 
 
-def edges_kernel(own_ref, prev_ref, diff_ref, react_ref, same_ref, cross_ref):
+MINE = (0, 1, 4, 5, 6)
+
+
+def border_start():
+    first = lax.axis_index("section") == 0
+    high, low = LANES - EDGE, 0
+    return jnp.where(first, high, low)
+
+
+def pack_border(tile, cell, field, part, lanes, start):
+    at = part * 64 + field * EDGE
+    moved = pltpu.roll(cell, lax.rem(at + LANES - start, LANES), 1)
+    return jnp.where((lanes >= at) & (lanes < at + EDGE), moved, tile)
+
+
+def pack_rows(low_ref, high_ref, cells, z, nx):
+    count = len(cells)
+    for f, cell in enumerate(cells):
+        low_ref[z, 8 * f : 8 * f + 8] = cell[0:8]
+        low_ref[z, 8 * count + f : 8 * count + f + 1] = cell[8:9]
+        high_ref[z, 8 * f : 8 * f + 8] = cell[nx - 8 : nx]
+        high_ref[z, 8 * count + f : 8 * count + f + 1] = cell[nx - 9 : nx - 8]
+    rest = low_ref.shape[1] - 9 * count
+    for ref in (low_ref, high_ref):
+        ref[z, 9 * count :] = jnp.zeros((rest, LANES), jnp.float32)
+
+
+def own_kernel(own_ref, prev_ref, diff_ref, react_ref, border_ref, low_ref, high_ref):
     nz, nx = prev_ref.shape[0], prev_ref.shape[1]
     lanes = lane_ids(nx)
-    first = lax.axis_index("section") == 0
-    high, low = LANES - EDGE, 0
-    same_from = jnp.where(first, high, low)
-    cross_from = jnp.where(first, low, high)
-
-    def pack(ref, start, slot, fields):
-        parts = LANES // slot
-        planes = nz // parts
-        for z in range(planes):
-            tile = jnp.zeros((nx, LANES), jnp.float32)
-            for part in range(parts):
-                for f, load in enumerate(fields):
-                    at = part * slot + f * EDGE
-                    moved = pltpu.roll(load(part * planes + z), lax.rem(at + LANES - start, LANES), 1)
-                    tile = jnp.where((lanes >= at) & (lanes < at + EDGE), moved, tile)
-            ref[z] = tile
-
-    sections = [lambda z: own_ref[0, z], lambda z: own_ref[1, z]]
-    others = [lambda z: prev_ref[z], lambda z: diff_ref[z], lambda z: react_ref[z]]
-    pack(same_ref, same_from, 64, sections + others)
-    pack(cross_ref, cross_from, 32, sections)
-
-
-def rows_kernel(own_ref, other_ref, prev_ref, diff_ref, react_ref, same_ref, cross_ref, ring_ref, low_ref, high_ref):
-    nz, nx = prev_ref.shape[0], prev_ref.shape[1]
+    start = border_start()
+    half = nz // 2
+    for plane in range(half):
+        tile = jnp.zeros((nx, LANES), jnp.float32)
+        for part in range(2):
+            z = part * half + plane
+            cells = [own_ref[0, z], own_ref[1, z], prev_ref[z], diff_ref[z], react_ref[z]]
+            for f, cell in zip(MINE, cells):
+                tile = pack_border(tile, cell, f, part, lanes, start)
+            pack_rows(low_ref, high_ref, cells, z, nx)
+        border_ref[plane] = tile
+
+
+def other_kernel(other_ref, partial_ref, border_ref, low_ref, high_ref):
+    nz, nx = other_ref.shape[1], other_ref.shape[2]
     lanes = lane_ids(nx)
-    first = lax.axis_index("section") == 0
-    to = jnp.where(first, LANES - EDGE, 0)
-    border = (lanes >= to) & (lanes < to + EDGE)
-
-    def unpack(ref, slot, f, z):
-        planes = nz // (LANES // slot)
-        part, plane = divmod(z, planes)
-        at = part * slot + f * EDGE
-        return pltpu.roll(ref[plane], lax.rem(to + LANES - at, LANES), 1)
-
-    for z in range(nz):
-        cells = [own_ref[0, z], own_ref[1, z], other_ref[0, z], other_ref[1, z], prev_ref[z], diff_ref[z], react_ref[z]]
-        for f, cell in enumerate(cells):
-            side = unpack(cross_ref, 32, f - 2, z) if f in (2, 3) else unpack(same_ref, 64, (0, 1, 0, 0, 2, 3, 4)[f], z)
-            cell = jnp.where(border, side, cell)
-            ring_ref[f, z] = cell
-            low_ref[z, 8 * f : 8 * f + 8] = cell[0:8]
-            low_ref[z, 56 + f : 57 + f] = cell[8:9]
-            high_ref[z, 8 * f : 8 * f + 8] = cell[nx - 8 : nx]
-            high_ref[z, 56 + f : 57 + f] = cell[nx - 9 : nx - 8]
-        low_ref[z, 63:64] = jnp.zeros((1, LANES), jnp.float32)
-        high_ref[z, 63:64] = jnp.zeros((1, LANES), jnp.float32)
+    start = border_start()
+    half = nz // 2
+    for plane in range(half):
+        tile = partial_ref[plane]
+        for part in range(2):
+            z = part * half + plane
+            cells = [other_ref[0, z], other_ref[1, z]]
+            for f, cell in enumerate(cells):
+                tile = pack_border(tile, cell, 2 + f, part, lanes, start)
+            pack_rows(low_ref, high_ref, cells, z, nx)
+        border_ref[plane] = tile
 
 
 ROWS = 48
@@ -252,39 +258,64 @@
     lax.fori_loop(0, count // unroll, group, 0)
 
 
-def main_kernel(consts, ring_ref, from_low_ref, from_high_ref, part_ref, sums_ref,
-                val, kap, frozen, fx, fy, fz, alpha, beta, vec, ya, yb, table):
+def main_kernel(consts, own_ref, other_ref, prev_ref, diff_ref, react_ref, own_low_ref, own_high_ref, other_low_ref, other_high_ref,
+                border_ref, corner_low_ref, corner_high_ref, part_ref, sums_ref,
+                val, kap, frozen, prv, rea, dif, fx, fy, fz, alpha, beta, vec, ya, yb, table):
     eigen_basis, basis_inverse, shift_rows, pairs = consts
-    nz = ring_ref.shape[1]
+    nz, nx = prev_ref.shape[0], prev_ref.shape[1]
     section = lax.axis_index("section")
     zero_plane = jnp.zeros((ROWS, LANES), jnp.float32)
     zero_rows = jnp.zeros((FIRST, LANES), jnp.float32)
-
-    for edge in (0, nz + 1):
-        frozen[edge] = zero_plane
+    start = border_start()
+    lanes = lane_ids(ROWS)
+    edge = (lanes >= start) & (lanes < start + EDGE)
+    tile = lambda t: jnp.broadcast_to(t, (8, LANES))
+
+    for at in (0, nz + 1):
+        frozen[at] = zero_plane
         for f in range(4):
             for ref in (val, kap, ya, yb):
-                ref[f, edge] = zero_plane
-
-    def column(f, z):
-        tile = lambda t: jnp.broadcast_to(t, (8, LANES))
-        low, high = from_low_ref, from_high_ref
-        return jnp.concatenate(
-            [tile(low[z, 56 + f : 57 + f]), low[z, 8 * f : 8 * f + 8], ring_ref[f, z], high[z, 8 * f : 8 * f + 8], tile(high[z, 56 + f : 57 + f])], 0
+                ref[f, at] = zero_plane
+
+    def assemble(plane):
+        sides = jnp.concatenate(
+            [
+                tile(corner_low_ref[plane, nx - 9 : nx - 8]), corner_low_ref[plane, nx - 8 : nx], border_ref[plane],
+                corner_high_ref[plane, 0:8], tile(corner_high_ref[plane, 8:9]),
+            ],
+            0,
         )
-
-    def assemble(z):
-        diff = column(5, z)
-        frozen[z + 1] = diff * (0.5 + 0.25 * jnp.tanh(column(4, z)))
-        for f in range(4):
-            value = column(f, z)
-            val[f, z + 1] = value
-            kap[f, z + 1] = diff * (0.5 + 0.25 * jnp.tanh(value))
-            for ref in (ya, yb):
-                ref[f, z + 1, 0:FIRST] = zero_rows
-                ref[f, z + 1, LAST:ROWS] = zero_rows
-
-    each_plane(nz, 1, assemble)
+        for part in range(2):
+            z = part * (nz // 2) + plane
+
+            def column(f):
+                if f in (2, 3):
+                    low, high, slot, count, mid = other_low_ref, other_high_ref, f - 2, 2, other_ref[f - 2, z]
+                else:
+                    slot, count = MINE.index(f), len(MINE)
+                    low, high = own_low_ref, own_high_ref
+                    mid = (own_ref[0, z], own_ref[1, z], prev_ref[z], diff_ref[z], react_ref[z])[slot]
+                ninth = 8 * count + slot
+                cells = jnp.concatenate(
+                    [tile(low[z, ninth : ninth + 1]), low[z, 8 * slot : 8 * slot + 8], mid, high[z, 8 * slot : 8 * slot + 8], tile(high[z, ninth : ninth + 1])], 0
+                )
+                at = part * 64 + f * EDGE
+                return jnp.where(edge, pltpu.roll(sides, lax.rem(start + LANES - at, LANES), 1), cells)
+
+            diff, prev, react = column(5), column(4), column(6)
+            frozen[z + 1] = diff * (0.5 + 0.25 * jnp.tanh(prev))
+            prv[z] = prev[WORK]
+            rea[z] = react[WORK]
+            dif[z] = diff[WORK]
+            for f in range(4):
+                value = column(f)
+                val[f, z + 1] = value
+                kap[f, z + 1] = diff * (0.5 + 0.25 * jnp.tanh(value))
+                for ref in (ya, yb):
+                    ref[f, z + 1, 0:FIRST] = zero_rows
+                    ref[f, z + 1, LAST:ROWS] = zero_rows
+
+    each_plane(nz // 2, 1, assemble)
 
     def pick(matrix, m, j):
         return jnp.where(section == 0, jnp.float32(matrix[m][j]), jnp.float32(matrix[m][(j + 2) % 4]))
@@ -293,9 +324,6 @@
     c_rows = [[pick(shift_rows, m, j) for j in range(4)] for m in range(4)]
 
     def prepare(z):
-        def middle(f):
-            return jnp.concatenate([from_low_ref[z, 8 * f : 8 * f + 8], ring_ref[f, z], from_high_ref[z, 8 * f : 8 * f + 8]], 0)
-
         mid = frozen[z + 1, WORK]
         faces = [
             mid + frozen[z + 1, BEFORE], mid + frozen[z + 1, AFTER], mid + turn(mid, 1), mid + turn(mid, -1),
@@ -304,9 +332,9 @@
         for at, ref in enumerate((fx, fy, fz)):
             ref[0, z] = faces[2 * at]
             ref[1, z] = faces[2 * at + 1]
-        prev, react = middle(4), middle(6)
+        prev, react = prv[z], rea[z]
         base = ((faces[0] + faces[1]) + (faces[2] + faces[3])) + (faces[4] + faces[5]) - react * (1.0 - 3.0 * prev * prev)
-        inside = jnp.where(middle(5) > 0.0, 1.0, 0.0)
+        inside = jnp.where(dif[z] > 0.0, 1.0, 0.0)
         scaled = []
         for b in range(2):
             real, imag = pairs[b]
@@ -434,9 +462,9 @@
     return weight
 
 
-def finish_kernel(consts, total_ref, sums_ref, ring_ref, mine_ref, send_ref):
+def send_kernel(consts, total_ref, sums_ref, other_ref, send_ref, weight_ref):
     eigen_basis = consts[0]
-    nz, nx = mine_ref.shape[1], mine_ref.shape[2]
+    nz, nx = other_ref.shape[1], other_ref.shape[2]
     section = lax.axis_index("section")
     total = jnp.sum(total_ref[...], axis=0, keepdims=True)
     count = len(PAIRS)
@@ -444,24 +472,48 @@
     for b in range(2):
         gram = [jnp.broadcast_to(total[:, b * count + at : b * count + at + 1], (1, LANES)) for at in range(count)]
         weights.append(step_weights(gram))
+    for b in range(2):
+        for j in range(ITERS):
+            weight_ref[b * ITERS + j : b * ITERS + j + 1] = weights[b][j]
     basis = [
-        [jnp.where(section == 0, jnp.float32(eigen_basis[r][m]), jnp.float32(eigen_basis[(r + 2) % 4][m])) for m in range(4)]
-        for r in range(4)
+        [jnp.where(section == 0, jnp.float32(eigen_basis[2 + r][m]), jnp.float32(eigen_basis[r][m])) for m in range(4)]
+        for r in range(2)
     ]
     mine = half_mask(nx, section)
 
     def combine(z):
-        outs = [ring_ref[r, z] for r in range(4)]
+        outs = [other_ref[r, z] for r in range(2)]
         for m in range(4):
             field = weights[m // 2][0] * sums_ref[0, m, z]
             for j in range(1, ITERS):
                 field = field + weights[m // 2][j] * sums_ref[j, m, z]
-            outs = [outs[r] + basis[r][m] * field for r in range(4)]
+            outs = [outs[r] + basis[r][m] * field for r in range(2)]
+        send_ref[z] = jnp.where(mine, outs[0], turn(outs[1], LANES // 2))
+
+    each_plane(nz, 4, combine)
+
+
+def mine_kernel(consts, weight_ref, sums_ref, own_ref, mine_ref):
+    eigen_basis = consts[0]
+    nz = own_ref.shape[1]
+    section = lax.axis_index("section")
+    weights = [[weight_ref[b * ITERS + j : b * ITERS + j + 1] for j in range(ITERS)] for b in range(2)]
+    basis = [
+        [jnp.where(section == 0, jnp.float32(eigen_basis[r][m]), jnp.float32(eigen_basis[2 + r][m])) for m in range(4)]
+        for r in range(2)
+    ]
+
+    def combine(z):
+        outs = [own_ref[r, z] for r in range(2)]
+        for m in range(4):
+            field = weights[m // 2][0] * sums_ref[0, m, z]
+            for j in range(1, ITERS):
+                field = field + weights[m // 2][j] * sums_ref[j, m, z]
+            outs = [outs[r] + basis[r][m] * field for r in range(2)]
         mine_ref[0, z] = outs[0]
         mine_ref[1, z] = outs[1]
-        send_ref[z] = jnp.where(mine, outs[2], turn(outs[3], LANES // 2))
-
-    each_plane(nz, 2, combine)
+
+    each_plane(nz, 4, combine)
 
 
 def join_kernel(mine_ref, other_ref, out_ref):
@@ -493,47 +545,47 @@
     return run
 
 
-def beside(count, cross):
+def grid_pairs(columns, rows, x_step, y_out):
     pairs = []
     for s in range(2):
-        to = 1 - s if cross else s
-        step = 1 if to == 0 else -1
-        for i in range(count):
-            if 0 <= i + step < count:
-                pairs.append((s * count + i, to * count + i + step))
+        y_step = (1 - 2 * s) if y_out else 0
+        for x in range(rows):
+            for y in range(columns):
+                if 0 <= x + x_step < rows and 0 <= y + y_step < columns:
+                    pairs.append(((s * rows + x) * columns + y, (s * rows + x + x_step) * columns + y + y_step))
     return pairs
-
-
-def neighbours(count, step):
-    return [(i, i + step) for i in range(count) if 0 <= i + step < count]
 
 
 def body(previous, sections, diffusivity, reaction):
     consts = constants()
     nz, nx, ny = previous.shape
     columns, rows = lax.axis_size("sy"), lax.axis_size("sx")
+    axes = ("section", "sx", "sy")
     swap = [(0, 1), (1, 0)]
+    send = lambda a, x_step, y_out: lax.ppermute(a, axes, grid_pairs(columns, rows, x_step, y_out))
     other = lax.ppermute(sections, "section", swap)
-    same, cross = call(edges_kernel, [(nz // 2, nx, ny), (nz // 4, nx, ny)], name="edges")(sections, previous, diffusivity, reaction)
-    same = lax.ppermute(same, ("section", "sy"), beside(columns, False))
-    cross = lax.ppermute(cross, ("section", "sy"), beside(columns, True))
-    ring, low_rows, high_rows = call(rows_kernel, [(7, nz, nx, ny), (nz, 64, ny), (nz, 64, ny)], name="rows")(
-        sections, other, previous, diffusivity, reaction, same, cross
+    partial, low, high = call(own_kernel, [(nz // 2, nx, ny), (nz, 48, ny), (nz, 48, ny)], name="own")(
+        sections, previous, diffusivity, reaction
     )
-    from_low = lax.ppermute(high_rows, "sx", neighbours(rows, 1))
-    from_high = lax.ppermute(low_rows, "sx", neighbours(rows, -1))
+    own_low, own_high = send(high, 1, False), send(low, -1, False)
+    other, own_low, own_high = lax.optimization_barrier((other, own_low, own_high))
+    border, low, high = call(other_kernel, [(nz // 2, nx, ny), (nz, 24, ny), (nz, 24, ny)], name="other")(other, partial)
+    other_low, other_high = send(high, 1, False), send(low, -1, False)
+    side = send(border, 0, True)
+    corner_low, corner_high = send(border, 1, True), send(border, -1, True)
     peers = 2 * columns * rows
     padded, work = (nz + 2, ROWS, ny), (nz, LAST - FIRST, ny)
     scratch = [
-        (4,) + padded, (4,) + padded, padded, (2,) + work, (2,) + work, (2,) + work, (2,) + work, (2,) + work,
+        (4,) + padded, (4,) + padded, padded, work, work, work, (2,) + work, (2,) + work, (2,) + work, (2,) + work, (2,) + work,
         (SIZE, 4) + work, (4,) + padded, (4,) + padded, (LANES, LANES),
     ]
     part, sums = call(
         functools.partial(main_kernel, consts), [(peers, LANES), (ITERS, 4, nz, nx, ny)], scratch, 50_000_000, name="main"
-    )(ring, from_low, from_high)
-    total = lax.all_to_all(part.reshape(peers, 1, LANES), ("section", "sx", "sy"), 0, 0).reshape(peers, LANES)
-    mine, send = call(functools.partial(finish_kernel, consts), [sections.shape, previous.shape], name="finish")(total, sums, ring)
-    got = lax.ppermute(send, "section", swap)
+    )(sections, other, previous, diffusivity, reaction, own_low, own_high, other_low, other_high, side, corner_low, corner_high)
+    total = lax.all_to_all(part.reshape(peers, 1, LANES), axes, 0, 0).reshape(peers, LANES)
+    half, weight = call(functools.partial(send_kernel, consts), [previous.shape, (2 * ITERS, LANES)], name="send")(total, sums, other)
+    got = lax.ppermute(half, "section", swap)
+    mine = call(functools.partial(mine_kernel, consts), sections.shape, name="mine")(weight, sums, sections)
     return call(join_kernel, sections.shape, name="join")(mine, got)
 
 

time: 89.4 us -> 94.1 us (1.053)
  starting transfers between devices: 15.6 us -> 27.4 us
  waiting for transfers between devices: 14.7 us -> 10.8 us
  Pallas kernels: 25.8 us -> 23.6 us
  blocking collectives: 30.2 us -> 29 us
    ppermute x5 -> x8, starting transfers between devices: 11.9 us -> 24.4 us  [the longest x7 23.7 us: body(): lax.ppermute(a, axes, grid_pairs(columns, rows, x_step, y_out))]
    ppermute x5 -> x8, waiting for transfers between devices: 14.7 us -> 4.53 us  [the longest x1 2.93 us: body(): got = lax.ppermute(half, 'section', swap)]
    ppermute x1, waiting for transfers between devices: 0.01 us -> 6.28 us  [body(): other = lax.ppermute(sections, 'section', swap)]
    pallas_call x5 -> x6, Pallas kernels: 25.8 us -> 23.6 us  [run(): pl.pallas_call(kernel, out_shape=shapes if many else shapes[0], in_specs=...]
    all_to_all x1, blocking collectives: 30.2 us -> 29 us  [body(): lax.all_to_all(part.reshape(peers, 1, LANES), axes, 0, 0)]
    unnamed x12 -> x18, local copies, waits for them, and re-layouts: 2.75 us -> 2.67 us
  transfers between devices with their start and end apart: 6 -> 9, of which waited for: 4 -> 3; matrix products, arithmetic and copies ran while one was open for 0% -> 0% of each run, Pallas kernels for 2% -> 3%
where the time goes in v3:
time: 94.1 us; the launch traced here: 93.6 us
  blocking collectives  29 us (31%)
  starting transfers between devices  27.4 us (29%)
  Pallas kernels  23.6 us (25%)
  waiting for transfers between devices  10.8 us (11%)
  local copies, waits for them, and re-layouts  2.67 us (3%)
    all_to_all x1, blocking collectives, body(): lax.all_to_all(part.reshape(peers, 1, LANES), axes, 0, 0)  29 us
    ppermute x7, starting transfers between devices, body(): lax.ppermute(a, axes, grid_pairs(columns, rows, x_step, y_out))  23.7 us
    pallas_call x6, Pallas kernels, run(): pl.pallas_call(kernel, out_shape=shapes if many else shapes[0], in_specs=...  23.6 us
    ppermute x1, waiting for transfers between devices, body(): other = lax.ppermute(sections, 'section', swap)  6.28 us
    ppermute x1, starting transfers between devices, body(): other = lax.ppermute(sections, 'section', swap)  3 us
    ppermute x1, waiting for transfers between devices, body(): got = lax.ppermute(half, 'section', swap)  2.93 us
    unnamed x18, local copies, waits for them, and re-layouts  2.67 us
  transfers between devices with their start and end apart: 9, of which 3 were waited for; matrix products, arithmetic and copies ran while one was open for 0% of the time, Pallas kernels for 3%

profile of v3, /device:TPU:1, one launch (start us, length us, event | category | flops | bytes accessed | tf_op | source)
XLA Modules:
  0.0 93.6 jit_solution(3273343489179213209)
XLA Ops:
  0.0 2.2 %own.1 = (f32[8,16,128]{2,1,0:T(8,128)}, f32[16,48,128]{2,1,0:T(8,128)}, f32[16,48,128]{2,1,0:T(8,128)}) custom-call(f32[2,16,16,128]{3,2,1,0:T(8,128)} %own_ref.5, f32[16,16,128]{2,1,0:T(8,128)} %prev_ref.3, f32[16,16,128]{2,1,0:T(8,128)} %diff_ref.3, f32[16,16,128]{2,1,0:T(8,128)} %react_ref.3), custom_call_target="tpu_custom_call" | custom-call | flops 1000000 | bytes 1507328 | tf_op jit(solution)/shard_map/own/pallas_call | solution.py:534
  2.2 4.9 %collective-permute-start.1 = (f32[16,48,128]{2,1,0:T(8,128)}, f32[16,48,128]{2,1,0:T(8,128)S(1)}, u32[]{:S(2)}, u32[]{:S(2)}) collective-permute-start(f32[16,48,128]{2,1,0:T(8,128)} %get-tuple-element.18), channel_id=1, source_target_pairs={{0,8},{1,9},{2,10},{3,11},{4,12},{5,13},{6,14},{7,15},{8,16},{9,17... | collective-permute-start | bytes 1179656 | tf_op jit(solution)/shard_map/ppermute | solution.py:565
  7.1 1.9 %collective-permute-start.2 = (f32[16,48,128]{2,1,0:T(8,128)}, f32[16,48,128]{2,1,0:T(8,128)S(1)}, u32[]{:S(2)}, u32[]{:S(2)}) collective-permute-start(f32[16,48,128]{2,1,0:T(8,128)} %get-tuple-element.19), channel_id=1, source_target_pairs={{8,0},{9,1},{10,2},{11,3},{12,4},{13,5},{14,6},{15,7},{16,8},{17,9... | collective-permute-start | bytes 1179656 | tf_op jit(solution)/shard_map/ppermute | solution.py:565
  9.0 3.0 %collective-permute-start = (f32[2,16,16,128]{3,2,1,0:T(8,128)}, f32[2,16,16,128]{3,2,1,0:T(8,128)S(1)}, u32[]{:S(2)}, u32[]{:S(2)}) collective-permute-start(f32[2,16,16,128]{3,2,1,0:T(8,128)} %own_ref.5), channel_id=1, source_target_pairs={{0,128},{128,0},{1,129},{129,1},{2,130},{130,2},{3,131},{131,3},{4... | collective-permute-start | bytes 786440 | tf_op jit(solution)/shard_map/ppermute | solution.py:566
  12.0 6.3 %collective-permute-done.other_ref = f32[2,16,16,128]{3,2,1,0:T(8,128)S(1)} collective-permute-done((f32[2,16,16,128]{3,2,1,0:T(8,128)}, f32[2,16,16,128]{3,2,1,0:T(8,128)S(1)}, u32[]{:S(2)}, u32[]{:S(2)}) %collective-permute-start) | collective-permute-done | bytes 262176 | tf_op jit(solution)/shard_map/ppermute | solution.py:566
  18.4 0.7 copy-done
  19.0 1.8 %other.1 = (f32[8,16,128]{2,1,0:T(8,128)}, f32[16,24,128]{2,1,0:T(8,128)}, f32[16,24,128]{2,1,0:T(8,128)}) custom-call(f32[2,16,16,128]{3,2,1,0:T(8,128)} %copy-done, f32[8,16,128]{2,1,0:T(8,128)} %get-tuple-element.23.partial_ref), custom_call_target="tpu_custom_call" | custom-call | flops 1000000 | bytes 786432 | tf_op jit(solution)/shard_map/other/pallas_call | solution.py:534
  20.8 4.7 %collective-permute-start.3 = (f32[16,24,128]{2,1,0:T(8,128)}, f32[16,24,128]{2,1,0:T(8,128)S(1)}, u32[]{:S(2)}, u32[]{:S(2)}) collective-permute-start(f32[16,24,128]{2,1,0:T(8,128)} %get-tuple-element.24), channel_id=1, source_target_pairs={{0,8},{1,9},{2,10},{3,11},{4,12},{5,13},{6,14},{7,15},{8,16},{9,17... | collective-permute-start | bytes 589832 | tf_op jit(solution)/shard_map/ppermute | solution.py:565
  25.5 1.9 %collective-permute-start.4 = (f32[16,24,128]{2,1,0:T(8,128)}, f32[16,24,128]{2,1,0:T(8,128)S(1)}, u32[]{:S(2)}, u32[]{:S(2)}) collective-permute-start(f32[16,24,128]{2,1,0:T(8,128)} %get-tuple-element.25), channel_id=1, source_target_pairs={{8,0},{9,1},{10,2},{11,3},{12,4},{13,5},{14,6},{15,7},{16,8},{17,9... | collective-permute-start | bytes 589832 | tf_op jit(solution)/shard_map/ppermute | solution.py:565
  27.4 1.3 %collective-permute-start.7 = (f32[8,16,128]{2,1,0:T(8,128)}, f32[8,16,128]{2,1,0:T(8,128)S(1)}, u32[]{:S(2)}, u32[]{:S(2)}) collective-permute-start(f32[8,16,128]{2,1,0:T(8,128)} %get-tuple-element.26), channel_id=1, source_target_pairs={{8,1},{9,2},{10,3},{11,4},{12,5},{13,6},{14,7},{16,9},{17,10},{18,... | collective-permute-start | bytes 196616 | tf_op jit(solution)/shard_map/ppermute | solution.py:565
  28.7 6.1 %collective-permute-start.6 = (f32[8,16,128]{2,1,0:T(8,128)}, f32[8,16,128]{2,1,0:T(8,128)S(1)}, u32[]{:S(2)}, u32[]{:S(2)}) collective-permute-start(f32[8,16,128]{2,1,0:T(8,128)} %get-tuple-element.26), channel_id=1, source_target_pairs={{0,9},{1,10},{2,11},{3,12},{4,13},{5,14},{6,15},{8,17},{9,18},{10,... | collective-permute-start | bytes 196616 | tf_op jit(solution)/shard_map/ppermute | solution.py:565
  34.8 2.8 %collective-permute-start.5 = (f32[8,16,128]{2,1,0:T(8,128)}, f32[8,16,128]{2,1,0:T(8,128)S(1)}, u32[]{:S(2)}, u32[]{:S(2)}) collective-permute-start(f32[8,16,128]{2,1,0:T(8,128)} %get-tuple-element.26), channel_id=1, source_target_pairs={{0,1},{1,2},{2,3},{3,4},{4,5},{5,6},{6,7},{8,9},{9,10},{10,11},{11... | collective-permute-start | bytes 196616 | tf_op jit(solution)/shard_map/ppermute | solution.py:565
  37.7 1.6 %collective-permute-done.5.border_ref = f32[8,16,128]{2,1,0:T(8,128)S(1)} collective-permute-done((f32[8,16,128]{2,1,0:T(8,128)}, f32[8,16,128]{2,1,0:T(8,128)S(1)}, u32[]{:S(2)}, u32[]{:S(2)}) %collective-permute-start.5) | collective-permute-done | bytes 65568 | tf_op jit(solution)/shard_map/ppermute | solution.py:565
  39.3 0.6 copy-done.8
  39.9 0.1 copy-done.3
  40.0 0.7 copy-done.4
  40.7 12.4 %main.1 = (f32[256,128]{1,0:T(8,128)}, f32[4,4,16,16,128]{4,3,2,1,0:T(8,128)}) custom-call(f32[2,16,16,128]{3,2,1,0:T(8,128)} %own_ref.5, f32[2,16,16,128]{3,2,1,0:T(8,128)} %copy-done, f32[16,16,128]{2,1,0:T(8,128)} %prev_ref.3, f32[16,16,128]{2,1,0:T(8,128)} %diff_ref.3, f32[16,16,128]{2,1,0:T(8,128)} %react_ref.3, f32[16,48,128]{2,1,0:T(8,128)} %copy-done.1, ...), custom_call_target="tpu_custom_call" | custom-call | flops 50000000 | bytes 4521984 | tf_op jit(solution)/shard_map/main/pallas_call | solution.py:534
  53.1 29.0 %all_to_all.5 = f32[256,1,128]{2,1,0:T(1,128)} all-to-all(f32[256,1,128]{2,1,0:T(1,128)} %bitcast.5), channel_id=1, replica_groups=mesh['section'=2,'sx'=16,'sy'=8] {'section','sx','sy'}, dimensions={0} | all-to-all | bytes 262144 | tf_op jit(solution)/shard_map/all_to_all | solution.py:585
  82.1 3.0 %send.1 = (f32[16,16,128]{2,1,0:T(8,128)}, f32[8,128]{1,0:T(8,128)}) custom-call(f32[256,128]{1,0:T(8,128)} %bitcast.4, f32[4,4,16,16,128]{4,3,2,1,0:T(8,128)} %get-tuple-element.28.sums_ref, f32[2,16,16,128]{3,2,1,0:T(8,128)} %copy-done), custom_call_target="tpu_custom_call" | custom-call | flops 1000000 | bytes 2625536 | tf_op jit(solution)/shard_map/send/pallas_call | solution.py:534
  85.0 0.7 collective-permute-start.8
  85.7 2.5 %mine.1.mine_ref = f32[2,16,16,128]{3,2,1,0:T(8,128)} custom-call(f32[8,128]{1,0:T(8,128)} %get-tuple-element.29.weight_ref, f32[4,4,16,16,128]{4,3,2,1,0:T(8,128)} %get-tuple-element.28.sums_ref, f32[2,16,16,128]{3,2,1,0:T(8,128)} %own_ref.5), custom_call_target="tpu_custom_call" | custom-call | flops 1000000 | bytes 2625536 | tf_op jit(solution)/shard_map/mine/pallas_call | solution.py:534
  88.2 2.9 %collective-permute-done.8.other_ref = f32[16,16,128]{2,1,0:T(8,128)S(1)} collective-permute-done((f32[16,16,128]{2,1,0:T(8,128)}, f32[16,16,128]{2,1,0:T(8,128)S(1)}, u32[]{:S(2)}, u32[]{:S(2)}) %collective-permute-start.8) | collective-permute-done | bytes 131104 | tf_op jit(solution)/shard_map/ppermute | solution.py:587
  91.2 0.6 copy-done.5
  91.8 1.8 %join.1 = f32[2,16,16,128]{3,2,1,0:T(8,128)} custom-call(f32[2,16,16,128]{3,2,1,0:T(8,128)} %mine.1.mine_ref, f32[16,16,128]{2,1,0:T(8,128)} %copy-done.5), custom_call_target="tpu_custom_call" | custom-call | flops 1000000 | bytes 655360 | tf_op jit(solution)/shard_map/join/pallas_call | solution.py:534
  (19 shorter events, 0.0 us)
Async XLA Ops:
  2.2 16.1 %collective-permute-start.1 = (f32[16,48,128]{2,1,0:T(8,128)}, f32[16,48,128]{2,1,0:T(8,128)S(1)}, u32[]{:S(2)}, u32[]{:S(2)}) collective-permute-start(f32[16,48,128]{2,1,0:T(8,128)} %get-tuple-element.18), channel_id=1, source_target_pairs={{0,8},{1,9},{2,10},{3,11},{4,12},{5,13},{6,14},{7,15},{8,16},{9,17... | collective-permute-start | bytes 1179656 | tf_op jit(solution)/shard_map/ppermute | solution.py:565
  7.1 11.2 %collective-permute-start.2 = (f32[16,48,128]{2,1,0:T(8,128)}, f32[16,48,128]{2,1,0:T(8,128)S(1)}, u32[]{:S(2)}, u32[]{:S(2)}) collective-permute-start(f32[16,48,128]{2,1,0:T(8,128)} %get-tuple-element.19), channel_id=1, source_target_pairs={{8,0},{9,1},{10,2},{11,3},{12,4},{13,5},{14,6},{15,7},{16,8},{17,9... | collective-permute-start | bytes 1179656 | tf_op jit(solution)/shard_map/ppermute | solution.py:565
  9.0 9.3 %collective-permute-start = (f32[2,16,16,128]{3,2,1,0:T(8,128)}, f32[2,16,16,128]{3,2,1,0:T(8,128)S(1)}, u32[]{:S(2)}, u32[]{:S(2)}) collective-permute-start(f32[2,16,16,128]{3,2,1,0:T(8,128)} %own_ref.5), channel_id=1, source_target_pairs={{0,128},{128,0},{1,129},{129,1},{2,130},{130,2},{3,131},{131,3},{4... | collective-permute-start | bytes 786440 | tf_op jit(solution)/shard_map/ppermute | solution.py:566
  18.3 0.7 copy-start
  18.3 21.0 %copy-start.1 = (f32[16,48,128]{2,1,0:T(8,128)}, f32[16,48,128]{2,1,0:T(8,128)S(1)}, u32[]{:S(2)}) copy-start(f32[16,48,128]{2,1,0:T(8,128)S(1)} %collective-permute-done.1.own_low_ref) | copy-start | bytes 1179652
  18.3 21.0 %copy-start.2 = (f32[16,48,128]{2,1,0:T(8,128)}, f32[16,48,128]{2,1,0:T(8,128)S(1)}, u32[]{:S(2)}) copy-start(f32[16,48,128]{2,1,0:T(8,128)S(1)} %collective-permute-done.2.own_high_ref) | copy-start | bytes 1179652
  20.8 18.5 %collective-permute-start.3 = (f32[16,24,128]{2,1,0:T(8,128)}, f32[16,24,128]{2,1,0:T(8,128)S(1)}, u32[]{:S(2)}, u32[]{:S(2)}) collective-permute-start(f32[16,24,128]{2,1,0:T(8,128)} %get-tuple-element.24), channel_id=1, source_target_pairs={{0,8},{1,9},{2,10},{3,11},{4,12},{5,13},{6,14},{7,15},{8,16},{9,17... | collective-permute-start | bytes 589832 | tf_op jit(solution)/shard_map/ppermute | solution.py:565
  25.5 13.8 %collective-permute-start.4 = (f32[16,24,128]{2,1,0:T(8,128)}, f32[16,24,128]{2,1,0:T(8,128)S(1)}, u32[]{:S(2)}, u32[]{:S(2)}) collective-permute-start(f32[16,24,128]{2,1,0:T(8,128)} %get-tuple-element.25), channel_id=1, source_target_pairs={{8,0},{9,1},{10,2},{11,3},{12,4},{13,5},{14,6},{15,7},{16,8},{17,9... | collective-permute-start | bytes 589832 | tf_op jit(solution)/shard_map/ppermute | solution.py:565
  27.4 10.3 %collective-permute-start.7 = (f32[8,16,128]{2,1,0:T(8,128)}, f32[8,16,128]{2,1,0:T(8,128)S(1)}, u32[]{:S(2)}, u32[]{:S(2)}) collective-permute-start(f32[8,16,128]{2,1,0:T(8,128)} %get-tuple-element.26), channel_id=1, source_target_pairs={{8,1},{9,2},{10,3},{11,4},{12,5},{13,6},{14,7},{16,9},{17,10},{18,... | collective-permute-start | bytes 196616 | tf_op jit(solution)/shard_map/ppermute | solution.py:565
  28.7 9.0 %collective-permute-start.6 = (f32[8,16,128]{2,1,0:T(8,128)}, f32[8,16,128]{2,1,0:T(8,128)S(1)}, u32[]{:S(2)}, u32[]{:S(2)}) collective-permute-start(f32[8,16,128]{2,1,0:T(8,128)} %get-tuple-element.26), channel_id=1, source_target_pairs={{0,9},{1,10},{2,11},{3,12},{4,13},{5,14},{6,15},{8,17},{9,18},{10,... | collective-permute-start | bytes 196616 | tf_op jit(solution)/shard_map/ppermute | solution.py:565
  34.8 4.5 %collective-permute-start.5 = (f32[8,16,128]{2,1,0:T(8,128)}, f32[8,16,128]{2,1,0:T(8,128)S(1)}, u32[]{:S(2)}, u32[]{:S(2)}) collective-permute-start(f32[8,16,128]{2,1,0:T(8,128)} %get-tuple-element.26), channel_id=1, source_target_pairs={{0,1},{1,2},{2,3},{3,4},{4,5},{5,6},{6,7},{8,9},{9,10},{10,11},{11... | collective-permute-start | bytes 196616 | tf_op jit(solution)/shard_map/ppermute | solution.py:565
  37.7 1.7 %copy-start.6 = (f32[8,16,128]{2,1,0:T(8,128)}, f32[8,16,128]{2,1,0:T(8,128)S(1)}, u32[]{:S(2)}) copy-start(f32[8,16,128]{2,1,0:T(8,128)S(1)} %collective-permute-done.7.corner_high_ref) | copy-start | bytes 196612
  37.7 1.6 %copy-start.7 = (f32[8,16,128]{2,1,0:T(8,128)}, f32[8,16,128]{2,1,0:T(8,128)S(1)}, u32[]{:S(2)}) copy-start(f32[8,16,128]{2,1,0:T(8,128)S(1)} %collective-permute-done.6.corner_low_ref) | copy-start | bytes 196612
  39.3 0.6 copy-start.8
  39.3 0.7 copy-start.3
  40.0 0.7 copy-start.4
  85.0 6.1 %collective-permute-start.8 = (f32[16,16,128]{2,1,0:T(8,128)}, f32[16,16,128]{2,1,0:T(8,128)S(1)}, u32[]{:S(2)}, u32[]{:S(2)}) collective-permute-start(f32[16,16,128]{2,1,0:T(8,128)} %get-tuple-element.30), channel_id=1, source_target_pairs={{0,128},{128,0},{1,129},{129,1},{2,130},{130,2},{3,131},{131,3},{4... | collective-permute-start | bytes 393224 | tf_op jit(solution)/shard_map/ppermute | solution.py:587
  91.2 0.6 copy-start.5

commit v4 on v3

--- a/solution.py
+++ b/solution.py
@@ -15,7 +15,6 @@
 PAIRS = [(i, j) for i in range(SIZE) for j in range(i, SIZE)]
 PREPARE_UNROLL = 2
 STEP_UNROLL = 8
-VMEM_LIMIT = 58 * 1024 * 1024
 
 
 step_size = 1.0
@@ -178,67 +177,69 @@
     return pltpu.roll(cells, amount % LANES, cells.ndim - 1)
 
 
-def half_mask(rows, section):
-    return (lane_ids(rows) < LANES // 2) == (section == 0)
-
-
-MINE = (0, 1, 4, 5, 6)
+def left_half():
+    return lax.rem(lax.axis_index("section") + lax.axis_index("sy"), 2) == 1
+
+
+def half_mask(rows):
+    return (lane_ids(rows) < LANES // 2) == left_half()
+
+
+ORDER = (0, 1, 4, 5, 6, 2, 3)
+TALL = 16
+PARTS = 4
 
 
 def border_start():
-    first = lax.axis_index("section") == 0
-    high, low = LANES - EDGE, 0
-    return jnp.where(first, high, low)
-
-
-def pack_border(tile, cell, field, part, lanes, start):
-    at = part * 64 + field * EDGE
-    moved = pltpu.roll(cell, lax.rem(at + LANES - start, LANES), 1)
-    return jnp.where((lanes >= at) & (lanes < at + EDGE), moved, tile)
-
-
-def pack_rows(low_ref, high_ref, cells, z, nx):
-    count = len(cells)
-    for f, cell in enumerate(cells):
-        low_ref[z, 8 * f : 8 * f + 8] = cell[0:8]
-        low_ref[z, 8 * count + f : 8 * count + f + 1] = cell[8:9]
-        high_ref[z, 8 * f : 8 * f + 8] = cell[nx - 8 : nx]
-        high_ref[z, 8 * count + f : 8 * count + f + 1] = cell[nx - 9 : nx - 8]
-    rest = low_ref.shape[1] - 9 * count
-    for ref in (low_ref, high_ref):
-        ref[z, 9 * count :] = jnp.zeros((rest, LANES), jnp.float32)
-
-
-def own_kernel(own_ref, prev_ref, diff_ref, react_ref, border_ref, low_ref, high_ref):
-    nz, nx = prev_ref.shape[0], prev_ref.shape[1]
+    return jnp.where(left_half(), LANES - EDGE, 0)
+
+
+def leaving_start():
+    return jnp.where(left_half(), 0, LANES - EDGE)
+
+
+def on_even_row():
+    return lax.rem(lax.axis_index("sx"), 2) == 0
+
+
+def pack(border_ref, near_ref, far_ref, load, fields, first_slot, partial):
+    nz = 2 * border_ref.shape[0]
+    nx = border_ref.shape[1]
     lanes = lane_ids(nx)
-    start = border_start()
-    half = nz // 2
-    for plane in range(half):
-        tile = jnp.zeros((nx, LANES), jnp.float32)
+    start = leaving_start()
+    even = on_even_row()
+
+    def plane_pair(plane):
+        tile = partial(plane)
         for part in range(2):
-            z = part * half + plane
-            cells = [own_ref[0, z], own_ref[1, z], prev_ref[z], diff_ref[z], react_ref[z]]
-            for f, cell in zip(MINE, cells):
-                tile = pack_border(tile, cell, f, part, lanes, start)
-            pack_rows(low_ref, high_ref, cells, z, nx)
+            z = part * (nz // 2) + plane
+            for slot, f in enumerate(fields, first_slot):
+                cell = load(f, z)
+                at = part * 64 + f * EDGE
+                moved = pltpu.roll(cell, lax.rem(at + LANES - start, LANES), 1)
+                tile = jnp.where((lanes >= at) & (lanes < at + EDGE), moved, tile)
+                entry, row = divmod(8 * slot, TALL)
+                last, ninth = divmod(56 + slot, TALL)
+                near_ref[z * PARTS + entry, row : row + 8] = jnp.where(even, cell[nx - 8 : nx], cell[0:8])
+                far_ref[z * PARTS + entry, row : row + 8] = jnp.where(even, cell[0:8], cell[nx - 8 : nx])
+                near_ref[z * PARTS + last, ninth : ninth + 1] = jnp.where(even, cell[nx - 9 : nx - 8], cell[8:9])
+                far_ref[z * PARTS + last, ninth : ninth + 1] = jnp.where(even, cell[8:9], cell[nx - 9 : nx - 8])
         border_ref[plane] = tile
 
-
-def other_kernel(other_ref, partial_ref, border_ref, low_ref, high_ref):
-    nz, nx = other_ref.shape[1], other_ref.shape[2]
-    lanes = lane_ids(nx)
-    start = border_start()
-    half = nz // 2
-    for plane in range(half):
-        tile = partial_ref[plane]
-        for part in range(2):
-            z = part * half + plane
-            cells = [other_ref[0, z], other_ref[1, z]]
-            for f, cell in enumerate(cells):
-                tile = pack_border(tile, cell, 2 + f, part, lanes, start)
-            pack_rows(low_ref, high_ref, cells, z, nx)
-        border_ref[plane] = tile
+    each_plane(nz // 2, 4, plane_pair)
+
+
+def own_kernel(own_ref, prev_ref, diff_ref, react_ref, border_ref, near_ref, far_ref):
+    nx = prev_ref.shape[1]
+    refs = {4: prev_ref, 5: diff_ref, 6: react_ref}
+    load = lambda f, z: own_ref[f, z] if f < 2 else refs[f][z]
+    pack(border_ref, near_ref, far_ref, load, ORDER[:5], 0, lambda plane: jnp.zeros((nx, LANES), jnp.float32))
+
+
+def other_kernel(other_ref, own_border_ref, own_near_ref, own_far_ref, border_ref, near_ref, far_ref):
+    near_ref[...] = own_near_ref[...]
+    far_ref[...] = own_far_ref[...]
+    pack(border_ref, near_ref, far_ref, lambda f, z: other_ref[f - 2, z], ORDER[5:], 5, lambda plane: own_border_ref[plane])
 
 
 ROWS = 48
@@ -258,8 +259,7 @@
     lax.fori_loop(0, count // unroll, group, 0)
 
 
-def main_kernel(consts, own_ref, other_ref, prev_ref, diff_ref, react_ref, own_low_ref, own_high_ref, other_low_ref, other_high_ref,
-                border_ref, corner_low_ref, corner_high_ref, part_ref, sums_ref,
+def main_kernel(consts, own_ref, other_ref, prev_ref, diff_ref, react_ref, border_ref, near_ref, far_ref, part_ref, sums_ref,
                 val, kap, frozen, prv, rea, dif, fx, fy, fz, alpha, beta, vec, ya, yb, table):
     eigen_basis, basis_inverse, shift_rows, pairs = consts
     nz, nx = prev_ref.shape[0], prev_ref.shape[1]
@@ -267,6 +267,7 @@
     zero_plane = jnp.zeros((ROWS, LANES), jnp.float32)
     zero_rows = jnp.zeros((FIRST, LANES), jnp.float32)
     start = border_start()
+    even = on_even_row()
     lanes = lane_ids(ROWS)
     edge = (lanes >= start) & (lanes < start + EDGE)
     tile = lambda t: jnp.broadcast_to(t, (8, LANES))
@@ -277,28 +278,26 @@
             for ref in (val, kap, ya, yb):
                 ref[f, at] = zero_plane
 
+    def both(entry, row, count):
+        near, far = near_ref[entry, row : row + count], far_ref[entry, row : row + count]
+        return jnp.where(even, far, near), jnp.where(even, near, far)
+
     def assemble(plane):
-        sides = jnp.concatenate(
-            [
-                tile(corner_low_ref[plane, nx - 9 : nx - 8]), corner_low_ref[plane, nx - 8 : nx], border_ref[plane],
-                corner_high_ref[plane, 0:8], tile(corner_high_ref[plane, 8:9]),
-            ],
-            0,
-        )
+        at = nz * PARTS + plane
+        low = jnp.where(even, far_ref[at], near_ref[at])
+        high = jnp.where(even, near_ref[at], far_ref[at])
+        sides = jnp.concatenate([tile(low[nx - 9 : nx - 8]), low[nx - 8 : nx], border_ref[plane], high[0:8], tile(high[8:9])], 0)
         for part in range(2):
             z = part * (nz // 2) + plane
 
             def column(f):
-                if f in (2, 3):
-                    low, high, slot, count, mid = other_low_ref, other_high_ref, f - 2, 2, other_ref[f - 2, z]
-                else:
-                    slot, count = MINE.index(f), len(MINE)
-                    low, high = own_low_ref, own_high_ref
-                    mid = (own_ref[0, z], own_ref[1, z], prev_ref[z], diff_ref[z], react_ref[z])[slot]
-                ninth = 8 * count + slot
-                cells = jnp.concatenate(
-                    [tile(low[z, ninth : ninth + 1]), low[z, 8 * slot : 8 * slot + 8], mid, high[z, 8 * slot : 8 * slot + 8], tile(high[z, ninth : ninth + 1])], 0
-                )
+                slot = ORDER.index(f)
+                mid = (own_ref[0, z], own_ref[1, z], prev_ref[z], diff_ref[z], react_ref[z], other_ref[0, z], other_ref[1, z])[slot]
+                entry, row = divmod(8 * slot, TALL)
+                low, high = both(z * PARTS + entry, row, 8)
+                entry, row = divmod(56 + slot, TALL)
+                low_end, high_end = both(z * PARTS + entry, row, 1)
+                cells = jnp.concatenate([tile(low_end), low, mid, high, tile(high_end)], 0)
                 at = part * 64 + f * EDGE
                 return jnp.where(edge, pltpu.roll(sides, lax.rem(start + LANES - at, LANES), 1), cells)
 
@@ -410,7 +409,7 @@
         each_plane(nz, STEP_UNROLL, even)
 
     table[...] = jnp.zeros((LANES, LANES), jnp.float32)
-    mine = half_mask(8, section)
+    mine = half_mask(8)
     for b in range(2):
 
         def dots(z, carry):
@@ -479,7 +478,7 @@
         [jnp.where(section == 0, jnp.float32(eigen_basis[2 + r][m]), jnp.float32(eigen_basis[r][m])) for m in range(4)]
         for r in range(2)
     ]
-    mine = half_mask(nx, section)
+    mine = half_mask(nx)
 
     def combine(z):
         outs = [other_ref[r, z] for r in range(2)]
@@ -518,14 +517,14 @@
 
 def join_kernel(mine_ref, other_ref, out_ref):
     nz, nx = mine_ref.shape[1], mine_ref.shape[2]
-    mine = half_mask(nx, lax.axis_index("section"))
+    mine = half_mask(nx)
     for z in range(nz):
         other = other_ref[z]
         out_ref[0, z] = jnp.where(mine, mine_ref[0, z], other)
         out_ref[1, z] = jnp.where(mine, mine_ref[1, z], turn(other, LANES // 2))
 
 
-def call(kernel, outs, scratch=(), flops=1_000_000, name=None):
+def call(kernel, outs, scratch=(), flops=1_000_000, name=None, limit=12):
     many = isinstance(outs, list)
     shapes = [jax.ShapeDtypeStruct(o, jnp.float32) for o in (outs if many else [outs])]
 
@@ -537,7 +536,7 @@
             in_specs=[pl.BlockSpec(memory_space=pltpu.VMEM)] * len(args),
             out_specs=[pl.BlockSpec(memory_space=pltpu.VMEM)] * len(shapes) if many else pl.BlockSpec(memory_space=pltpu.VMEM),
             scratch_shapes=[pltpu.VMEM(s, jnp.float32) for s in scratch],
-            compiler_params=pltpu.CompilerParams(vmem_limit_bytes=VMEM_LIMIT),
+            compiler_params=pltpu.CompilerParams(vmem_limit_bytes=limit * 1024 * 1024),
             cost_estimate=pl.CostEstimate(flops=flops, bytes_accessed=moved, transcendentals=0),
             name=name,
         )(*args)
@@ -545,15 +544,8 @@
     return run
 
 
-def grid_pairs(columns, rows, x_step, y_out):
-    pairs = []
-    for s in range(2):
-        y_step = (1 - 2 * s) if y_out else 0
-        for x in range(rows):
-            for y in range(columns):
-                if 0 <= x + x_step < rows and 0 <= y + y_step < columns:
-                    pairs.append(((s * rows + x) * columns + y, (s * rows + x + x_step) * columns + y + y_step))
-    return pairs
+def swaps(count, start):
+    return [pair for i in range(start, count - 1, 2) for pair in ((i, i + 1), (i + 1, i))]
 
 
 def body(previous, sections, diffusivity, reaction):
@@ -561,18 +553,17 @@
     nz, nx, ny = previous.shape
     columns, rows = lax.axis_size("sy"), lax.axis_size("sx")
     axes = ("section", "sx", "sy")
-    swap = [(0, 1), (1, 0)]
-    send = lambda a, x_step, y_out: lax.ppermute(a, axes, grid_pairs(columns, rows, x_step, y_out))
-    other = lax.ppermute(sections, "section", swap)
-    partial, low, high = call(own_kernel, [(nz // 2, nx, ny), (nz, 48, ny), (nz, 48, ny)], name="own")(
-        sections, previous, diffusivity, reaction
-    )
-    own_low, own_high = send(high, 1, False), send(low, -1, False)
-    other, own_low, own_high = lax.optimization_barrier((other, own_low, own_high))
-    border, low, high = call(other_kernel, [(nz // 2, nx, ny), (nz, 24, ny), (nz, 24, ny)], name="other")(other, partial)
-    other_low, other_high = send(high, 1, False), send(low, -1, False)
-    side = send(border, 0, True)
-    corner_low, corner_high = send(border, 1, True), send(border, -1, True)
+    partner = [(0, 1), (1, 0)]
+    other = lax.ppermute(sections, "section", partner)
+    shapes = [(nz // 2, nx, ny), (nz * PARTS + nz // 2, TALL, ny), (nz * PARTS + nz // 2, TALL, ny)]
+    packed = call(own_kernel, shapes, name="own")(sections, previous, diffusivity, reaction)
+    border, near, far = call(other_kernel, shapes, name="other")(other, *packed)
+    edges = [(s * columns + a, s * columns + b) for s in range(2) for a, b in swaps(columns, s)]
+    border = lax.ppermute(border, ("section", "sy"), edges)
+    near = lax.dynamic_update_slice(near, border, (nz * PARTS, 0, 0))
+    far = lax.dynamic_update_slice(far, border, (nz * PARTS, 0, 0))
+    far = lax.ppermute(far, "sx", swaps(rows, 1))
+    near = lax.ppermute(near, "sx", swaps(rows, 0))
     peers = 2 * columns * rows
     padded, work = (nz + 2, ROWS, ny), (nz, LAST - FIRST, ny)
     scratch = [
@@ -580,11 +571,11 @@
         (SIZE, 4) + work, (4,) + padded, (4,) + padded, (LANES, LANES),
     ]
     part, sums = call(
-        functools.partial(main_kernel, consts), [(peers, LANES), (ITERS, 4, nz, nx, ny)], scratch, 50_000_000, name="main"
-    )(sections, other, previous, diffusivity, reaction, own_low, own_high, other_low, other_high, side, corner_low, corner_high)
+        functools.partial(main_kernel, consts), [(peers, LANES), (ITERS, 4, nz, nx, ny)], scratch, 50_000_000, "main", 26
+    )(sections, other, previous, diffusivity, reaction, border, near, far)
     total = lax.all_to_all(part.reshape(peers, 1, LANES), axes, 0, 0).reshape(peers, LANES)
     half, weight = call(functools.partial(send_kernel, consts), [previous.shape, (2 * ITERS, LANES)], name="send")(total, sums, other)
-    got = lax.ppermute(half, "section", swap)
+    got = lax.ppermute(half, "section", partner)
     mine = call(functools.partial(mine_kernel, consts), sections.shape, name="mine")(weight, sums, sections)
     return call(join_kernel, sections.shape, name="join")(mine, got)
 

time: 94.1 us -> 76.2 us (0.81)
  starting transfers between devices: 27.4 us -> 14.6 us
  Pallas kernels: 23.6 us -> 12 us
  waiting for transfers between devices: 10.8 us -> 15.6 us
  local copies, waits for them, and re-layouts: 2.67 us -> 3.72 us
  blocking collectives: 29 us -> 30 us
    ppermute x9 -> x5, starting transfers between devices: 27.4 us -> 14.6 us  [the longest x1 6.37 us: body(): far = lax.ppermute(far, 'sx', swaps(rows, 1))]
    pallas_call x6, Pallas kernels: 23.6 us -> 12 us  [run(): pl.pallas_call(kernel, out_shape=shapes if many else shapes[0], in_specs=...]
    ppermute x9 -> x5, waiting for transfers between devices: 10.8 us -> 15.6 us  [the longest x1 7.45 us: body(): far = lax.ppermute(far, 'sx', swaps(rows, 1))]
    unnamed x18 -> x16, local copies, waits for them, and re-layouts: 2.67 us -> 3.71 us
    all_to_all x1, blocking collectives: 29 us -> 30 us  [body(): lax.all_to_all(part.reshape(peers, 1, LANES), axes, 0, 0)]
  transfers between devices with their start and end apart: 9 -> 5, of which waited for: 3 -> 4; matrix products, arithmetic and copies ran while one was open for 0% -> 0% of each run, Pallas kernels for 3% -> 1%
where the time goes in v4:
time: 76.2 us; the launch traced here: 76 us
  blocking collectives  30 us (39%)
  waiting for transfers between devices  15.6 us (20%)
  starting transfers between devices  14.6 us (19%)
  Pallas kernels  12 us (16%)
  local copies, waits for them, and re-layouts  3.72 us (5%)
    all_to_all x1, blocking collectives, body(): lax.all_to_all(part.reshape(peers, 1, LANES), axes, 0, 0)  30 us
    pallas_call x6, Pallas kernels, run(): pl.pallas_call(kernel, out_shape=shapes if many else shapes[0], in_specs=...  12 us
    ppermute x1, waiting for transfers between devices, body(): far = lax.ppermute(far, 'sx', swaps(rows, 1))  7.45 us
    ppermute x1, starting transfers between devices, body(): far = lax.ppermute(far, 'sx', swaps(rows, 1))  6.37 us
    ppermute x1, waiting for transfers between devices, body(): got = lax.ppermute(half, 'section', partner)  5.27 us
    ppermute x1, starting transfers between devices, body(): border = lax.ppermute(border, ('section', 'sy'), edges)  3.8 us
    ppermute x1, starting transfers between devices, body(): other = lax.ppermute(sections, 'section', partner)  3.74 us
    unnamed x16, local copies, waits for them, and re-layouts  3.71 us
  transfers between devices with their start and end apart: 5, of which 4 were waited for; matrix products, arithmetic and copies ran while one was open for 0% of the time, Pallas kernels for 1%

profile of v4, /device:TPU:1, one launch (start us, length us, event | category | flops | bytes accessed | tf_op | source)
XLA Modules:
  0.0 76.0 jit_solution(1464303481081449879)
XLA Ops:
  0.0 3.7 %collective-permute-start = (f32[2,16,16,128]{3,2,1,0:T(8,128)}, f32[2,16,16,128]{3,2,1,0:T(8,128)S(1)}, u32[]{:S(2)}, u32[]{:S(2)}) collective-permute-start(f32[2,16,16,128]{3,2,1,0:T(8,128)} %own_ref.5), channel_id=1, source_target_pairs={{0,128},{128,0},{1,129},{129,1},{2,130},{130,2},{3,131},{131,3},{4... | collective-permute-start | bytes 786440 | tf_op jit(solution)/shard_map/ppermute | solution.py:557
  3.7 1.0 %copy-done = f32[2,16,16,128]{3,2,1,0:T(8,128)S(1)} copy-done((f32[2,16,16,128]{3,2,1,0:T(8,128)S(1)}, f32[2,16,16,128]{3,2,1,0:T(8,128)}, u32[]{:S(2)}) %copy-start) | copy-done | bytes 262168
  4.7 0.9 %copy-done.2 = f32[16,16,128]{2,1,0:T(8,128)S(1)} copy-done((f32[16,16,128]{2,1,0:T(8,128)S(1)}, f32[16,16,128]{2,1,0:T(8,128)}, u32[]{:S(2)}) %copy-start.2) | copy-done | bytes 131096
  5.6 0.9 %copy-done.4 = f32[16,16,128]{2,1,0:T(8,128)S(1)} copy-done((f32[16,16,128]{2,1,0:T(8,128)S(1)}, f32[16,16,128]{2,1,0:T(8,128)}, u32[]{:S(2)}) %copy-start.4) | copy-done | bytes 131096
  6.5 0.9 %copy-done.6 = f32[16,16,128]{2,1,0:T(8,128)S(1)} copy-done((f32[16,16,128]{2,1,0:T(8,128)S(1)}, f32[16,16,128]{2,1,0:T(8,128)}, u32[]{:S(2)}) %copy-start.6) | copy-done | bytes 131096
  7.5 0.3 own.1
  7.8 1.2 %collective-permute-done.other_ref = f32[2,16,16,128]{3,2,1,0:T(8,128)S(1)} collective-permute-done((f32[2,16,16,128]{3,2,1,0:T(8,128)}, f32[2,16,16,128]{3,2,1,0:T(8,128)S(1)}, u32[]{:S(2)}, u32[]{:S(2)}) %collective-permute-start) | collective-permute-done | bytes 262176 | tf_op jit(solution)/shard_map/ppermute | solution.py:557
  9.0 0.3 other.1
  9.3 3.8 %collective-permute-start.1 = (f32[8,16,128]{2,1,0:T(8,128)S(1)}, f32[8,16,128]{2,1,0:T(8,128)S(1)}, u32[]{:S(2)}, u32[]{:S(2)}) collective-permute-start(f32[8,16,128]{2,1,0:T(8,128)S(1)} %get-tuple-element.18), channel_id=1, source_target_pairs={{0,1},{1,0},{2,3},{3,2},{4,5},{5,4},{6,7},{7,6},{129,130},{130,129... | collective-permute-start | bytes 196616 | tf_op jit(solution)/shard_map/ppermute | solution.py:562
  13.1 1.6 %collective-permute-done.1.border_ref = f32[8,16,128]{2,1,0:T(8,128)S(1)} collective-permute-done((f32[8,16,128]{2,1,0:T(8,128)S(1)}, f32[8,16,128]{2,1,0:T(8,128)S(1)}, u32[]{:S(2)}, u32[]{:S(2)}) %collective-permute-start.1) | collective-permute-done | bytes 65568 | tf_op jit(solution)/shard_map/ppermute | solution.py:562
  14.8 6.4 %collective-permute-start.3 = (f32[72,16,128]{2,1,0:T(8,128)S(1)}, f32[72,16,128]{2,1,0:T(8,128)S(1)}, u32[]{:S(2)}, u32[]{:S(2)}) collective-permute-start(f32[72,16,128]{2,1,0:T(8,128)S(1)} %get-tuple-element.25), channel_id=1, source_target_pairs={{8,16},{16,8},{24,32},{32,24},{40,48},{48,40},{56,64},{64,56},{72,... | collective-permute-start | bytes 1769480 | tf_op jit(solution)/shard_map/ppermute | solution.py:565
  21.2 0.1 collective-permute-start.2
  21.3 7.5 %collective-permute-done.3.far_ref = f32[72,16,128]{2,1,0:T(8,128)S(1)} collective-permute-done((f32[72,16,128]{2,1,0:T(8,128)S(1)}, f32[72,16,128]{2,1,0:T(8,128)S(1)}, u32[]{:S(2)}, u32[]{:S(2)}) %collective-permute-start.3) | collective-permute-done | bytes 589856 | tf_op jit(solution)/shard_map/ppermute | solution.py:565
  28.7 0.0 collective-permute-done.2.near_ref
  28.7 0.0 copy-done.1
  28.7 0.0 copy-done.3
  28.7 0.0 copy-done.5
  28.8 9.7 %main.1 = (f32[256,128]{1,0:T(8,128)S(1)}, f32[4,4,16,16,128]{4,3,2,1,0:T(8,128)S(1)}) custom-call(f32[2,16,16,128]{3,2,1,0:T(8,128)S(1)} %copy-done.1, f32[2,16,16,128]{3,2,1,0:T(8,128)S(1)} %collective-permute-done.other_ref, f32[16,16,128]{2,1,0:T(8,128)S(1)} %copy-done.3, f32[16,16,128]{2,1,0:T(8,128)S(1)} %copy-done.5, f32[16,16,128]{2,1,0:T(8,128)S(1)} %copy-done.7, ...), custom_call_target="tpu_custom_call" | custom-call | flops 50000000 | bytes 4390912 | tf_op jit(solution)/shard_map/main/pallas_call | solution.py:533
  38.4 30.0 %all_to_all.5 = f32[256,1,128]{2,1,0:T(1,128)S(1)} all-to-all(f32[256,1,128]{2,1,0:T(1,128)S(1)} %bitcast.5), channel_id=1, replica_groups=mesh['section'=2,'sx'=16,'sy'=8] {'section','sx','sy'}, dimensions={0} | all-to-all | bytes 262144 | tf_op jit(solution)/shard_map/all_to_all | solution.py:576
  68.4 0.7 send.1
  69.1 0.6 collective-permute-start.4
  69.7 0.2 mine.1.mine_ref
  69.9 5.3 %collective-permute-done.4.other_ref = f32[16,16,128]{2,1,0:T(8,128)S(1)} collective-permute-done((f32[16,16,128]{2,1,0:T(8,128)S(1)}, f32[16,16,128]{2,1,0:T(8,128)S(1)}, u32[]{:S(2)}, u32[]{:S(2)}) %collective-permute-start.4) | collective-permute-done | bytes 131104 | tf_op jit(solution)/shard_map/ppermute | solution.py:578
  75.2 0.8 %join.1 = f32[2,16,16,128]{3,2,1,0:T(8,128)} custom-call(f32[2,16,16,128]{3,2,1,0:T(8,128)S(1)} %mine.1.mine_ref, f32[16,16,128]{2,1,0:T(8,128)S(1)} %collective-permute-done.4.other_ref), custom_call_target="tpu_custom_call" | custom-call | flops 1000000 | bytes 655360 | tf_op jit(solution)/shard_map/join/pallas_call | solution.py:533
  (10 shorter events, 0.0 us)
Async XLA Ops:
  0.0 9.0 %collective-permute-start = (f32[2,16,16,128]{3,2,1,0:T(8,128)}, f32[2,16,16,128]{3,2,1,0:T(8,128)S(1)}, u32[]{:S(2)}, u32[]{:S(2)}) collective-permute-start(f32[2,16,16,128]{3,2,1,0:T(8,128)} %own_ref.5), channel_id=1, source_target_pairs={{0,128},{128,0},{1,129},{129,1},{2,130},{130,2},{3,131},{131,3},{4... | collective-permute-start | bytes 786440 | tf_op jit(solution)/shard_map/ppermute | solution.py:557
  3.7 1.0 %copy-start = (f32[2,16,16,128]{3,2,1,0:T(8,128)S(1)}, f32[2,16,16,128]{3,2,1,0:T(8,128)}, u32[]{:S(2)}) copy-start(f32[2,16,16,128]{3,2,1,0:T(8,128)} %own_ref.5) | copy-start | bytes 786436
  4.7 0.9 %copy-start.2 = (f32[16,16,128]{2,1,0:T(8,128)S(1)}, f32[16,16,128]{2,1,0:T(8,128)}, u32[]{:S(2)}) copy-start(f32[16,16,128]{2,1,0:T(8,128)} %prev_ref.3) | copy-start | bytes 393220
  5.6 0.9 %copy-start.4 = (f32[16,16,128]{2,1,0:T(8,128)S(1)}, f32[16,16,128]{2,1,0:T(8,128)}, u32[]{:S(2)}) copy-start(f32[16,16,128]{2,1,0:T(8,128)} %diff_ref.3) | copy-start | bytes 393220
  6.5 0.9 %copy-start.6 = (f32[16,16,128]{2,1,0:T(8,128)S(1)}, f32[16,16,128]{2,1,0:T(8,128)}, u32[]{:S(2)}) copy-start(f32[16,16,128]{2,1,0:T(8,128)} %react_ref.3) | copy-start | bytes 393220
  7.4 21.3 %copy-start.1 = (f32[2,16,16,128]{3,2,1,0:T(8,128)S(1)}, f32[2,16,16,128]{3,2,1,0:T(8,128)}, u32[]{:S(2)}) copy-start(f32[2,16,16,128]{3,2,1,0:T(8,128)} %own_ref.5) | copy-start | bytes 786436
  7.4 21.3 %copy-start.3 = (f32[16,16,128]{2,1,0:T(8,128)S(1)}, f32[16,16,128]{2,1,0:T(8,128)}, u32[]{:S(2)}) copy-start(f32[16,16,128]{2,1,0:T(8,128)} %prev_ref.3) | copy-start | bytes 393220
  7.4 21.3 %copy-start.5 = (f32[16,16,128]{2,1,0:T(8,128)S(1)}, f32[16,16,128]{2,1,0:T(8,128)}, u32[]{:S(2)}) copy-start(f32[16,16,128]{2,1,0:T(8,128)} %diff_ref.3) | copy-start | bytes 393220
  7.4 21.3 %copy-start.7 = (f32[16,16,128]{2,1,0:T(8,128)S(1)}, f32[16,16,128]{2,1,0:T(8,128)}, u32[]{:S(2)}) copy-start(f32[16,16,128]{2,1,0:T(8,128)} %react_ref.3) | copy-start | bytes 393220
  9.3 5.5 %collective-permute-start.1 = (f32[8,16,128]{2,1,0:T(8,128)S(1)}, f32[8,16,128]{2,1,0:T(8,128)S(1)}, u32[]{:S(2)}, u32[]{:S(2)}) collective-permute-start(f32[8,16,128]{2,1,0:T(8,128)S(1)} %get-tuple-element.18), channel_id=1, source_target_pairs={{0,1},{1,0},{2,3},{3,2},{4,5},{5,4},{6,7},{7,6},{129,130},{130,129... | collective-permute-start | bytes 196616 | tf_op jit(solution)/shard_map/ppermute | solution.py:562
  14.8 13.9 %collective-permute-start.3 = (f32[72,16,128]{2,1,0:T(8,128)S(1)}, f32[72,16,128]{2,1,0:T(8,128)S(1)}, u32[]{:S(2)}, u32[]{:S(2)}) collective-permute-start(f32[72,16,128]{2,1,0:T(8,128)S(1)} %get-tuple-element.25), channel_id=1, source_target_pairs={{8,16},{16,8},{24,32},{32,24},{40,48},{48,40},{56,64},{64,56},{72,... | collective-permute-start | bytes 1769480 | tf_op jit(solution)/shard_map/ppermute | solution.py:565
  21.2 7.6 %collective-permute-start.2 = (f32[72,16,128]{2,1,0:T(8,128)S(1)}, f32[72,16,128]{2,1,0:T(8,128)S(1)}, u32[]{:S(2)}, u32[]{:S(2)}) collective-permute-start(f32[72,16,128]{2,1,0:T(8,128)S(1)} %get-tuple-element.26), channel_id=1, source_target_pairs={{0,8},{8,0},{16,24},{24,16},{32,40},{40,32},{48,56},{56,48},{64,72... | collective-permute-start | bytes 1769480 | tf_op jit(solution)/shard_map/ppermute | solution.py:566
  69.1 6.1 %collective-permute-start.4 = (f32[16,16,128]{2,1,0:T(8,128)S(1)}, f32[16,16,128]{2,1,0:T(8,128)S(1)}, u32[]{:S(2)}, u32[]{:S(2)}) collective-permute-start(f32[16,16,128]{2,1,0:T(8,128)S(1)} %get-tuple-element.24), channel_id=1, source_target_pairs={{0,128},{128,0},{1,129},{129,1},{2,130},{130,2},{3,131},{131,3},{4... | collective-permute-start | bytes 393224 | tf_op jit(solution)/shard_map/ppermute | solution.py:578

commit v5 on v4

--- a/solution.py
+++ b/solution.py
@@ -259,7 +259,7 @@
     lax.fori_loop(0, count // unroll, group, 0)
 
 
-def main_kernel(consts, own_ref, other_ref, prev_ref, diff_ref, react_ref, border_ref, near_ref, far_ref, part_ref, sums_ref,
+def main_kernel(consts, own_ref, other_ref, prev_ref, diff_ref, react_ref, border_ref, near_side_ref, far_side_ref, near_ref, far_ref, part_ref, sums_ref,
                 val, kap, frozen, prv, rea, dif, fx, fy, fz, alpha, beta, vec, ya, yb, table):
     eigen_basis, basis_inverse, shift_rows, pairs = consts
     nz, nx = prev_ref.shape[0], prev_ref.shape[1]
@@ -283,9 +283,8 @@
         return jnp.where(even, far, near), jnp.where(even, near, far)
 
     def assemble(plane):
-        at = nz * PARTS + plane
-        low = jnp.where(even, far_ref[at], near_ref[at])
-        high = jnp.where(even, near_ref[at], far_ref[at])
+        low = jnp.where(even, far_side_ref[plane], near_side_ref[plane])
+        high = jnp.where(even, near_side_ref[plane], far_side_ref[plane])
         sides = jnp.concatenate([tile(low[nx - 9 : nx - 8]), low[nx - 8 : nx], border_ref[plane], high[0:8], tile(high[8:9])], 0)
         for part in range(2):
             z = part * (nz // 2) + plane
@@ -555,15 +554,21 @@
     axes = ("section", "sx", "sy")
     partner = [(0, 1), (1, 0)]
     other = lax.ppermute(sections, "section", partner)
-    shapes = [(nz // 2, nx, ny), (nz * PARTS + nz // 2, TALL, ny), (nz * PARTS + nz // 2, TALL, ny)]
+    shapes = [(nz // 2, nx, ny), (nz * PARTS, TALL, ny), (nz * PARTS, TALL, ny)]
     packed = call(own_kernel, shapes, name="own")(sections, previous, diffusivity, reaction)
     border, near, far = call(other_kernel, shapes, name="other")(other, *packed)
-    edges = [(s * columns + a, s * columns + b) for s in range(2) for a, b in swaps(columns, s)]
-    border = lax.ppermute(border, ("section", "sy"), edges)
-    near = lax.dynamic_update_slice(near, border, (nz * PARTS, 0, 0))
-    far = lax.dynamic_update_slice(far, border, (nz * PARTS, 0, 0))
-    far = lax.ppermute(far, "sx", swaps(rows, 1))
-    near = lax.ppermute(near, "sx", swaps(rows, 0))
+    on_chip, off_chip, stay = swaps(rows, 0), swaps(rows, 1), [(i, i) for i in range(rows)]
+
+    def across(in_x):
+        return [
+            ((s * rows + a) * columns + c, (s * rows + b) * columns + d) for s in range(2) for a, b in in_x for c, d in swaps(columns, s)
+        ]
+
+    far = lax.ppermute(far, "sx", off_chip)
+    near = lax.ppermute(near, "sx", on_chip)
+    far_side = lax.ppermute(border, axes, across(off_chip))
+    near_side = lax.ppermute(border, axes, across(on_chip))
+    border = lax.ppermute(border, axes, across(stay))
     peers = 2 * columns * rows
     padded, work = (nz + 2, ROWS, ny), (nz, LAST - FIRST, ny)
     scratch = [
@@ -572,7 +577,7 @@
     ]
     part, sums = call(
         functools.partial(main_kernel, consts), [(peers, LANES), (ITERS, 4, nz, nx, ny)], scratch, 50_000_000, "main", 26
-    )(sections, other, previous, diffusivity, reaction, border, near, far)
+    )(sections, other, previous, diffusivity, reaction, border, near_side, far_side, near, far)
     total = lax.all_to_all(part.reshape(peers, 1, LANES), axes, 0, 0).reshape(peers, LANES)
     half, weight = call(functools.partial(send_kernel, consts), [previous.shape, (2 * ITERS, LANES)], name="send")(total, sums, other)
     got = lax.ppermute(half, "section", partner)

time: 76.2 us -> 75.6 us (level)
  waiting for transfers between devices: 15.6 us -> 9.32 us
  blocking collectives: 30 us -> 32.9 us
  starting transfers between devices: 14.6 us -> 17.3 us
    ppermute x3 -> x5, waiting for transfers between devices: 9.09 us -> 2.83 us  [the longest x1 1.57 us: body(): far_side = lax.ppermute(border, axes, across(off_chip))]
    all_to_all x1, blocking collectives: 30 us -> 32.9 us  [body(): lax.all_to_all(part.reshape(peers, 1, LANES), axes, 0, 0)]
    ppermute x3 -> x5, starting transfers between devices: 10.3 us -> 12.9 us  [the longest x1 3.38 us: body(): far = lax.ppermute(far, 'sx', off_chip)]
  transfers between devices with their start and end apart: 5 -> 7, of which waited for: 4 -> 5; matrix products, arithmetic and copies ran while one was open for 0% -> 0% of each run, Pallas kernels for 1% -> 1%
where the time goes in v5:
time: 75.6 us; the launch traced here: 75.3 us
  blocking collectives  32.9 us (44%)
  starting transfers between devices  17.3 us (23%)
  Pallas kernels  12 us (16%)
  waiting for transfers between devices  9.32 us (12%)
  local copies, waits for them, and re-layouts  3.71 us (5%)
    all_to_all x1, blocking collectives, body(): lax.all_to_all(part.reshape(peers, 1, LANES), axes, 0, 0)  32.9 us
    pallas_call x6, Pallas kernels, run(): pl.pallas_call(kernel, out_shape=shapes if many else shapes[0], in_specs=...  12 us
    ppermute x1, waiting for transfers between devices, body(): got = lax.ppermute(half, 'section', partner)  5.27 us
    ppermute x1, starting transfers between devices, body(): other = lax.ppermute(sections, 'section', partner)  3.74 us
    unnamed x16, local copies, waits for them, and re-layouts  3.71 us
    ppermute x1, starting transfers between devices, body(): far = lax.ppermute(far, 'sx', off_chip)  3.38 us
    ppermute x1, starting transfers between devices, body(): far_side = lax.ppermute(border, axes, across(off_chip))  3.03 us
    ppermute x1, starting transfers between devices, body(): near = lax.ppermute(near, 'sx', on_chip)  2.38 us
  transfers between devices with their start and end apart: 7, of which 5 were waited for; matrix products, arithmetic and copies ran while one was open for 0% of the time, Pallas kernels for 1%

profile of v5, /device:TPU:1, one launch (start us, length us, event | category | flops | bytes accessed | tf_op | source)
XLA Modules:
  0.0 75.3 jit_solution(8984074854511443498)
XLA Ops:
  0.0 3.7 %collective-permute-start = (f32[2,16,16,128]{3,2,1,0:T(8,128)}, f32[2,16,16,128]{3,2,1,0:T(8,128)S(1)}, u32[]{:S(2)}, u32[]{:S(2)}) collective-permute-start(f32[2,16,16,128]{3,2,1,0:T(8,128)} %own_ref.5), channel_id=1, source_target_pairs={{0,128},{128,0},{1,129},{129,1},{2,130},{130,2},{3,131},{131,3},{4... | collective-permute-start | bytes 786440 | tf_op jit(solution)/shard_map/ppermute | solution.py:556
  3.7 1.0 %copy-done = f32[2,16,16,128]{3,2,1,0:T(8,128)S(1)} copy-done((f32[2,16,16,128]{3,2,1,0:T(8,128)S(1)}, f32[2,16,16,128]{3,2,1,0:T(8,128)}, u32[]{:S(2)}) %copy-start) | copy-done | bytes 262168
  4.7 0.9 %copy-done.2 = f32[16,16,128]{2,1,0:T(8,128)S(1)} copy-done((f32[16,16,128]{2,1,0:T(8,128)S(1)}, f32[16,16,128]{2,1,0:T(8,128)}, u32[]{:S(2)}) %copy-start.2) | copy-done | bytes 131096
  5.6 0.9 %copy-done.4 = f32[16,16,128]{2,1,0:T(8,128)S(1)} copy-done((f32[16,16,128]{2,1,0:T(8,128)S(1)}, f32[16,16,128]{2,1,0:T(8,128)}, u32[]{:S(2)}) %copy-start.4) | copy-done | bytes 131096
  6.5 0.9 %copy-done.6 = f32[16,16,128]{2,1,0:T(8,128)S(1)} copy-done((f32[16,16,128]{2,1,0:T(8,128)S(1)}, f32[16,16,128]{2,1,0:T(8,128)}, u32[]{:S(2)}) %copy-start.6) | copy-done | bytes 131096
  7.5 0.3 own.1
  7.8 1.2 %collective-permute-done.other_ref = f32[2,16,16,128]{3,2,1,0:T(8,128)S(1)} collective-permute-done((f32[2,16,16,128]{3,2,1,0:T(8,128)}, f32[2,16,16,128]{3,2,1,0:T(8,128)S(1)}, u32[]{:S(2)}, u32[]{:S(2)}) %collective-permute-start) | collective-permute-done | bytes 262176 | tf_op jit(solution)/shard_map/ppermute | solution.py:556
  9.0 0.3 other.1
  9.3 2.4 %collective-permute-start.4 = (f32[64,16,128]{2,1,0:T(8,128)S(1)}, f32[64,16,128]{2,1,0:T(8,128)S(1)}, u32[]{:S(2)}, u32[]{:S(2)}) collective-permute-start(f32[64,16,128]{2,1,0:T(8,128)S(1)} %get-tuple-element.19), channel_id=1, source_target_pairs={{0,8},{8,0},{16,24},{24,16},{32,40},{40,32},{48,56},{56,48},{64,72... | collective-permute-start | bytes 1572872 | tf_op jit(solution)/shard_map/ppermute | solution.py:568
  11.7 3.4 %collective-permute-start.5 = (f32[64,16,128]{2,1,0:T(8,128)S(1)}, f32[64,16,128]{2,1,0:T(8,128)S(1)}, u32[]{:S(2)}, u32[]{:S(2)}) collective-permute-start(f32[64,16,128]{2,1,0:T(8,128)S(1)} %get-tuple-element.20), channel_id=1, source_target_pairs={{8,16},{16,8},{24,32},{32,24},{40,48},{48,40},{56,64},{64,56},{72,... | collective-permute-start | bytes 1572872 | tf_op jit(solution)/shard_map/ppermute | solution.py:567
  15.1 3.0 %collective-permute-start.3 = (f32[8,16,128]{2,1,0:T(8,128)S(1)}, f32[8,16,128]{2,1,0:T(8,128)S(1)}, u32[]{:S(2)}, u32[]{:S(2)}) collective-permute-start(f32[8,16,128]{2,1,0:T(8,128)S(1)} %get-tuple-element.18), channel_id=1, source_target_pairs={{8,17},{9,16},{10,19},{11,18},{12,21},{13,20},{14,23},{15,22},{16,... | collective-permute-start | bytes 196616 | tf_op jit(solution)/shard_map/ppermute | solution.py:569
  18.1 1.9 %collective-permute-start.2 = (f32[8,16,128]{2,1,0:T(8,128)S(1)}, f32[8,16,128]{2,1,0:T(8,128)S(1)}, u32[]{:S(2)}, u32[]{:S(2)}) collective-permute-start(f32[8,16,128]{2,1,0:T(8,128)S(1)} %get-tuple-element.18), channel_id=1, source_target_pairs={{0,9},{1,8},{2,11},{3,10},{4,13},{5,12},{6,15},{7,14},{8,1},{9,0},... | collective-permute-start | bytes 196616 | tf_op jit(solution)/shard_map/ppermute | solution.py:570
  20.1 2.2 %collective-permute-start.1 = (f32[8,16,128]{2,1,0:T(8,128)S(1)}, f32[8,16,128]{2,1,0:T(8,128)S(1)}, u32[]{:S(2)}, u32[]{:S(2)}) collective-permute-start(f32[8,16,128]{2,1,0:T(8,128)S(1)} %get-tuple-element.18), channel_id=1, source_target_pairs={{0,1},{1,0},{2,3},{3,2},{4,5},{5,4},{6,7},{7,6},{8,9},{9,8},{10,11... | collective-permute-start | bytes 196616 | tf_op jit(solution)/shard_map/ppermute | solution.py:571
  22.3 1.6 %collective-permute-done.3.far_side_ref = f32[8,16,128]{2,1,0:T(8,128)S(1)} collective-permute-done((f32[8,16,128]{2,1,0:T(8,128)S(1)}, f32[8,16,128]{2,1,0:T(8,128)S(1)}, u32[]{:S(2)}, u32[]{:S(2)}) %collective-permute-start.3) | collective-permute-done | bytes 65568 | tf_op jit(solution)/shard_map/ppermute | solution.py:569
  23.9 0.6 collective-permute-done.2.near_side_ref
  24.4 0.7 collective-permute-done.1.border_ref
  25.1 0.0 collective-permute-done.4.near_ref
  25.2 9.7 %main.1 = (f32[256,128]{1,0:T(8,128)S(1)}, f32[4,4,16,16,128]{4,3,2,1,0:T(8,128)S(1)}) custom-call(f32[2,16,16,128]{3,2,1,0:T(8,128)S(1)} %copy-done.1, f32[2,16,16,128]{3,2,1,0:T(8,128)S(1)} %collective-permute-done.other_ref, f32[16,16,128]{2,1,0:T(8,128)S(1)} %copy-done.3, f32[16,16,128]{2,1,0:T(8,128)S(1)} %copy-done.5, f32[16,16,128]{2,1,0:T(8,128)S(1)} %copy-done.7, ...), custom_call_target="tpu_custom_call" | custom-call | flops 50000000 | bytes 4390912 | tf_op jit(solution)/shard_map/main/pallas_call | solution.py:532
  34.8 32.9 %all_to_all.5 = f32[256,1,128]{2,1,0:T(1,128)S(1)} all-to-all(f32[256,1,128]{2,1,0:T(1,128)S(1)} %bitcast.5), channel_id=1, replica_groups=mesh['section'=2,'sx'=16,'sy'=8] {'section','sx','sy'}, dimensions={0} | all-to-all | bytes 262144 | tf_op jit(solution)/shard_map/all_to_all | solution.py:581
  67.7 0.7 send.1
  68.4 0.6 collective-permute-start.6
  69.0 0.2 mine.1.mine_ref
  69.2 5.3 %collective-permute-done.6.other_ref = f32[16,16,128]{2,1,0:T(8,128)S(1)} collective-permute-done((f32[16,16,128]{2,1,0:T(8,128)S(1)}, f32[16,16,128]{2,1,0:T(8,128)S(1)}, u32[]{:S(2)}, u32[]{:S(2)}) %collective-permute-start.6) | collective-permute-done | bytes 131104 | tf_op jit(solution)/shard_map/ppermute | solution.py:583
  74.5 0.8 %join.1 = f32[2,16,16,128]{3,2,1,0:T(8,128)} custom-call(f32[2,16,16,128]{3,2,1,0:T(8,128)S(1)} %mine.1.mine_ref, f32[16,16,128]{2,1,0:T(8,128)S(1)} %collective-permute-done.6.other_ref), custom_call_target="tpu_custom_call" | custom-call | flops 1000000 | bytes 655360 | tf_op jit(solution)/shard_map/join/pallas_call | solution.py:532
  (13 shorter events, 0.0 us)
Async XLA Ops:
  0.0 9.0 %collective-permute-start = (f32[2,16,16,128]{3,2,1,0:T(8,128)}, f32[2,16,16,128]{3,2,1,0:T(8,128)S(1)}, u32[]{:S(2)}, u32[]{:S(2)}) collective-permute-start(f32[2,16,16,128]{3,2,1,0:T(8,128)} %own_ref.5), channel_id=1, source_target_pairs={{0,128},{128,0},{1,129},{129,1},{2,130},{130,2},{3,131},{131,3},{4... | collective-permute-start | bytes 786440 | tf_op jit(solution)/shard_map/ppermute | solution.py:556
  3.7 1.0 %copy-start = (f32[2,16,16,128]{3,2,1,0:T(8,128)S(1)}, f32[2,16,16,128]{3,2,1,0:T(8,128)}, u32[]{:S(2)}) copy-start(f32[2,16,16,128]{3,2,1,0:T(8,128)} %own_ref.5) | copy-start | bytes 786436
  4.7 0.9 %copy-start.2 = (f32[16,16,128]{2,1,0:T(8,128)S(1)}, f32[16,16,128]{2,1,0:T(8,128)}, u32[]{:S(2)}) copy-start(f32[16,16,128]{2,1,0:T(8,128)} %prev_ref.3) | copy-start | bytes 393220
  5.6 0.9 %copy-start.4 = (f32[16,16,128]{2,1,0:T(8,128)S(1)}, f32[16,16,128]{2,1,0:T(8,128)}, u32[]{:S(2)}) copy-start(f32[16,16,128]{2,1,0:T(8,128)} %diff_ref.3) | copy-start | bytes 393220
  6.5 0.9 %copy-start.6 = (f32[16,16,128]{2,1,0:T(8,128)S(1)}, f32[16,16,128]{2,1,0:T(8,128)}, u32[]{:S(2)}) copy-start(f32[16,16,128]{2,1,0:T(8,128)} %react_ref.3) | copy-start | bytes 393220
  7.4 17.7 %copy-start.1 = (f32[2,16,16,128]{3,2,1,0:T(8,128)S(1)}, f32[2,16,16,128]{3,2,1,0:T(8,128)}, u32[]{:S(2)}) copy-start(f32[2,16,16,128]{3,2,1,0:T(8,128)} %own_ref.5) | copy-start | bytes 786436
  7.4 17.7 %copy-start.3 = (f32[16,16,128]{2,1,0:T(8,128)S(1)}, f32[16,16,128]{2,1,0:T(8,128)}, u32[]{:S(2)}) copy-start(f32[16,16,128]{2,1,0:T(8,128)} %prev_ref.3) | copy-start | bytes 393220
  7.4 17.7 %copy-start.5 = (f32[16,16,128]{2,1,0:T(8,128)S(1)}, f32[16,16,128]{2,1,0:T(8,128)}, u32[]{:S(2)}) copy-start(f32[16,16,128]{2,1,0:T(8,128)} %diff_ref.3) | copy-start | bytes 393220
  7.4 17.7 %copy-start.7 = (f32[16,16,128]{2,1,0:T(8,128)S(1)}, f32[16,16,128]{2,1,0:T(8,128)}, u32[]{:S(2)}) copy-start(f32[16,16,128]{2,1,0:T(8,128)} %react_ref.3) | copy-start | bytes 393220
  9.3 15.8 %collective-permute-start.4 = (f32[64,16,128]{2,1,0:T(8,128)S(1)}, f32[64,16,128]{2,1,0:T(8,128)S(1)}, u32[]{:S(2)}, u32[]{:S(2)}) collective-permute-start(f32[64,16,128]{2,1,0:T(8,128)S(1)} %get-tuple-element.19), channel_id=1, source_target_pairs={{0,8},{8,0},{16,24},{24,16},{32,40},{40,32},{48,56},{56,48},{64,72... | collective-permute-start | bytes 1572872 | tf_op jit(solution)/shard_map/ppermute | solution.py:568
  11.7 13.4 %collective-permute-start.5 = (f32[64,16,128]{2,1,0:T(8,128)S(1)}, f32[64,16,128]{2,1,0:T(8,128)S(1)}, u32[]{:S(2)}, u32[]{:S(2)}) collective-permute-start(f32[64,16,128]{2,1,0:T(8,128)S(1)} %get-tuple-element.20), channel_id=1, source_target_pairs={{8,16},{16,8},{24,32},{32,24},{40,48},{48,40},{56,64},{64,56},{72,... | collective-permute-start | bytes 1572872 | tf_op jit(solution)/shard_map/ppermute | solution.py:567
  15.1 8.8 %collective-permute-start.3 = (f32[8,16,128]{2,1,0:T(8,128)S(1)}, f32[8,16,128]{2,1,0:T(8,128)S(1)}, u32[]{:S(2)}, u32[]{:S(2)}) collective-permute-start(f32[8,16,128]{2,1,0:T(8,128)S(1)} %get-tuple-element.18), channel_id=1, source_target_pairs={{8,17},{9,16},{10,19},{11,18},{12,21},{13,20},{14,23},{15,22},{16,... | collective-permute-start | bytes 196616 | tf_op jit(solution)/shard_map/ppermute | solution.py:569
  18.1 6.3 %collective-permute-start.2 = (f32[8,16,128]{2,1,0:T(8,128)S(1)}, f32[8,16,128]{2,1,0:T(8,128)S(1)}, u32[]{:S(2)}, u32[]{:S(2)}) collective-permute-start(f32[8,16,128]{2,1,0:T(8,128)S(1)} %get-tuple-element.18), channel_id=1, source_target_pairs={{0,9},{1,8},{2,11},{3,10},{4,13},{5,12},{6,15},{7,14},{8,1},{9,0},... | collective-permute-start | bytes 196616 | tf_op jit(solution)/shard_map/ppermute | solution.py:570
  20.1 5.1 %collective-permute-start.1 = (f32[8,16,128]{2,1,0:T(8,128)S(1)}, f32[8,16,128]{2,1,0:T(8,128)S(1)}, u32[]{:S(2)}, u32[]{:S(2)}) collective-permute-start(f32[8,16,128]{2,1,0:T(8,128)S(1)} %get-tuple-element.18), channel_id=1, source_target_pairs={{0,1},{1,0},{2,3},{3,2},{4,5},{5,4},{6,7},{7,6},{8,9},{9,8},{10,11... | collective-permute-start | bytes 196616 | tf_op jit(solution)/shard_map/ppermute | solution.py:571
  68.4 6.1 %collective-permute-start.6 = (f32[16,16,128]{2,1,0:T(8,128)S(1)}, f32[16,16,128]{2,1,0:T(8,128)S(1)}, u32[]{:S(2)}, u32[]{:S(2)}) collective-permute-start(f32[16,16,128]{2,1,0:T(8,128)S(1)} %get-tuple-element.24), channel_id=1, source_target_pairs={{0,128},{128,0},{1,129},{129,1},{2,130},{130,2},{3,131},{131,3},{4... | collective-permute-start | bytes 393224 | tf_op jit(solution)/shard_map/ppermute | solution.py:583

commit v6 on v4

--- a/solution.py
+++ b/solution.py
@@ -187,7 +187,7 @@
 
 ORDER = (0, 1, 4, 5, 6, 2, 3)
 TALL = 16
-PARTS = 4
+OWN_PARTS = 3
 
 
 def border_start():
@@ -202,44 +202,54 @@
     return lax.rem(lax.axis_index("sx"), 2) == 0
 
 
-def pack(border_ref, near_ref, far_ref, load, fields, first_slot, partial):
+def own_place(slot, z):
+    entry, row = divmod(8 * slot, TALL)
+    last, ninth = divmod(40 + slot, TALL)
+    return z * OWN_PARTS + entry, row, z * OWN_PARTS + last, ninth
+
+
+def other_place(slot, z, nz):
+    return z, 8 * slot, nz + z // 8, 2 * lax.rem(z, 8) + slot
+
+
+def pack(border_ref, near_ref, far_ref, load, fields, place, partial):
     nz = 2 * border_ref.shape[0]
     nx = border_ref.shape[1]
     lanes = lane_ids(nx)
     start = leaving_start()
     even = on_even_row()
 
-    def plane_pair(plane):
+    for plane in range(nz // 2):
         tile = partial(plane)
         for part in range(2):
             z = part * (nz // 2) + plane
-            for slot, f in enumerate(fields, first_slot):
+            for slot, f in enumerate(fields):
                 cell = load(f, z)
                 at = part * 64 + f * EDGE
                 moved = pltpu.roll(cell, lax.rem(at + LANES - start, LANES), 1)
                 tile = jnp.where((lanes >= at) & (lanes < at + EDGE), moved, tile)
-                entry, row = divmod(8 * slot, TALL)
-                last, ninth = divmod(56 + slot, TALL)
-                near_ref[z * PARTS + entry, row : row + 8] = jnp.where(even, cell[nx - 8 : nx], cell[0:8])
-                far_ref[z * PARTS + entry, row : row + 8] = jnp.where(even, cell[0:8], cell[nx - 8 : nx])
-                near_ref[z * PARTS + last, ninth : ninth + 1] = jnp.where(even, cell[nx - 9 : nx - 8], cell[8:9])
-                far_ref[z * PARTS + last, ninth : ninth + 1] = jnp.where(even, cell[8:9], cell[nx - 9 : nx - 8])
+                entry, row, last, ninth = place(slot, z)
+                near_ref[entry, row : row + 8] = jnp.where(even, cell[nx - 8 : nx], cell[0:8])
+                far_ref[entry, row : row + 8] = jnp.where(even, cell[0:8], cell[nx - 8 : nx])
+                near_ref[last, ninth : ninth + 1] = jnp.where(even, cell[nx - 9 : nx - 8], cell[8:9])
+                far_ref[last, ninth : ninth + 1] = jnp.where(even, cell[8:9], cell[nx - 9 : nx - 8])
         border_ref[plane] = tile
-
-    each_plane(nz // 2, 4, plane_pair)
 
 
 def own_kernel(own_ref, prev_ref, diff_ref, react_ref, border_ref, near_ref, far_ref):
     nx = prev_ref.shape[1]
     refs = {4: prev_ref, 5: diff_ref, 6: react_ref}
     load = lambda f, z: own_ref[f, z] if f < 2 else refs[f][z]
-    pack(border_ref, near_ref, far_ref, load, ORDER[:5], 0, lambda plane: jnp.zeros((nx, LANES), jnp.float32))
-
-
-def other_kernel(other_ref, own_border_ref, own_near_ref, own_far_ref, border_ref, near_ref, far_ref):
-    near_ref[...] = own_near_ref[...]
-    far_ref[...] = own_far_ref[...]
-    pack(border_ref, near_ref, far_ref, lambda f, z: other_ref[f - 2, z], ORDER[5:], 5, lambda plane: own_border_ref[plane])
+    pack(border_ref, near_ref, far_ref, load, ORDER[:5], own_place, lambda plane: jnp.zeros((nx, LANES), jnp.float32))
+
+
+def other_kernel(other_ref, own_border_ref, border_ref, near_ref, far_ref):
+    nz = other_ref.shape[1]
+
+    def place(slot, z):
+        return z, 8 * slot, nz + z // 8, 2 * (z % 8) + slot
+
+    pack(border_ref, near_ref, far_ref, lambda f, z: other_ref[f - 2, z], ORDER[5:], place, lambda plane: own_border_ref[plane])
 
 
 ROWS = 48
@@ -259,7 +269,7 @@
     lax.fori_loop(0, count // unroll, group, 0)
 
 
-def main_kernel(consts, own_ref, other_ref, prev_ref, diff_ref, react_ref, border_ref, near_ref, far_ref, part_ref, sums_ref,
+def main_kernel(consts, own_ref, other_ref, prev_ref, diff_ref, react_ref, border_ref, own_near_ref, own_far_ref, near_ref, far_ref, part_ref, sums_ref,
                 val, kap, frozen, prv, rea, dif, fx, fy, fz, alpha, beta, vec, ya, yb, table):
     eigen_basis, basis_inverse, shift_rows, pairs = consts
     nz, nx = prev_ref.shape[0], prev_ref.shape[1]
@@ -278,12 +288,13 @@
             for ref in (val, kap, ya, yb):
                 ref[f, at] = zero_plane
 
-    def both(entry, row, count):
-        near, far = near_ref[entry, row : row + count], far_ref[entry, row : row + count]
+    def both(slot, entry, row, count):
+        refs = (own_near_ref, own_far_ref) if slot < 5 else (near_ref, far_ref)
+        near, far = [ref[entry, pl.ds(row, count)] for ref in refs]
         return jnp.where(even, far, near), jnp.where(even, near, far)
 
     def assemble(plane):
-        at = nz * PARTS + plane
+        at = nz + nz // 8 + plane
         low = jnp.where(even, far_ref[at], near_ref[at])
         high = jnp.where(even, near_ref[at], far_ref[at])
         sides = jnp.concatenate([tile(low[nx - 9 : nx - 8]), low[nx - 8 : nx], border_ref[plane], high[0:8], tile(high[8:9])], 0)
@@ -293,10 +304,9 @@
             def column(f):
                 slot = ORDER.index(f)
                 mid = (own_ref[0, z], own_ref[1, z], prev_ref[z], diff_ref[z], react_ref[z], other_ref[0, z], other_ref[1, z])[slot]
-                entry, row = divmod(8 * slot, TALL)
-                low, high = both(z * PARTS + entry, row, 8)
-                entry, row = divmod(56 + slot, TALL)
-                low_end, high_end = both(z * PARTS + entry, row, 1)
+                entry, row, last, ninth = own_place(slot, z) if slot < 5 else other_place(slot - 5, z, nz)
+                low, high = both(slot, entry, row, 8)
+                low_end, high_end = both(slot, last, ninth, 1)
                 cells = jnp.concatenate([tile(low_end), low, mid, high, tile(high_end)], 0)
                 at = part * 64 + f * EDGE
                 return jnp.where(edge, pltpu.roll(sides, lax.rem(start + LANES - at, LANES), 1), cells)
@@ -555,13 +565,17 @@
     axes = ("section", "sx", "sy")
     partner = [(0, 1), (1, 0)]
     other = lax.ppermute(sections, "section", partner)
-    shapes = [(nz // 2, nx, ny), (nz * PARTS + nz // 2, TALL, ny), (nz * PARTS + nz // 2, TALL, ny)]
-    packed = call(own_kernel, shapes, name="own")(sections, previous, diffusivity, reaction)
-    border, near, far = call(other_kernel, shapes, name="other")(other, *packed)
+    edge, rest = (nz // 2, nx, ny), nz + nz // 8
+    own = (nz * OWN_PARTS, TALL, ny)
+    border, own_near, own_far = call(own_kernel, [edge, own, own], name="own")(sections, previous, diffusivity, reaction)
+    own_far = lax.ppermute(own_far, "sx", swaps(rows, 1))
+    own_near = lax.ppermute(own_near, "sx", swaps(rows, 0))
+    late = (rest + nz // 2, TALL, ny)
+    border, near, far = call(other_kernel, [edge, late, late], name="other")(other, border)
     edges = [(s * columns + a, s * columns + b) for s in range(2) for a, b in swaps(columns, s)]
     border = lax.ppermute(border, ("section", "sy"), edges)
-    near = lax.dynamic_update_slice(near, border, (nz * PARTS, 0, 0))
-    far = lax.dynamic_update_slice(far, border, (nz * PARTS, 0, 0))
+    near = lax.dynamic_update_slice(near, border, (rest, 0, 0))
+    far = lax.dynamic_update_slice(far, border, (rest, 0, 0))
     far = lax.ppermute(far, "sx", swaps(rows, 1))
     near = lax.ppermute(near, "sx", swaps(rows, 0))
     peers = 2 * columns * rows
@@ -572,7 +586,7 @@
     ]
     part, sums = call(
         functools.partial(main_kernel, consts), [(peers, LANES), (ITERS, 4, nz, nx, ny)], scratch, 50_000_000, "main", 26
-    )(sections, other, previous, diffusivity, reaction, border, near, far)
+    )(sections, other, previous, diffusivity, reaction, border, own_near, own_far, near, far)
     total = lax.all_to_all(part.reshape(peers, 1, LANES), axes, 0, 0).reshape(peers, LANES)
     half, weight = call(functools.partial(send_kernel, consts), [previous.shape, (2 * ITERS, LANES)], name="send")(total, sums, other)
     got = lax.ppermute(half, "section", partner)

time: 76.2 us -> 75.8 us (level)
  waiting for transfers between devices: 15.6 us -> 11.7 us
  local copies, waits for them, and re-layouts: 3.72 us -> 7.37 us
  blocking collectives: 30 us -> 28.3 us
  starting transfers between devices: 14.6 us -> 16.2 us
    ppermute x0 -> x2, starting transfers between devices: none -> 5.36 us  [the longest x1 3.44 us: body(): own_far = lax.ppermute(own_far, 'sx', swaps(rows, 1))]
    ppermute x1, waiting for transfers between devices: 7.45 us -> 2.28 us  [body(): far = lax.ppermute(far, 'sx', swaps(rows, 1))]
    ppermute x1, starting transfers between devices: 6.37 us -> 2.63 us  [body(): far = lax.ppermute(far, 'sx', swaps(rows, 1))]
    unnamed x16, local copies, waits for them, and re-layouts: 3.71 us -> 7.36 us
    ppermute x0 -> x2, waiting for transfers between devices: none -> 2.86 us  [the longest x1 2.86 us: body(): own_far = lax.ppermute(own_far, 'sx', swaps(rows, 1))]
    all_to_all x1, blocking collectives: 30 us -> 28.3 us  [body(): lax.all_to_all(part.reshape(peers, 1, LANES), axes, 0, 0)]
    ppermute x1, waiting for transfers between devices: 1.64 us -> 0.01 us  [body(): border = lax.ppermute(border, ('section', 'sy'), edges)]
  transfers between devices with their start and end apart: 5 -> 7, of which waited for: 4 -> 4; matrix products, arithmetic and copies ran while one was open for 0% -> 0% of each run, Pallas kernels for 1% -> 1%
where the time goes in v6:
time: 75.8 us; the launch traced here: 75.5 us
  blocking collectives  28.3 us (37%)
  starting transfers between devices  16.2 us (21%)
  Pallas kernels  11.8 us (16%)
  waiting for transfers between devices  11.7 us (15%)
  local copies, waits for them, and re-layouts  7.37 us (10%)
    all_to_all x1, blocking collectives, body(): lax.all_to_all(part.reshape(peers, 1, LANES), axes, 0, 0)  28.3 us
    pallas_call x6, Pallas kernels, run(): pl.pallas_call(kernel, out_shape=shapes if many else shapes[0], in_specs=...  11.8 us
    unnamed x16, local copies, waits for them, and re-layouts  7.36 us
    ppermute x1, waiting for transfers between devices, body(): got = lax.ppermute(half, 'section', partner)  5.27 us
    ppermute x1, starting transfers between devices, body(): border = lax.ppermute(border, ('section', 'sy'), edges)  3.8 us
    ppermute x1, starting transfers between devices, body(): other = lax.ppermute(sections, 'section', partner)  3.74 us
    ppermute x1, starting transfers between devices, body(): own_far = lax.ppermute(own_far, 'sx', swaps(rows, 1))  3.44 us
    ppermute x1, waiting for transfers between devices, body(): own_far = lax.ppermute(own_far, 'sx', swaps(rows, 1))  2.86 us
  transfers between devices with their start and end apart: 7, of which 4 were waited for; matrix products, arithmetic and copies ran while one was open for 0% of the time, Pallas kernels for 1%

profile of v6, /device:TPU:1, one launch (start us, length us, event | category | flops | bytes accessed | tf_op | source)
XLA Modules:
  0.0 75.5 jit_solution(12395004205844989321)
XLA Ops:
  0.0 3.7 %collective-permute-start = (f32[2,16,16,128]{3,2,1,0:T(8,128)}, f32[2,16,16,128]{3,2,1,0:T(8,128)S(1)}, u32[]{:S(2)}, u32[]{:S(2)}) collective-permute-start(f32[2,16,16,128]{3,2,1,0:T(8,128)} %own_ref.5), channel_id=1, source_target_pairs={{0,128},{128,0},{1,129},{129,1},{2,130},{130,2},{3,131},{131,3},{4... | collective-permute-start | bytes 786440 | tf_op jit(solution)/shard_map/ppermute | solution.py:567
  3.7 1.0 %copy-done = f32[2,16,16,128]{3,2,1,0:T(8,128)S(1)} copy-done((f32[2,16,16,128]{3,2,1,0:T(8,128)S(1)}, f32[2,16,16,128]{3,2,1,0:T(8,128)}, u32[]{:S(2)}) %copy-start) | copy-done | bytes 262168
  4.7 0.9 %copy-done.2 = f32[16,16,128]{2,1,0:T(8,128)S(1)} copy-done((f32[16,16,128]{2,1,0:T(8,128)S(1)}, f32[16,16,128]{2,1,0:T(8,128)}, u32[]{:S(2)}) %copy-start.2) | copy-done | bytes 131096
  5.6 0.9 %copy-done.4 = f32[16,16,128]{2,1,0:T(8,128)S(1)} copy-done((f32[16,16,128]{2,1,0:T(8,128)S(1)}, f32[16,16,128]{2,1,0:T(8,128)}, u32[]{:S(2)}) %copy-start.4) | copy-done | bytes 131096
  6.5 0.9 %copy-done.6 = f32[16,16,128]{2,1,0:T(8,128)S(1)} copy-done((f32[16,16,128]{2,1,0:T(8,128)S(1)}, f32[16,16,128]{2,1,0:T(8,128)}, u32[]{:S(2)}) %copy-start.6) | copy-done | bytes 131096
  7.4 0.3 own.1
  7.7 1.3 %collective-permute-done.other_ref = f32[2,16,16,128]{3,2,1,0:T(8,128)S(1)} collective-permute-done((f32[2,16,16,128]{3,2,1,0:T(8,128)}, f32[2,16,16,128]{3,2,1,0:T(8,128)S(1)}, u32[]{:S(2)}, u32[]{:S(2)}) %collective-permute-start) | collective-permute-done | bytes 262176 | tf_op jit(solution)/shard_map/ppermute | solution.py:567
  9.2 3.8 %collective-permute-start.1 = (f32[8,16,128]{2,1,0:T(8,128)S(1)}, f32[8,16,128]{2,1,0:T(8,128)S(1)}, u32[]{:S(2)}, u32[]{:S(2)}) collective-permute-start(f32[8,16,128]{2,1,0:T(8,128)S(1)} %get-tuple-element.16), channel_id=1, source_target_pairs={{0,1},{1,0},{2,3},{3,2},{4,5},{5,4},{6,7},{7,6},{129,130},{130,129... | collective-permute-start | bytes 196616 | tf_op jit(solution)/shard_map/ppermute | solution.py:576
  13.0 1.9 %collective-permute-start.2 = (f32[48,16,128]{2,1,0:T(8,128)S(1)}, f32[48,16,128]{2,1,0:T(8,128)S(1)}, u32[]{:S(2)}, u32[]{:S(2)}) collective-permute-start(f32[48,16,128]{2,1,0:T(8,128)S(1)} %get-tuple-element.17), channel_id=1, source_target_pairs={{0,8},{8,0},{16,24},{24,16},{32,40},{40,32},{48,56},{56,48},{64,72... | collective-permute-start | bytes 1179656 | tf_op jit(solution)/shard_map/ppermute | solution.py:572
  14.9 3.4 %collective-permute-start.3 = (f32[48,16,128]{2,1,0:T(8,128)S(1)}, f32[48,16,128]{2,1,0:T(8,128)S(1)}, u32[]{:S(2)}, u32[]{:S(2)}) collective-permute-start(f32[48,16,128]{2,1,0:T(8,128)S(1)} %get-tuple-element.18), channel_id=1, source_target_pairs={{8,16},{16,8},{24,32},{32,24},{40,48},{48,40},{56,64},{64,56},{72,... | collective-permute-start | bytes 1179656 | tf_op jit(solution)/shard_map/ppermute | solution.py:571
  18.4 2.6 %collective-permute-start.5 = (f32[26,16,128]{2,1,0:T(8,128)S(1)}, f32[26,16,128]{2,1,0:T(8,128)S(1)}, u32[]{:S(2)}, u32[]{:S(2)}) collective-permute-start(f32[26,16,128]{2,1,0:T(8,128)S(1)} %get-tuple-element.25), channel_id=1, source_target_pairs={{8,16},{16,8},{24,32},{32,24},{40,48},{48,40},{56,64},{64,56},{72,... | collective-permute-start | bytes 638984 | tf_op jit(solution)/shard_map/ppermute | solution.py:579
  21.1 2.9 %collective-permute-done.3.own_far_ref = f32[48,16,128]{2,1,0:T(8,128)S(1)} collective-permute-done((f32[48,16,128]{2,1,0:T(8,128)S(1)}, f32[48,16,128]{2,1,0:T(8,128)S(1)}, u32[]{:S(2)}, u32[]{:S(2)}) %collective-permute-start.3) | collective-permute-done | bytes 393248 | tf_op jit(solution)/shard_map/ppermute | solution.py:571
  24.0 2.3 %collective-permute-done.5.far_ref = f32[26,16,128]{2,1,0:T(8,128)S(1)} collective-permute-done((f32[26,16,128]{2,1,0:T(8,128)S(1)}, f32[26,16,128]{2,1,0:T(8,128)S(1)}, u32[]{:S(2)}, u32[]{:S(2)}) %collective-permute-start.5) | collective-permute-done | bytes 213024 | tf_op jit(solution)/shard_map/ppermute | solution.py:579
  26.3 0.9 %copy-done.1 = f32[2,16,16,128]{3,2,1,0:T(8,128)S(1)} copy-done((f32[2,16,16,128]{3,2,1,0:T(8,128)S(1)}, f32[2,16,16,128]{3,2,1,0:T(8,128)}, u32[]{:S(2)}) %copy-start.1) | copy-done | bytes 262168
  27.2 0.9 %copy-done.3 = f32[16,16,128]{2,1,0:T(8,128)S(1)} copy-done((f32[16,16,128]{2,1,0:T(8,128)S(1)}, f32[16,16,128]{2,1,0:T(8,128)}, u32[]{:S(2)}) %copy-start.3) | copy-done | bytes 131096
  28.1 0.9 %copy-done.5 = f32[16,16,128]{2,1,0:T(8,128)S(1)} copy-done((f32[16,16,128]{2,1,0:T(8,128)S(1)}, f32[16,16,128]{2,1,0:T(8,128)}, u32[]{:S(2)}) %copy-start.5) | copy-done | bytes 131096
  29.0 0.9 %copy-done.7 = f32[16,16,128]{2,1,0:T(8,128)S(1)} copy-done((f32[16,16,128]{2,1,0:T(8,128)S(1)}, f32[16,16,128]{2,1,0:T(8,128)}, u32[]{:S(2)}) %copy-start.7) | copy-done | bytes 131096
  30.0 9.6 %main.1 = (f32[256,128]{1,0:T(8,128)S(1)}, f32[4,4,16,16,128]{4,3,2,1,0:T(8,128)S(1)}) custom-call(f32[2,16,16,128]{3,2,1,0:T(8,128)S(1)} %copy-done.1, f32[2,16,16,128]{3,2,1,0:T(8,128)S(1)} %collective-permute-done.other_ref, f32[16,16,128]{2,1,0:T(8,128)S(1)} %copy-done.3, f32[16,16,128]{2,1,0:T(8,128)S(1)} %copy-done.5, f32[16,16,128]{2,1,0:T(8,128)S(1)} %copy-done.7, ...), custom_call_target="tpu_custom_call" | custom-call | flops 50000000 | bytes 4423680 | tf_op jit(solution)/shard_map/main/pallas_call | solution.py:543
  39.6 28.3 %all_to_all.5 = f32[256,1,128]{2,1,0:T(1,128)S(1)} all-to-all(f32[256,1,128]{2,1,0:T(1,128)S(1)} %bitcast.5), channel_id=1, replica_groups=mesh['section'=2,'sx'=16,'sy'=8] {'section','sx','sy'}, dimensions={0} | all-to-all | bytes 262144 | tf_op jit(solution)/shard_map/all_to_all | solution.py:590
  67.9 0.7 send.1
  68.6 0.6 collective-permute-start.6
  69.2 0.2 mine.1.mine_ref
  69.4 5.3 %collective-permute-done.6.other_ref = f32[16,16,128]{2,1,0:T(8,128)S(1)} collective-permute-done((f32[16,16,128]{2,1,0:T(8,128)S(1)}, f32[16,16,128]{2,1,0:T(8,128)S(1)}, u32[]{:S(2)}, u32[]{:S(2)}) %collective-permute-start.6) | collective-permute-done | bytes 131104 | tf_op jit(solution)/shard_map/ppermute | solution.py:592
  74.7 0.8 %join.1 = f32[2,16,16,128]{3,2,1,0:T(8,128)} custom-call(f32[2,16,16,128]{3,2,1,0:T(8,128)S(1)} %mine.1.mine_ref, f32[16,16,128]{2,1,0:T(8,128)S(1)} %collective-permute-done.6.other_ref), custom_call_target="tpu_custom_call" | custom-call | flops 1000000 | bytes 655360 | tf_op jit(solution)/shard_map/join/pallas_call | solution.py:543
  (14 shorter events, 0.3 us)
Async XLA Ops:
  0.0 9.0 %collective-permute-start = (f32[2,16,16,128]{3,2,1,0:T(8,128)}, f32[2,16,16,128]{3,2,1,0:T(8,128)S(1)}, u32[]{:S(2)}, u32[]{:S(2)}) collective-permute-start(f32[2,16,16,128]{3,2,1,0:T(8,128)} %own_ref.5), channel_id=1, source_target_pairs={{0,128},{128,0},{1,129},{129,1},{2,130},{130,2},{3,131},{131,3},{4... | collective-permute-start | bytes 786440 | tf_op jit(solution)/shard_map/ppermute | solution.py:567
  3.7 1.0 %copy-start = (f32[2,16,16,128]{3,2,1,0:T(8,128)S(1)}, f32[2,16,16,128]{3,2,1,0:T(8,128)}, u32[]{:S(2)}) copy-start(f32[2,16,16,128]{3,2,1,0:T(8,128)} %own_ref.5) | copy-start | bytes 786436
  4.7 0.9 %copy-start.2 = (f32[16,16,128]{2,1,0:T(8,128)S(1)}, f32[16,16,128]{2,1,0:T(8,128)}, u32[]{:S(2)}) copy-start(f32[16,16,128]{2,1,0:T(8,128)} %prev_ref.3) | copy-start | bytes 393220
  5.6 0.9 %copy-start.4 = (f32[16,16,128]{2,1,0:T(8,128)S(1)}, f32[16,16,128]{2,1,0:T(8,128)}, u32[]{:S(2)}) copy-start(f32[16,16,128]{2,1,0:T(8,128)} %diff_ref.3) | copy-start | bytes 393220
  6.5 0.9 %copy-start.6 = (f32[16,16,128]{2,1,0:T(8,128)S(1)}, f32[16,16,128]{2,1,0:T(8,128)}, u32[]{:S(2)}) copy-start(f32[16,16,128]{2,1,0:T(8,128)} %react_ref.3) | copy-start | bytes 393220
  9.2 9.2 %collective-permute-start.1 = (f32[8,16,128]{2,1,0:T(8,128)S(1)}, f32[8,16,128]{2,1,0:T(8,128)S(1)}, u32[]{:S(2)}, u32[]{:S(2)}) collective-permute-start(f32[8,16,128]{2,1,0:T(8,128)S(1)} %get-tuple-element.16), channel_id=1, source_target_pairs={{0,1},{1,0},{2,3},{3,2},{4,5},{5,4},{6,7},{7,6},{129,130},{130,129... | collective-permute-start | bytes 196616 | tf_op jit(solution)/shard_map/ppermute | solution.py:576
  13.0 8.1 %collective-permute-start.2 = (f32[48,16,128]{2,1,0:T(8,128)S(1)}, f32[48,16,128]{2,1,0:T(8,128)S(1)}, u32[]{:S(2)}, u32[]{:S(2)}) collective-permute-start(f32[48,16,128]{2,1,0:T(8,128)S(1)} %get-tuple-element.17), channel_id=1, source_target_pairs={{0,8},{8,0},{16,24},{24,16},{32,40},{40,32},{48,56},{56,48},{64,72... | collective-permute-start | bytes 1179656 | tf_op jit(solution)/shard_map/ppermute | solution.py:572
  14.9 9.1 %collective-permute-start.3 = (f32[48,16,128]{2,1,0:T(8,128)S(1)}, f32[48,16,128]{2,1,0:T(8,128)S(1)}, u32[]{:S(2)}, u32[]{:S(2)}) collective-permute-start(f32[48,16,128]{2,1,0:T(8,128)S(1)} %get-tuple-element.18), channel_id=1, source_target_pairs={{8,16},{16,8},{24,32},{32,24},{40,48},{48,40},{56,64},{64,56},{72,... | collective-permute-start | bytes 1179656 | tf_op jit(solution)/shard_map/ppermute | solution.py:571
  18.4 7.9 %collective-permute-start.5 = (f32[26,16,128]{2,1,0:T(8,128)S(1)}, f32[26,16,128]{2,1,0:T(8,128)S(1)}, u32[]{:S(2)}, u32[]{:S(2)}) collective-permute-start(f32[26,16,128]{2,1,0:T(8,128)S(1)} %get-tuple-element.25), channel_id=1, source_target_pairs={{8,16},{16,8},{24,32},{32,24},{40,48},{48,40},{56,64},{64,56},{72,... | collective-permute-start | bytes 638984 | tf_op jit(solution)/shard_map/ppermute | solution.py:579
  21.0 5.3 %collective-permute-start.4 = (f32[26,16,128]{2,1,0:T(8,128)S(1)}, f32[26,16,128]{2,1,0:T(8,128)S(1)}, u32[]{:S(2)}, u32[]{:S(2)}) collective-permute-start(f32[26,16,128]{2,1,0:T(8,128)S(1)} %get-tuple-element.26), channel_id=1, source_target_pairs={{0,8},{8,0},{16,24},{24,16},{32,40},{40,32},{48,56},{56,48},{64,72... | collective-permute-start | bytes 638984 | tf_op jit(solution)/shard_map/ppermute | solution.py:580
  26.3 1.0 %copy-start.1 = (f32[2,16,16,128]{3,2,1,0:T(8,128)S(1)}, f32[2,16,16,128]{3,2,1,0:T(8,128)}, u32[]{:S(2)}) copy-start(f32[2,16,16,128]{3,2,1,0:T(8,128)} %own_ref.5) | copy-start | bytes 786436
  27.2 0.9 %copy-start.3 = (f32[16,16,128]{2,1,0:T(8,128)S(1)}, f32[16,16,128]{2,1,0:T(8,128)}, u32[]{:S(2)}) copy-start(f32[16,16,128]{2,1,0:T(8,128)} %prev_ref.3) | copy-start | bytes 393220
  28.1 0.9 %copy-start.5 = (f32[16,16,128]{2,1,0:T(8,128)S(1)}, f32[16,16,128]{2,1,0:T(8,128)}, u32[]{:S(2)}) copy-start(f32[16,16,128]{2,1,0:T(8,128)} %diff_ref.3) | copy-start | bytes 393220
  29.0 0.9 %copy-start.7 = (f32[16,16,128]{2,1,0:T(8,128)S(1)}, f32[16,16,128]{2,1,0:T(8,128)}, u32[]{:S(2)}) copy-start(f32[16,16,128]{2,1,0:T(8,128)} %react_ref.3) | copy-start | bytes 393220
  68.6 6.1 %collective-permute-start.6 = (f32[16,16,128]{2,1,0:T(8,128)S(1)}, f32[16,16,128]{2,1,0:T(8,128)S(1)}, u32[]{:S(2)}, u32[]{:S(2)}) collective-permute-start(f32[16,16,128]{2,1,0:T(8,128)S(1)} %get-tuple-element.24), channel_id=1, source_target_pairs={{0,128},{128,0},{1,129},{129,1},{2,130},{130,2},{3,131},{131,3},{4... | collective-permute-start | bytes 393224 | tf_op jit(solution)/shard_map/ppermute | solution.py:592

commit v7 on v6

--- a/solution.py
+++ b/solution.py
@@ -178,7 +178,7 @@
 
 
 def left_half():
-    return lax.rem(lax.axis_index("section") + lax.axis_index("sy"), 2) == 1
+    return lax.axis_index("section") == 0
 
 
 def half_mask(rows):
@@ -192,10 +192,6 @@
 
 def border_start():
     return jnp.where(left_half(), LANES - EDGE, 0)
-
-
-def leaving_start():
-    return jnp.where(left_half(), 0, LANES - EDGE)
 
 
 def on_even_row():
@@ -208,48 +204,54 @@
     return z * OWN_PARTS + entry, row, z * OWN_PARTS + last, ninth
 
 
-def other_place(slot, z, nz):
-    return z, 8 * slot, nz + z // 8, 2 * lax.rem(z, 8) + slot
-
-
-def pack(border_ref, near_ref, far_ref, load, fields, place, partial):
-    nz = 2 * border_ref.shape[0]
-    nx = border_ref.shape[1]
+def pack_rows(near_ref, far_ref, cell, place, even):
+    nx = cell.shape[0]
+    entry, row, last, ninth = place
+    near_ref[entry, row : row + 8] = jnp.where(even, cell[nx - 8 : nx], cell[0:8])
+    far_ref[entry, row : row + 8] = jnp.where(even, cell[0:8], cell[nx - 8 : nx])
+    near_ref[last, ninth : ninth + 1] = jnp.where(even, cell[nx - 9 : nx - 8], cell[8:9])
+    far_ref[last, ninth : ninth + 1] = jnp.where(even, cell[8:9], cell[nx - 9 : nx - 8])
+
+
+def own_kernel(own_ref, prev_ref, diff_ref, react_ref, held_ref, same_ref, cross_ref, near_ref, far_ref):
+    nz, nx = prev_ref.shape[0], prev_ref.shape[1]
     lanes = lane_ids(nx)
-    start = leaving_start()
     even = on_even_row()
+    incoming = border_start()
+    outgoing = LANES - EDGE - incoming
+
+    def put(tile, cell, at, start):
+        moved = pltpu.roll(cell, lax.rem(at + LANES - start, LANES), 1)
+        return jnp.where((lanes >= at) & (lanes < at + EDGE), moved, tile)
 
     for plane in range(nz // 2):
-        tile = partial(plane)
+        same = jnp.zeros((nx, LANES), jnp.float32)
+        cross = same
         for part in range(2):
             z = part * (nz // 2) + plane
-            for slot, f in enumerate(fields):
-                cell = load(f, z)
-                at = part * 64 + f * EDGE
-                moved = pltpu.roll(cell, lax.rem(at + LANES - start, LANES), 1)
-                tile = jnp.where((lanes >= at) & (lanes < at + EDGE), moved, tile)
-                entry, row, last, ninth = place(slot, z)
-                near_ref[entry, row : row + 8] = jnp.where(even, cell[nx - 8 : nx], cell[0:8])
-                far_ref[entry, row : row + 8] = jnp.where(even, cell[0:8], cell[nx - 8 : nx])
-                near_ref[last, ninth : ninth + 1] = jnp.where(even, cell[nx - 9 : nx - 8], cell[8:9])
-                far_ref[last, ninth : ninth + 1] = jnp.where(even, cell[8:9], cell[nx - 9 : nx - 8])
-        border_ref[plane] = tile
-
-
-def own_kernel(own_ref, prev_ref, diff_ref, react_ref, border_ref, near_ref, far_ref):
-    nx = prev_ref.shape[1]
-    refs = {4: prev_ref, 5: diff_ref, 6: react_ref}
-    load = lambda f, z: own_ref[f, z] if f < 2 else refs[f][z]
-    pack(border_ref, near_ref, far_ref, load, ORDER[:5], own_place, lambda plane: jnp.zeros((nx, LANES), jnp.float32))
-
-
-def other_kernel(other_ref, own_border_ref, border_ref, near_ref, far_ref):
+            cells = [own_ref[0, z], own_ref[1, z], prev_ref[z], diff_ref[z], react_ref[z]]
+            for slot, cell in enumerate(cells):
+                held_ref[slot, z] = cell
+                same = put(same, cell, part * 64 + ORDER[slot] * EDGE, incoming)
+                if slot < 2:
+                    cross = put(cross, cell, part * 64 + (2 + slot) * EDGE, outgoing)
+                pack_rows(near_ref, far_ref, cell, own_place(slot, z), even)
+        same_ref[plane] = same
+        cross_ref[plane] = cross
+
+
+def other_kernel(other_ref, same_ref, cross_ref, border_ref, near_ref, far_ref):
     nz = other_ref.shape[1]
-
-    def place(slot, z):
-        return z, 8 * slot, nz + z // 8, 2 * (z % 8) + slot
-
-    pack(border_ref, near_ref, far_ref, lambda f, z: other_ref[f - 2, z], ORDER[5:], place, lambda plane: own_border_ref[plane])
+    even = on_even_row()
+    rest = nz + nz // 8
+    for z in range(nz):
+        for slot in range(2):
+            pack_rows(near_ref, far_ref, other_ref[slot, z], (z, 8 * slot, nz + z // 8, 2 * (z % 8) + slot), even)
+    for plane in range(nz // 2):
+        border = same_ref[plane] + cross_ref[plane]
+        border_ref[plane] = border
+        near_ref[rest + plane] = border
+        far_ref[rest + plane] = border
 
 
 ROWS = 48
@@ -269,10 +271,10 @@
     lax.fori_loop(0, count // unroll, group, 0)
 
 
-def main_kernel(consts, own_ref, other_ref, prev_ref, diff_ref, react_ref, border_ref, own_near_ref, own_far_ref, near_ref, far_ref, part_ref, sums_ref,
+def main_kernel(consts, held_ref, other_ref, border_ref, own_near_ref, own_far_ref, near_ref, far_ref, part_ref, sums_ref,
                 val, kap, frozen, prv, rea, dif, fx, fy, fz, alpha, beta, vec, ya, yb, table):
     eigen_basis, basis_inverse, shift_rows, pairs = consts
-    nz, nx = prev_ref.shape[0], prev_ref.shape[1]
+    nz, nx = held_ref.shape[1], held_ref.shape[2]
     section = lax.axis_index("section")
     zero_plane = jnp.zeros((ROWS, LANES), jnp.float32)
     zero_rows = jnp.zeros((FIRST, LANES), jnp.float32)
@@ -303,8 +305,8 @@
 
             def column(f):
                 slot = ORDER.index(f)
-                mid = (own_ref[0, z], own_ref[1, z], prev_ref[z], diff_ref[z], react_ref[z], other_ref[0, z], other_ref[1, z])[slot]
-                entry, row, last, ninth = own_place(slot, z) if slot < 5 else other_place(slot - 5, z, nz)
+                mid = held_ref[slot, z] if slot < 5 else other_ref[slot - 5, z]
+                entry, row, last, ninth = own_place(slot, z) if slot < 5 else (z, 8 * (slot - 5), nz + z // 8, 2 * lax.rem(z, 8) + slot - 5)
                 low, high = both(slot, entry, row, 8)
                 low_end, high_end = both(slot, last, ninth, 1)
                 cells = jnp.concatenate([tile(low_end), low, mid, high, tile(high_end)], 0)
@@ -558,6 +560,17 @@
     return [pair for i in range(start, count - 1, 2) for pair in ((i, i + 1), (i + 1, i))]
 
 
+def beside(count, cross):
+    pairs = []
+    for s in range(2):
+        to = 1 - s if cross else s
+        step = 1 if to == 0 else -1
+        for i in range(count):
+            if 0 <= i + step < count:
+                pairs.append((s * count + i, to * count + i + step))
+    return pairs
+
+
 def body(previous, sections, diffusivity, reaction):
     consts = constants()
     nz, nx, ny = previous.shape
@@ -565,17 +578,15 @@
     axes = ("section", "sx", "sy")
     partner = [(0, 1), (1, 0)]
     other = lax.ppermute(sections, "section", partner)
-    edge, rest = (nz // 2, nx, ny), nz + nz // 8
-    own = (nz * OWN_PARTS, TALL, ny)
-    border, own_near, own_far = call(own_kernel, [edge, own, own], name="own")(sections, previous, diffusivity, reaction)
+    edge, own, late = (nz // 2, nx, ny), (nz * OWN_PARTS, TALL, ny), (nz + nz // 8 + nz // 2, TALL, ny)
+    held, same, cross, own_near, own_far = call(own_kernel, [(5, nz, nx, ny), edge, edge, own, own], name="own")(
+        sections, previous, diffusivity, reaction
+    )
+    same = lax.ppermute(same, ("section", "sy"), beside(columns, False))
+    cross = lax.ppermute(cross, ("section", "sy"), beside(columns, True))
     own_far = lax.ppermute(own_far, "sx", swaps(rows, 1))
     own_near = lax.ppermute(own_near, "sx", swaps(rows, 0))
-    late = (rest + nz // 2, TALL, ny)
-    border, near, far = call(other_kernel, [edge, late, late], name="other")(other, border)
-    edges = [(s * columns + a, s * columns + b) for s in range(2) for a, b in swaps(columns, s)]
-    border = lax.ppermute(border, ("section", "sy"), edges)
-    near = lax.dynamic_update_slice(near, border, (rest, 0, 0))
-    far = lax.dynamic_update_slice(far, border, (rest, 0, 0))
+    border, near, far = call(other_kernel, [edge, late, late], name="other")(other, same, cross)
     far = lax.ppermute(far, "sx", swaps(rows, 1))
     near = lax.ppermute(near, "sx", swaps(rows, 0))
     peers = 2 * columns * rows
@@ -586,11 +597,11 @@
     ]
     part, sums = call(
         functools.partial(main_kernel, consts), [(peers, LANES), (ITERS, 4, nz, nx, ny)], scratch, 50_000_000, "main", 26
-    )(sections, other, previous, diffusivity, reaction, border, own_near, own_far, near, far)
+    )(held, other, border, own_near, own_far, near, far)
     total = lax.all_to_all(part.reshape(peers, 1, LANES), axes, 0, 0).reshape(peers, LANES)
     half, weight = call(functools.partial(send_kernel, consts), [previous.shape, (2 * ITERS, LANES)], name="send")(total, sums, other)
     got = lax.ppermute(half, "section", partner)
-    mine = call(functools.partial(mine_kernel, consts), sections.shape, name="mine")(weight, sums, sections)
+    mine = call(functools.partial(mine_kernel, consts), sections.shape, name="mine")(weight, sums, held)
     return call(join_kernel, sections.shape, name="join")(mine, got)
 
 

time: 75.8 us -> 73.3 us (0.967)
  local copies, waits for them, and re-layouts: 7.37 us -> 3.69 us
  blocking collectives: 28.3 us -> 31.5 us
  waiting for transfers between devices: 11.7 us -> 9.4 us
    unnamed x16 -> x8, local copies, waits for them, and re-layouts: 7.36 us -> 3.69 us
    all_to_all x1, blocking collectives: 28.3 us -> 31.5 us  [body(): lax.all_to_all(part.reshape(peers, 1, LANES), axes, 0, 0)]
    ppermute x1, waiting for transfers between devices: 2.86 us -> 0.01 us  [body(): own_far = lax.ppermute(own_far, 'sx', swaps(rows, 1))]
    ppermute x1, waiting for transfers between devices: 1.32 us -> 0.01 us  [body(): other = lax.ppermute(sections, 'section', partner)]
    ppermute x1, starting transfers between devices: 2.63 us -> 3.92 us  [body(): far = lax.ppermute(far, 'sx', swaps(rows, 1))]
    ppermute x1, waiting for transfers between devices: 2.28 us -> 3.48 us  [body(): far = lax.ppermute(far, 'sx', swaps(rows, 1))]
    ppermute x1, starting transfers between devices: 1.91 us -> 1.04 us  [body(): own_near = lax.ppermute(own_near, 'sx', swaps(rows, 0))]
    ppermute x1 -> x2, starting transfers between devices: 3.8 us -> 3.78 us  [the longest x1 3.12 us: body(): same = lax.ppermute(same, ('section', 'sy'), beside(columns, False))]
  transfers between devices with their start and end apart: 7 -> 8, of which waited for: 4 -> 3; matrix products, arithmetic and copies ran while one was open for 0% -> 0% of each run, Pallas kernels for 1% -> 1%
where the time goes in v7:
time: 73.3 us; the launch traced here: 73 us
  blocking collectives  31.5 us (43%)
  starting transfers between devices  16.6 us (23%)
  Pallas kernels  11.7 us (16%)
  waiting for transfers between devices  9.4 us (13%)
  local copies, waits for them, and re-layouts  3.69 us (5%)
    all_to_all x1, blocking collectives, body(): lax.all_to_all(part.reshape(peers, 1, LANES), axes, 0, 0)  31.5 us
    pallas_call x6, Pallas kernels, run(): pl.pallas_call(kernel, out_shape=shapes if many else shapes[0], in_specs=...  11.7 us
    ppermute x1, waiting for transfers between devices, body(): got = lax.ppermute(half, 'section', partner)  5.27 us
    ppermute x1, starting transfers between devices, body(): far = lax.ppermute(far, 'sx', swaps(rows, 1))  3.92 us
    ppermute x1, starting transfers between devices, body(): other = lax.ppermute(sections, 'section', partner)  3.74 us
    unnamed x8, local copies, waits for them, and re-layouts  3.69 us
    ppermute x1, waiting for transfers between devices, body(): far = lax.ppermute(far, 'sx', swaps(rows, 1))  3.48 us
    ppermute x1, starting transfers between devices, body(): own_far = lax.ppermute(own_far, 'sx', swaps(rows, 1))  3.44 us
  transfers between devices with their start and end apart: 8, of which 3 were waited for; matrix products, arithmetic and copies ran while one was open for 0% of the time, Pallas kernels for 1%

profile of v7, /device:TPU:1, one launch (start us, length us, event | category | flops | bytes accessed | tf_op | source)
XLA Modules:
  0.0 73.0 jit_solution(3369522462106611559)
XLA Ops:
  0.0 3.7 %collective-permute-start = (f32[2,16,16,128]{3,2,1,0:T(8,128)}, f32[2,16,16,128]{3,2,1,0:T(8,128)S(1)}, u32[]{:S(2)}, u32[]{:S(2)}) collective-permute-start(f32[2,16,16,128]{3,2,1,0:T(8,128)} %own_ref.1), channel_id=1, source_target_pairs={{0,128},{128,0},{1,129},{129,1},{2,130},{130,2},{3,131},{131,3},{4... | collective-permute-start | bytes 786440 | tf_op jit(solution)/shard_map/ppermute | solution.py:580
  3.7 1.0 %copy-done = f32[2,16,16,128]{3,2,1,0:T(8,128)S(1)} copy-done((f32[2,16,16,128]{3,2,1,0:T(8,128)S(1)}, f32[2,16,16,128]{3,2,1,0:T(8,128)}, u32[]{:S(2)}) %copy-start) | copy-done | bytes 262168
  4.7 0.9 %copy-done.1 = f32[16,16,128]{2,1,0:T(8,128)S(1)} copy-done((f32[16,16,128]{2,1,0:T(8,128)S(1)}, f32[16,16,128]{2,1,0:T(8,128)}, u32[]{:S(2)}) %copy-start.1) | copy-done | bytes 131096
  5.6 0.9 %copy-done.2 = f32[16,16,128]{2,1,0:T(8,128)S(1)} copy-done((f32[16,16,128]{2,1,0:T(8,128)S(1)}, f32[16,16,128]{2,1,0:T(8,128)}, u32[]{:S(2)}) %copy-start.2) | copy-done | bytes 131096
  6.5 0.9 %copy-done.3 = f32[16,16,128]{2,1,0:T(8,128)S(1)} copy-done((f32[16,16,128]{2,1,0:T(8,128)S(1)}, f32[16,16,128]{2,1,0:T(8,128)}, u32[]{:S(2)}) %copy-start.3) | copy-done | bytes 131096
  7.4 0.3 own.1
  7.8 1.0 %collective-permute-start.3 = (f32[48,16,128]{2,1,0:T(8,128)S(1)}, f32[48,16,128]{2,1,0:T(8,128)S(1)}, u32[]{:S(2)}, u32[]{:S(2)}) collective-permute-start(f32[48,16,128]{2,1,0:T(8,128)S(1)} %get-tuple-element.21), channel_id=1, source_target_pairs={{0,8},{8,0},{16,24},{24,16},{32,40},{40,32},{48,56},{56,48},{64,72... | collective-permute-start | bytes 1179656 | tf_op jit(solution)/shard_map/ppermute | solution.py:588
  8.8 3.4 %collective-permute-start.4 = (f32[48,16,128]{2,1,0:T(8,128)S(1)}, f32[48,16,128]{2,1,0:T(8,128)S(1)}, u32[]{:S(2)}, u32[]{:S(2)}) collective-permute-start(f32[48,16,128]{2,1,0:T(8,128)S(1)} %get-tuple-element.22), channel_id=1, source_target_pairs={{8,16},{16,8},{24,32},{32,24},{40,48},{48,40},{56,64},{64,56},{72,... | collective-permute-start | bytes 1179656 | tf_op jit(solution)/shard_map/ppermute | solution.py:587
  12.3 3.1 %collective-permute-start.1 = (f32[8,16,128]{2,1,0:T(8,128)S(1)}, f32[8,16,128]{2,1,0:T(8,128)S(1)}, u32[]{:S(2)}, u32[]{:S(2)}) collective-permute-start(f32[8,16,128]{2,1,0:T(8,128)S(1)} %get-tuple-element.18), channel_id=1, source_target_pairs={{0,1},{1,2},{2,3},{3,4},{4,5},{5,6},{6,7},{129,128},{130,129},{131... | collective-permute-start | bytes 196616 | tf_op jit(solution)/shard_map/ppermute | solution.py:585
  15.4 0.7 collective-permute-start.2
  16.1 0.6 collective-permute-done.1.same_ref
  16.7 0.1 other.1
  16.8 0.1 collective-permute-start.5
  16.9 3.9 %collective-permute-start.6 = (f32[26,16,128]{2,1,0:T(8,128)S(1)}, f32[26,16,128]{2,1,0:T(8,128)S(1)}, u32[]{:S(2)}, u32[]{:S(2)}) collective-permute-start(f32[26,16,128]{2,1,0:T(8,128)S(1)} %get-tuple-element.24), channel_id=1, source_target_pairs={{8,16},{16,8},{24,32},{32,24},{40,48},{48,40},{56,64},{64,56},{72,... | collective-permute-start | bytes 638984 | tf_op jit(solution)/shard_map/ppermute | solution.py:590
  20.8 0.0 collective-permute-done.4.own_far_ref
  20.8 0.0 collective-permute-done.5.near_ref
  20.8 3.5 %collective-permute-done.6.far_ref = f32[26,16,128]{2,1,0:T(8,128)S(1)} collective-permute-done((f32[26,16,128]{2,1,0:T(8,128)S(1)}, f32[26,16,128]{2,1,0:T(8,128)S(1)}, u32[]{:S(2)}, u32[]{:S(2)}) %collective-permute-start.6) | collective-permute-done | bytes 213024 | tf_op jit(solution)/shard_map/ppermute | solution.py:590
  24.3 9.6 %main.1 = (f32[256,128]{1,0:T(8,128)S(1)}, f32[4,4,16,16,128]{4,3,2,1,0:T(8,128)S(1)}) custom-call(f32[5,16,16,128]{3,2,1,0:T(8,128)S(1)} %get-tuple-element.17.held_ref.own_ref, f32[2,16,16,128]{3,2,1,0:T(8,128)S(1)} %collective-permute-done.other_ref, f32[8,16,128]{2,1,0:T(8,128)S(1)} %get-tuple-element.20.border_ref, ...), custom_call_target="tpu_custom_call" | custom-call | flops 50000000 | bytes 4423680 | tf_op jit(solution)/shard_map/main/pallas_call | solution.py:545
  34.0 31.5 %all_to_all.5 = f32[256,1,128]{2,1,0:T(1,128)S(1)} all-to-all(f32[256,1,128]{2,1,0:T(1,128)S(1)} %bitcast.5), channel_id=1, replica_groups=mesh['section'=2,'sx'=16,'sy'=8] {'section','sx','sy'}, dimensions={0} | all-to-all | bytes 262144 | tf_op jit(solution)/shard_map/all_to_all | solution.py:601
  65.4 0.7 send.1
  66.1 0.6 collective-permute-start.7
  66.7 0.2 mine.1.mine_ref
  66.9 5.3 %collective-permute-done.7.other_ref = f32[16,16,128]{2,1,0:T(8,128)S(1)} collective-permute-done((f32[16,16,128]{2,1,0:T(8,128)S(1)}, f32[16,16,128]{2,1,0:T(8,128)S(1)}, u32[]{:S(2)}, u32[]{:S(2)}) %collective-permute-start.7) | collective-permute-done | bytes 131104 | tf_op jit(solution)/shard_map/ppermute | solution.py:603
  72.2 0.8 %join.1 = f32[2,16,16,128]{3,2,1,0:T(8,128)} custom-call(f32[2,16,16,128]{3,2,1,0:T(8,128)S(1)} %mine.1.mine_ref, f32[16,16,128]{2,1,0:T(8,128)S(1)} %collective-permute-done.7.other_ref), custom_call_target="tpu_custom_call" | custom-call | flops 1000000 | bytes 655360 | tf_op jit(solution)/shard_map/join/pallas_call | solution.py:545
  (7 shorter events, 0.0 us)
Async XLA Ops:
  0.0 16.7 %collective-permute-start = (f32[2,16,16,128]{3,2,1,0:T(8,128)}, f32[2,16,16,128]{3,2,1,0:T(8,128)S(1)}, u32[]{:S(2)}, u32[]{:S(2)}) collective-permute-start(f32[2,16,16,128]{3,2,1,0:T(8,128)} %own_ref.1), channel_id=1, source_target_pairs={{0,128},{128,0},{1,129},{129,1},{2,130},{130,2},{3,131},{131,3},{4... | collective-permute-start | bytes 786440 | tf_op jit(solution)/shard_map/ppermute | solution.py:580
  3.7 1.0 %copy-start = (f32[2,16,16,128]{3,2,1,0:T(8,128)S(1)}, f32[2,16,16,128]{3,2,1,0:T(8,128)}, u32[]{:S(2)}) copy-start(f32[2,16,16,128]{3,2,1,0:T(8,128)} %own_ref.1) | copy-start | bytes 786436
  4.7 0.9 %copy-start.1 = (f32[16,16,128]{2,1,0:T(8,128)S(1)}, f32[16,16,128]{2,1,0:T(8,128)}, u32[]{:S(2)}) copy-start(f32[16,16,128]{2,1,0:T(8,128)} %prev_ref.1) | copy-start | bytes 393220
  5.6 0.9 %copy-start.2 = (f32[16,16,128]{2,1,0:T(8,128)S(1)}, f32[16,16,128]{2,1,0:T(8,128)}, u32[]{:S(2)}) copy-start(f32[16,16,128]{2,1,0:T(8,128)} %diff_ref.1) | copy-start | bytes 393220
  6.5 0.9 %copy-start.3 = (f32[16,16,128]{2,1,0:T(8,128)S(1)}, f32[16,16,128]{2,1,0:T(8,128)}, u32[]{:S(2)}) copy-start(f32[16,16,128]{2,1,0:T(8,128)} %react_ref.1) | copy-start | bytes 393220
  7.8 13.0 %collective-permute-start.3 = (f32[48,16,128]{2,1,0:T(8,128)S(1)}, f32[48,16,128]{2,1,0:T(8,128)S(1)}, u32[]{:S(2)}, u32[]{:S(2)}) collective-permute-start(f32[48,16,128]{2,1,0:T(8,128)S(1)} %get-tuple-element.21), channel_id=1, source_target_pairs={{0,8},{8,0},{16,24},{24,16},{32,40},{40,32},{48,56},{56,48},{64,72... | collective-permute-start | bytes 1179656 | tf_op jit(solution)/shard_map/ppermute | solution.py:588
  8.8 12.0 %collective-permute-start.4 = (f32[48,16,128]{2,1,0:T(8,128)S(1)}, f32[48,16,128]{2,1,0:T(8,128)S(1)}, u32[]{:S(2)}, u32[]{:S(2)}) collective-permute-start(f32[48,16,128]{2,1,0:T(8,128)S(1)} %get-tuple-element.22), channel_id=1, source_target_pairs={{8,16},{16,8},{24,32},{32,24},{40,48},{48,40},{56,64},{64,56},{72,... | collective-permute-start | bytes 1179656 | tf_op jit(solution)/shard_map/ppermute | solution.py:587
  12.3 4.4 %collective-permute-start.1 = (f32[8,16,128]{2,1,0:T(8,128)S(1)}, f32[8,16,128]{2,1,0:T(8,128)S(1)}, u32[]{:S(2)}, u32[]{:S(2)}) collective-permute-start(f32[8,16,128]{2,1,0:T(8,128)S(1)} %get-tuple-element.18), channel_id=1, source_target_pairs={{0,1},{1,2},{2,3},{3,4},{4,5},{5,6},{6,7},{129,128},{130,129},{131... | collective-permute-start | bytes 196616 | tf_op jit(solution)/shard_map/ppermute | solution.py:585
  15.4 1.3 %collective-permute-start.2 = (f32[8,16,128]{2,1,0:T(8,128)S(1)}, f32[8,16,128]{2,1,0:T(8,128)S(1)}, u32[]{:S(2)}, u32[]{:S(2)}) collective-permute-start(f32[8,16,128]{2,1,0:T(8,128)S(1)} %get-tuple-element.19), channel_id=1, source_target_pairs={{1,128},{2,129},{3,130},{4,131},{5,132},{6,133},{7,134},{128,1},{1... | collective-permute-start | bytes 196616 | tf_op jit(solution)/shard_map/ppermute | solution.py:586
  16.8 4.0 %collective-permute-start.5 = (f32[26,16,128]{2,1,0:T(8,128)S(1)}, f32[26,16,128]{2,1,0:T(8,128)S(1)}, u32[]{:S(2)}, u32[]{:S(2)}) collective-permute-start(f32[26,16,128]{2,1,0:T(8,128)S(1)} %get-tuple-element.23), channel_id=1, source_target_pairs={{0,8},{8,0},{16,24},{24,16},{32,40},{40,32},{48,56},{56,48},{64,72... | collective-permute-start | bytes 638984 | tf_op jit(solution)/shard_map/ppermute | solution.py:591
  16.9 7.4 %collective-permute-start.6 = (f32[26,16,128]{2,1,0:T(8,128)S(1)}, f32[26,16,128]{2,1,0:T(8,128)S(1)}, u32[]{:S(2)}, u32[]{:S(2)}) collective-permute-start(f32[26,16,128]{2,1,0:T(8,128)S(1)} %get-tuple-element.24), channel_id=1, source_target_pairs={{8,16},{16,8},{24,32},{32,24},{40,48},{48,40},{56,64},{64,56},{72,... | collective-permute-start | bytes 638984 | tf_op jit(solution)/shard_map/ppermute | solution.py:590
  66.1 6.1 %collective-permute-start.7 = (f32[16,16,128]{2,1,0:T(8,128)S(1)}, f32[16,16,128]{2,1,0:T(8,128)S(1)}, u32[]{:S(2)}, u32[]{:S(2)}) collective-permute-start(f32[16,16,128]{2,1,0:T(8,128)S(1)} %get-tuple-element.28), channel_id=1, source_target_pairs={{0,128},{128,0},{1,129},{129,1},{2,130},{130,2},{3,131},{131,3},{4... | collective-permute-start | bytes 393224 | tf_op jit(solution)/shard_map/ppermute | solution.py:603

commit v8 on v7

--- a/solution.py
+++ b/solution.py
@@ -187,7 +187,7 @@
 
 ORDER = (0, 1, 4, 5, 6, 2, 3)
 TALL = 16
-OWN_PARTS = 3
+PARTS = 4
 
 
 def border_start():
@@ -198,25 +198,24 @@
     return lax.rem(lax.axis_index("sx"), 2) == 0
 
 
-def own_place(slot, z):
+def place(slot, z):
     entry, row = divmod(8 * slot, TALL)
-    last, ninth = divmod(40 + slot, TALL)
-    return z * OWN_PARTS + entry, row, z * OWN_PARTS + last, ninth
-
-
-def pack_rows(near_ref, far_ref, cell, place, even):
+    last, ninth = divmod(56 + slot, TALL)
+    return z * PARTS + entry, row, z * PARTS + last, ninth
+
+
+def pack_rows(near_ref, far_ref, cell, slot, z, even):
     nx = cell.shape[0]
-    entry, row, last, ninth = place
+    entry, row, last, ninth = place(slot, z)
     near_ref[entry, row : row + 8] = jnp.where(even, cell[nx - 8 : nx], cell[0:8])
     far_ref[entry, row : row + 8] = jnp.where(even, cell[0:8], cell[nx - 8 : nx])
     near_ref[last, ninth : ninth + 1] = jnp.where(even, cell[nx - 9 : nx - 8], cell[8:9])
     far_ref[last, ninth : ninth + 1] = jnp.where(even, cell[8:9], cell[nx - 9 : nx - 8])
 
 
-def own_kernel(own_ref, prev_ref, diff_ref, react_ref, held_ref, same_ref, cross_ref, near_ref, far_ref):
-    nz, nx = prev_ref.shape[0], prev_ref.shape[1]
+def own_kernel(held_ref, same_ref, cross_ref):
+    nz, nx = held_ref.shape[1], held_ref.shape[2]
     lanes = lane_ids(nx)
-    even = on_even_row()
     incoming = border_start()
     outgoing = LANES - EDGE - incoming
 
@@ -229,29 +228,26 @@
         cross = same
         for part in range(2):
             z = part * (nz // 2) + plane
-            cells = [own_ref[0, z], own_ref[1, z], prev_ref[z], diff_ref[z], react_ref[z]]
-            for slot, cell in enumerate(cells):
-                held_ref[slot, z] = cell
+            for slot in range(5):
+                cell = held_ref[slot, z]
                 same = put(same, cell, part * 64 + ORDER[slot] * EDGE, incoming)
                 if slot < 2:
                     cross = put(cross, cell, part * 64 + (2 + slot) * EDGE, outgoing)
-                pack_rows(near_ref, far_ref, cell, own_place(slot, z), even)
         same_ref[plane] = same
         cross_ref[plane] = cross
 
 
-def other_kernel(other_ref, same_ref, cross_ref, border_ref, near_ref, far_ref):
+def rows_kernel(held_ref, other_ref, same_ref, cross_ref, border_ref, near_ref, far_ref):
     nz = other_ref.shape[1]
     even = on_even_row()
-    rest = nz + nz // 8
     for z in range(nz):
-        for slot in range(2):
-            pack_rows(near_ref, far_ref, other_ref[slot, z], (z, 8 * slot, nz + z // 8, 2 * (z % 8) + slot), even)
+        for slot in range(7):
+            pack_rows(near_ref, far_ref, held_ref[slot, z] if slot < 5 else other_ref[slot - 5, z], slot, z, even)
     for plane in range(nz // 2):
         border = same_ref[plane] + cross_ref[plane]
         border_ref[plane] = border
-        near_ref[rest + plane] = border
-        far_ref[rest + plane] = border
+        near_ref[nz * PARTS + plane] = border
+        far_ref[nz * PARTS + plane] = border
 
 
 ROWS = 48
@@ -271,7 +267,7 @@
     lax.fori_loop(0, count // unroll, group, 0)
 
 
-def main_kernel(consts, held_ref, other_ref, border_ref, own_near_ref, own_far_ref, near_ref, far_ref, part_ref, sums_ref,
+def main_kernel(consts, held_ref, other_ref, border_ref, near_ref, far_ref, part_ref, sums_ref,
                 val, kap, frozen, prv, rea, dif, fx, fy, fz, alpha, beta, vec, ya, yb, table):
     eigen_basis, basis_inverse, shift_rows, pairs = consts
     nz, nx = held_ref.shape[1], held_ref.shape[2]
@@ -290,13 +286,12 @@
             for ref in (val, kap, ya, yb):
                 ref[f, at] = zero_plane
 
-    def both(slot, entry, row, count):
-        refs = (own_near_ref, own_far_ref) if slot < 5 else (near_ref, far_ref)
-        near, far = [ref[entry, pl.ds(row, count)] for ref in refs]
+    def both(entry, row, count):
+        near, far = near_ref[entry, row : row + count], far_ref[entry, row : row + count]
         return jnp.where(even, far, near), jnp.where(even, near, far)
 
     def assemble(plane):
-        at = nz + nz // 8 + plane
+        at = nz * PARTS + plane
         low = jnp.where(even, far_ref[at], near_ref[at])
         high = jnp.where(even, near_ref[at], far_ref[at])
         sides = jnp.concatenate([tile(low[nx - 9 : nx - 8]), low[nx - 8 : nx], border_ref[plane], high[0:8], tile(high[8:9])], 0)
@@ -306,9 +301,9 @@
             def column(f):
                 slot = ORDER.index(f)
                 mid = held_ref[slot, z] if slot < 5 else other_ref[slot - 5, z]
-                entry, row, last, ninth = own_place(slot, z) if slot < 5 else (z, 8 * (slot - 5), nz + z // 8, 2 * lax.rem(z, 8) + slot - 5)
-                low, high = both(slot, entry, row, 8)
-                low_end, high_end = both(slot, last, ninth, 1)
+                entry, row, last, ninth = place(slot, z)
+                low, high = both(entry, row, 8)
+                low_end, high_end = both(last, ninth, 1)
                 cells = jnp.concatenate([tile(low_end), low, mid, high, tile(high_end)], 0)
                 at = part * 64 + f * EDGE
                 return jnp.where(edge, pltpu.roll(sides, lax.rem(start + LANES - at, LANES), 1), cells)
@@ -548,7 +543,7 @@
             in_specs=[pl.BlockSpec(memory_space=pltpu.VMEM)] * len(args),
             out_specs=[pl.BlockSpec(memory_space=pltpu.VMEM)] * len(shapes) if many else pl.BlockSpec(memory_space=pltpu.VMEM),
             scratch_shapes=[pltpu.VMEM(s, jnp.float32) for s in scratch],
-            compiler_params=pltpu.CompilerParams(vmem_limit_bytes=limit * 1024 * 1024),
+            compiler_params=pltpu.CompilerParams(vmem_limit_bytes=int(limit * 1024 * 1024)),
             cost_estimate=pl.CostEstimate(flops=flops, bytes_accessed=moved, transcendentals=0),
             name=name,
         )(*args)
@@ -578,15 +573,12 @@
     axes = ("section", "sx", "sy")
     partner = [(0, 1), (1, 0)]
     other = lax.ppermute(sections, "section", partner)
-    edge, own, late = (nz // 2, nx, ny), (nz * OWN_PARTS, TALL, ny), (nz + nz // 8 + nz // 2, TALL, ny)
-    held, same, cross, own_near, own_far = call(own_kernel, [(5, nz, nx, ny), edge, edge, own, own], name="own")(
-        sections, previous, diffusivity, reaction
-    )
+    edge, line = (nz // 2, nx, ny), (nz * PARTS + nz // 2, TALL, ny)
+    held = jnp.concatenate([sections, previous[None], diffusivity[None], reaction[None]], 0)
+    same, cross = call(own_kernel, [edge, edge], name="own")(held)
     same = lax.ppermute(same, ("section", "sy"), beside(columns, False))
     cross = lax.ppermute(cross, ("section", "sy"), beside(columns, True))
-    own_far = lax.ppermute(own_far, "sx", swaps(rows, 1))
-    own_near = lax.ppermute(own_near, "sx", swaps(rows, 0))
-    border, near, far = call(other_kernel, [edge, late, late], name="other")(other, same, cross)
+    border, near, far = call(rows_kernel, [edge, line, line], name="rows")(held, other, same, cross)
     far = lax.ppermute(far, "sx", swaps(rows, 1))
     near = lax.ppermute(near, "sx", swaps(rows, 0))
     peers = 2 * columns * rows
@@ -597,7 +589,7 @@
     ]
     part, sums = call(
         functools.partial(main_kernel, consts), [(peers, LANES), (ITERS, 4, nz, nx, ny)], scratch, 50_000_000, "main", 26
-    )(held, other, border, own_near, own_far, near, far)
+    )(held, other, border, near, far)
     total = lax.all_to_all(part.reshape(peers, 1, LANES), axes, 0, 0).reshape(peers, LANES)
     half, weight = call(functools.partial(send_kernel, consts), [previous.shape, (2 * ITERS, LANES)], name="send")(total, sums, other)
     got = lax.ppermute(half, "section", partner)

time: 73.3 us -> 72.2 us (0.985)
  waiting for transfers between devices: 9.4 us -> 13.6 us
  local copies, waits for them, and re-layouts: 3.69 us -> 0 us
  starting transfers between devices: 16.6 us -> 13.5 us
  other arithmetic: 0 us -> 1.2 us
    ppermute x2 -> x0, starting transfers between devices: 4.49 us -> none  [the longest x1 3.44 us: body(): own_far = lax.ppermute(own_far, 'sx', swaps(rows, 1))]
    ppermute x1, waiting for transfers between devices: 3.48 us -> 7.73 us  [body(): far = lax.ppermute(far, 'sx', swaps(rows, 1))]
    unnamed x8 -> x0, local copies, waits for them, and re-layouts: 3.69 us -> none
    ppermute x1, starting transfers between devices: 0.09 us -> 1.9 us  [body(): near = lax.ppermute(near, 'sx', swaps(rows, 0))]
    concatenate x0 -> x1, other arithmetic: none -> 1.2 us  [body(): jnp.concatenate([sections, previous[None], diffusivity[None], reaction[No...]
  transfers between devices with their start and end apart: 8 -> 6, of which waited for: 3 -> 3; matrix products, arithmetic and copies ran while one was open for 0% -> 2% of each run, Pallas kernels for 1% -> 1%
where the time goes in v8:
time: 72.2 us; the launch traced here: 72 us
  blocking collectives  31.9 us (44%)
  waiting for transfers between devices  13.6 us (19%)
  starting transfers between devices  13.5 us (19%)
  Pallas kernels  11.8 us (16%)
  other arithmetic  1.2 us (2%)
    all_to_all x1, blocking collectives, body(): lax.all_to_all(part.reshape(peers, 1, LANES), axes, 0, 0)  31.9 us
    pallas_call x6, Pallas kernels, run(): pl.pallas_call(kernel, out_shape=shapes if many else shapes[0], in_specs=...  11.8 us
    ppermute x1, waiting for transfers between devices, body(): far = lax.ppermute(far, 'sx', swaps(rows, 1))  7.73 us
    ppermute x1, waiting for transfers between devices, body(): got = lax.ppermute(half, 'section', partner)  5.27 us
    ppermute x1, starting transfers between devices, body(): other = lax.ppermute(sections, 'section', partner)  3.74 us
    ppermute x1, starting transfers between devices, body(): far = lax.ppermute(far, 'sx', swaps(rows, 1))  3.44 us
    ppermute x1, starting transfers between devices, body(): same = lax.ppermute(same, ('section', 'sy'), beside(columns, False))  3.12 us
    ppermute x1, starting transfers between devices, body(): near = lax.ppermute(near, 'sx', swaps(rows, 0))  1.9 us
  transfers between devices with their start and end apart: 6, of which 3 were waited for; matrix products, arithmetic and copies ran while one was open for 2% of the time, Pallas kernels for 1%

profile of v8, /device:TPU:1, one launch (start us, length us, event | category | flops | bytes accessed | tf_op | source)
XLA Modules:
  0.0 72.0 jit_solution(14439925446605773752)
XLA Ops:
  0.0 3.7 %collective-permute-start = (f32[2,16,16,128]{3,2,1,0:T(8,128)}, f32[2,16,16,128]{3,2,1,0:T(8,128)S(1)}, u32[]{:S(2)}, u32[]{:S(2)}) collective-permute-start(f32[2,16,16,128]{3,2,1,0:T(8,128)} %param.5), channel_id=1, source_target_pairs={{0,128},{128,0},{1,129},{129,1},{2,130},{130,2},{3,131},{131,3},{4... | collective-permute-start | bytes 786440 | tf_op jit(solution)/shard_map/ppermute | solution.py:575
  3.7 1.2 %pad_maximum_fusion.held_ref.own_ref = f32[5,16,16,128]{3,2,1,0:T(8,128)S(1)} fusion(f32[1,16,16,128]{3,2,1,0:T(8,128)} %bitcast.9, f32[1,16,16,128]{3,2,1,0:T(8,128)} %bitcast.10, f32[1,16,16,128]{3,2,1,0:T(8,128)} %bitcast.11, f32[2,16,16,128]{3,2,1,0:T(8,128)} %param.5), kind=kLoop, calls=%fused_computation | loop fusion | flops 491520 | bytes 1310720 | tf_op jit(solution)/shard_map/concatenate | solution.py:577
  5.0 0.3 own.1
  5.3 3.1 %collective-permute-start.1 = (f32[8,16,128]{2,1,0:T(8,128)S(1)}, f32[8,16,128]{2,1,0:T(8,128)S(1)}, u32[]{:S(2)}, u32[]{:S(2)}) collective-permute-start(f32[8,16,128]{2,1,0:T(8,128)S(1)} %get-tuple-element.14), channel_id=1, source_target_pairs={{0,1},{1,2},{2,3},{3,4},{4,5},{5,6},{6,7},{129,128},{130,129},{131... | collective-permute-start | bytes 196616 | tf_op jit(solution)/shard_map/ppermute | solution.py:579
  8.4 0.7 collective-permute-start.2
  9.1 0.6 collective-permute-done.1.same_ref
  9.7 0.0 collective-permute-done.2.cross_ref
  9.7 0.0 collective-permute-done.other_ref
  9.7 0.1 rows.1
  9.9 1.9 %collective-permute-start.3 = (f32[72,16,128]{2,1,0:T(8,128)S(1)}, f32[72,16,128]{2,1,0:T(8,128)S(1)}, u32[]{:S(2)}, u32[]{:S(2)}) collective-permute-start(f32[72,16,128]{2,1,0:T(8,128)S(1)} %get-tuple-element.17), channel_id=1, source_target_pairs={{0,8},{8,0},{16,24},{24,16},{32,40},{40,32},{48,56},{56,48},{64,72... | collective-permute-start | bytes 1769480 | tf_op jit(solution)/shard_map/ppermute | solution.py:583
  11.8 3.4 %collective-permute-start.4 = (f32[72,16,128]{2,1,0:T(8,128)S(1)}, f32[72,16,128]{2,1,0:T(8,128)S(1)}, u32[]{:S(2)}, u32[]{:S(2)}) collective-permute-start(f32[72,16,128]{2,1,0:T(8,128)S(1)} %get-tuple-element.18), channel_id=1, source_target_pairs={{8,16},{16,8},{24,32},{32,24},{40,48},{48,40},{56,64},{64,56},{72,... | collective-permute-start | bytes 1769480 | tf_op jit(solution)/shard_map/ppermute | solution.py:582
  15.2 0.0 collective-permute-done.3.near_ref
  15.2 7.7 %collective-permute-done.4.far_ref = f32[72,16,128]{2,1,0:T(8,128)S(1)} collective-permute-done((f32[72,16,128]{2,1,0:T(8,128)S(1)}, f32[72,16,128]{2,1,0:T(8,128)S(1)}, u32[]{:S(2)}, u32[]{:S(2)}) %collective-permute-start.4) | collective-permute-done | bytes 589856 | tf_op jit(solution)/shard_map/ppermute | solution.py:582
  23.0 9.6 %main.1 = (f32[256,128]{1,0:T(8,128)S(1)}, f32[4,4,16,16,128]{4,3,2,1,0:T(8,128)S(1)}) custom-call(f32[5,16,16,128]{3,2,1,0:T(8,128)S(1)} %pad_maximum_fusion.held_ref.own_ref, f32[2,16,16,128]{3,2,1,0:T(8,128)S(1)} %collective-permute-done.other_ref, f32[8,16,128]{2,1,0:T(8,128)S(1)} %get-tuple-element.16.border_ref, ...), custom_call_target="tpu_custom_call" | custom-call | flops 50000000 | bytes 4390912 | tf_op jit(solution)/shard_map/main/pallas_call | solution.py:540
  32.6 31.9 %all_to_all.5 = f32[256,1,128]{2,1,0:T(1,128)S(1)} all-to-all(f32[256,1,128]{2,1,0:T(1,128)S(1)} %bitcast.8), channel_id=1, replica_groups=mesh['section'=2,'sx'=16,'sy'=8] {'section','sx','sy'}, dimensions={0} | all-to-all | bytes 262144 | tf_op jit(solution)/shard_map/all_to_all | solution.py:593
  64.5 0.7 send.1
  65.2 0.6 collective-permute-start.5
  65.7 0.2 mine.1.mine_ref
  66.0 5.3 %collective-permute-done.5.other_ref = f32[16,16,128]{2,1,0:T(8,128)S(1)} collective-permute-done((f32[16,16,128]{2,1,0:T(8,128)S(1)}, f32[16,16,128]{2,1,0:T(8,128)S(1)}, u32[]{:S(2)}, u32[]{:S(2)}) %collective-permute-start.5) | collective-permute-done | bytes 131104 | tf_op jit(solution)/shard_map/ppermute | solution.py:595
  71.2 0.8 %join.1 = f32[2,16,16,128]{3,2,1,0:T(8,128)} custom-call(f32[2,16,16,128]{3,2,1,0:T(8,128)S(1)} %mine.1.mine_ref, f32[16,16,128]{2,1,0:T(8,128)S(1)} %collective-permute-done.5.other_ref), custom_call_target="tpu_custom_call" | custom-call | flops 1000000 | bytes 655360 | tf_op jit(solution)/shard_map/join/pallas_call | solution.py:540
Async XLA Ops:
  0.0 9.7 %collective-permute-start = (f32[2,16,16,128]{3,2,1,0:T(8,128)}, f32[2,16,16,128]{3,2,1,0:T(8,128)S(1)}, u32[]{:S(2)}, u32[]{:S(2)}) collective-permute-start(f32[2,16,16,128]{3,2,1,0:T(8,128)} %param.5), channel_id=1, source_target_pairs={{0,128},{128,0},{1,129},{129,1},{2,130},{130,2},{3,131},{131,3},{4... | collective-permute-start | bytes 786440 | tf_op jit(solution)/shard_map/ppermute | solution.py:575
  5.3 4.4 %collective-permute-start.1 = (f32[8,16,128]{2,1,0:T(8,128)S(1)}, f32[8,16,128]{2,1,0:T(8,128)S(1)}, u32[]{:S(2)}, u32[]{:S(2)}) collective-permute-start(f32[8,16,128]{2,1,0:T(8,128)S(1)} %get-tuple-element.14), channel_id=1, source_target_pairs={{0,1},{1,2},{2,3},{3,4},{4,5},{5,6},{6,7},{129,128},{130,129},{131... | collective-permute-start | bytes 196616 | tf_op jit(solution)/shard_map/ppermute | solution.py:579
  8.4 1.3 %collective-permute-start.2 = (f32[8,16,128]{2,1,0:T(8,128)S(1)}, f32[8,16,128]{2,1,0:T(8,128)S(1)}, u32[]{:S(2)}, u32[]{:S(2)}) collective-permute-start(f32[8,16,128]{2,1,0:T(8,128)S(1)} %get-tuple-element.15), channel_id=1, source_target_pairs={{1,128},{2,129},{3,130},{4,131},{5,132},{6,133},{7,134},{128,1},{1... | collective-permute-start | bytes 196616 | tf_op jit(solution)/shard_map/ppermute | solution.py:580
  9.9 5.4 %collective-permute-start.3 = (f32[72,16,128]{2,1,0:T(8,128)S(1)}, f32[72,16,128]{2,1,0:T(8,128)S(1)}, u32[]{:S(2)}, u32[]{:S(2)}) collective-permute-start(f32[72,16,128]{2,1,0:T(8,128)S(1)} %get-tuple-element.17), channel_id=1, source_target_pairs={{0,8},{8,0},{16,24},{24,16},{32,40},{40,32},{48,56},{56,48},{64,72... | collective-permute-start | bytes 1769480 | tf_op jit(solution)/shard_map/ppermute | solution.py:583
  11.8 11.2 %collective-permute-start.4 = (f32[72,16,128]{2,1,0:T(8,128)S(1)}, f32[72,16,128]{2,1,0:T(8,128)S(1)}, u32[]{:S(2)}, u32[]{:S(2)}) collective-permute-start(f32[72,16,128]{2,1,0:T(8,128)S(1)} %get-tuple-element.18), channel_id=1, source_target_pairs={{8,16},{16,8},{24,32},{32,24},{40,48},{48,40},{56,64},{64,56},{72,... | collective-permute-start | bytes 1769480 | tf_op jit(solution)/shard_map/ppermute | solution.py:582
  65.2 6.1 %collective-permute-start.5 = (f32[16,16,128]{2,1,0:T(8,128)S(1)}, f32[16,16,128]{2,1,0:T(8,128)S(1)}, u32[]{:S(2)}, u32[]{:S(2)}) collective-permute-start(f32[16,16,128]{2,1,0:T(8,128)S(1)} %get-tuple-element.22), channel_id=1, source_target_pairs={{0,128},{128,0},{1,129},{129,1},{2,130},{130,2},{3,131},{131,3},{4... | collective-permute-start | bytes 393224 | tf_op jit(solution)/shard_map/ppermute | solution.py:595

commit v9 on v8

--- a/solution.py
+++ b/solution.py
@@ -267,7 +267,7 @@
     lax.fori_loop(0, count // unroll, group, 0)
 
 
-def main_kernel(consts, held_ref, other_ref, border_ref, near_ref, far_ref, part_ref, sums_ref,
+def main_kernel(consts, held_ref, other_ref, border_ref, far_ref, near_ref, part_ref, sums_ref,
                 val, kap, frozen, prv, rea, dif, fx, fy, fz, alpha, beta, vec, ya, yb, table):
     eigen_basis, basis_inverse, shift_rows, pairs = consts
     nz, nx = held_ref.shape[1], held_ref.shape[2]
@@ -589,7 +589,7 @@
     ]
     part, sums = call(
         functools.partial(main_kernel, consts), [(peers, LANES), (ITERS, 4, nz, nx, ny)], scratch, 50_000_000, "main", 26
-    )(held, other, border, near, far)
+    )(held, other, border, far, near)
     total = lax.all_to_all(part.reshape(peers, 1, LANES), axes, 0, 0).reshape(peers, LANES)
     half, weight = call(functools.partial(send_kernel, consts), [previous.shape, (2 * ITERS, LANES)], name="send")(total, sums, other)
     got = lax.ppermute(half, "section", partner)

time: 72.2 us -> 72.1 us (level)
    ppermute x1, starting transfers between devices: 1.9 us -> 0.09 us  [body(): near = lax.ppermute(near, 'sx', swaps(rows, 0))]
    ppermute x1, starting transfers between devices: 3.44 us -> 5.24 us  [body(): far = lax.ppermute(far, 'sx', swaps(rows, 1))]
where the time goes in v9:
time: 72.1 us; the launch traced here: 71.9 us
  blocking collectives  32 us (44%)
  starting transfers between devices  13.4 us (19%)
  waiting for transfers between devices  13.4 us (19%)
  Pallas kernels  11.8 us (16%)
  other arithmetic  1.2 us (2%)
    all_to_all x1, blocking collectives, body(): lax.all_to_all(part.reshape(peers, 1, LANES), axes, 0, 0)  32 us
    pallas_call x6, Pallas kernels, run(): pl.pallas_call(kernel, out_shape=shapes if many else shapes[0], in_specs=...  11.8 us
    ppermute x1, waiting for transfers between devices, body(): far = lax.ppermute(far, 'sx', swaps(rows, 1))  7.45 us
    ppermute x1, waiting for transfers between devices, body(): got = lax.ppermute(half, 'section', partner)  5.27 us
    ppermute x1, starting transfers between devices, body(): far = lax.ppermute(far, 'sx', swaps(rows, 1))  5.24 us
    ppermute x1, starting transfers between devices, body(): other = lax.ppermute(sections, 'section', partner)  3.74 us
    ppermute x1, starting transfers between devices, body(): same = lax.ppermute(same, ('section', 'sy'), beside(columns, False))  3.12 us
  transfers between devices with their start and end apart: 6, of which 3 were waited for; matrix products, arithmetic and copies ran while one was open for 2% of the time, Pallas kernels for 1%

profile of v9, /device:TPU:1, one launch (start us, length us, event | category | flops | bytes accessed | tf_op | source)
XLA Modules:
  0.0 71.9 jit_solution(4620960520544578099)
XLA Ops:
  0.0 3.7 %collective-permute-start = (f32[2,16,16,128]{3,2,1,0:T(8,128)}, f32[2,16,16,128]{3,2,1,0:T(8,128)S(1)}, u32[]{:S(2)}, u32[]{:S(2)}) collective-permute-start(f32[2,16,16,128]{3,2,1,0:T(8,128)} %param.5), channel_id=1, source_target_pairs={{0,128},{128,0},{1,129},{129,1},{2,130},{130,2},{3,131},{131,3},{4... | collective-permute-start | bytes 786440 | tf_op jit(solution)/shard_map/ppermute | solution.py:575
  3.7 1.2 %pad_maximum_fusion.held_ref.own_ref = f32[5,16,16,128]{3,2,1,0:T(8,128)S(1)} fusion(f32[1,16,16,128]{3,2,1,0:T(8,128)} %bitcast.9, f32[1,16,16,128]{3,2,1,0:T(8,128)} %bitcast.10, f32[1,16,16,128]{3,2,1,0:T(8,128)} %bitcast.11, f32[2,16,16,128]{3,2,1,0:T(8,128)} %param.5), kind=kLoop, calls=%fused_computation | loop fusion | flops 491520 | bytes 1310720 | tf_op jit(solution)/shard_map/concatenate | solution.py:577
  5.0 0.3 own.1
  5.3 3.1 %collective-permute-start.1 = (f32[8,16,128]{2,1,0:T(8,128)S(1)}, f32[8,16,128]{2,1,0:T(8,128)S(1)}, u32[]{:S(2)}, u32[]{:S(2)}) collective-permute-start(f32[8,16,128]{2,1,0:T(8,128)S(1)} %get-tuple-element.14), channel_id=1, source_target_pairs={{0,1},{1,2},{2,3},{3,4},{4,5},{5,6},{6,7},{129,128},{130,129},{131... | collective-permute-start | bytes 196616 | tf_op jit(solution)/shard_map/ppermute | solution.py:579
  8.4 0.7 collective-permute-start.2
  9.1 0.6 collective-permute-done.1.same_ref
  9.7 0.0 collective-permute-done.2.cross_ref
  9.7 0.0 collective-permute-done.other_ref
  9.7 0.1 rows.1
  9.9 5.2 %collective-permute-start.3 = (f32[72,16,128]{2,1,0:T(8,128)S(1)}, f32[72,16,128]{2,1,0:T(8,128)S(1)}, u32[]{:S(2)}, u32[]{:S(2)}) collective-permute-start(f32[72,16,128]{2,1,0:T(8,128)S(1)} %get-tuple-element.17), channel_id=1, source_target_pairs={{8,16},{16,8},{24,32},{32,24},{40,48},{48,40},{56,64},{64,56},{72,... | collective-permute-start | bytes 1769480 | tf_op jit(solution)/shard_map/ppermute | solution.py:582
  15.1 0.1 collective-permute-start.4
  15.2 7.5 %collective-permute-done.3.far_ref = f32[72,16,128]{2,1,0:T(8,128)S(1)} collective-permute-done((f32[72,16,128]{2,1,0:T(8,128)S(1)}, f32[72,16,128]{2,1,0:T(8,128)S(1)}, u32[]{:S(2)}, u32[]{:S(2)}) %collective-permute-start.3) | collective-permute-done | bytes 589856 | tf_op jit(solution)/shard_map/ppermute | solution.py:582
  22.7 0.0 collective-permute-done.4.near_ref
  22.7 9.6 %main.1 = (f32[256,128]{1,0:T(8,128)S(1)}, f32[4,4,16,16,128]{4,3,2,1,0:T(8,128)S(1)}) custom-call(f32[5,16,16,128]{3,2,1,0:T(8,128)S(1)} %pad_maximum_fusion.held_ref.own_ref, f32[2,16,16,128]{3,2,1,0:T(8,128)S(1)} %collective-permute-done.other_ref, f32[8,16,128]{2,1,0:T(8,128)S(1)} %get-tuple-element.16.border_ref, ...), custom_call_target="tpu_custom_call" | custom-call | flops 50000000 | bytes 4390912 | tf_op jit(solution)/shard_map/main/pallas_call | solution.py:540
  32.3 32.0 %all_to_all.5 = f32[256,1,128]{2,1,0:T(1,128)S(1)} all-to-all(f32[256,1,128]{2,1,0:T(1,128)S(1)} %bitcast.8), channel_id=1, replica_groups=mesh['section'=2,'sx'=16,'sy'=8] {'section','sx','sy'}, dimensions={0} | all-to-all | bytes 262144 | tf_op jit(solution)/shard_map/all_to_all | solution.py:593
  64.4 0.7 send.1
  65.1 0.6 collective-permute-start.5
  65.7 0.2 mine.1.mine_ref
  65.9 5.3 %collective-permute-done.5.other_ref = f32[16,16,128]{2,1,0:T(8,128)S(1)} collective-permute-done((f32[16,16,128]{2,1,0:T(8,128)S(1)}, f32[16,16,128]{2,1,0:T(8,128)S(1)}, u32[]{:S(2)}, u32[]{:S(2)}) %collective-permute-start.5) | collective-permute-done | bytes 131104 | tf_op jit(solution)/shard_map/ppermute | solution.py:595
  71.1 0.8 %join.1 = f32[2,16,16,128]{3,2,1,0:T(8,128)} custom-call(f32[2,16,16,128]{3,2,1,0:T(8,128)S(1)} %mine.1.mine_ref, f32[16,16,128]{2,1,0:T(8,128)S(1)} %collective-permute-done.5.other_ref), custom_call_target="tpu_custom_call" | custom-call | flops 1000000 | bytes 655360 | tf_op jit(solution)/shard_map/join/pallas_call | solution.py:540
Async XLA Ops:
  0.0 9.7 %collective-permute-start = (f32[2,16,16,128]{3,2,1,0:T(8,128)}, f32[2,16,16,128]{3,2,1,0:T(8,128)S(1)}, u32[]{:S(2)}, u32[]{:S(2)}) collective-permute-start(f32[2,16,16,128]{3,2,1,0:T(8,128)} %param.5), channel_id=1, source_target_pairs={{0,128},{128,0},{1,129},{129,1},{2,130},{130,2},{3,131},{131,3},{4... | collective-permute-start | bytes 786440 | tf_op jit(solution)/shard_map/ppermute | solution.py:575
  5.3 4.4 %collective-permute-start.1 = (f32[8,16,128]{2,1,0:T(8,128)S(1)}, f32[8,16,128]{2,1,0:T(8,128)S(1)}, u32[]{:S(2)}, u32[]{:S(2)}) collective-permute-start(f32[8,16,128]{2,1,0:T(8,128)S(1)} %get-tuple-element.14), channel_id=1, source_target_pairs={{0,1},{1,2},{2,3},{3,4},{4,5},{5,6},{6,7},{129,128},{130,129},{131... | collective-permute-start | bytes 196616 | tf_op jit(solution)/shard_map/ppermute | solution.py:579
  8.4 1.3 %collective-permute-start.2 = (f32[8,16,128]{2,1,0:T(8,128)S(1)}, f32[8,16,128]{2,1,0:T(8,128)S(1)}, u32[]{:S(2)}, u32[]{:S(2)}) collective-permute-start(f32[8,16,128]{2,1,0:T(8,128)S(1)} %get-tuple-element.15), channel_id=1, source_target_pairs={{1,128},{2,129},{3,130},{4,131},{5,132},{6,133},{7,134},{128,1},{1... | collective-permute-start | bytes 196616 | tf_op jit(solution)/shard_map/ppermute | solution.py:580
  9.9 12.8 %collective-permute-start.3 = (f32[72,16,128]{2,1,0:T(8,128)S(1)}, f32[72,16,128]{2,1,0:T(8,128)S(1)}, u32[]{:S(2)}, u32[]{:S(2)}) collective-permute-start(f32[72,16,128]{2,1,0:T(8,128)S(1)} %get-tuple-element.17), channel_id=1, source_target_pairs={{8,16},{16,8},{24,32},{32,24},{40,48},{48,40},{56,64},{64,56},{72,... | collective-permute-start | bytes 1769480 | tf_op jit(solution)/shard_map/ppermute | solution.py:582
  15.1 7.6 %collective-permute-start.4 = (f32[72,16,128]{2,1,0:T(8,128)S(1)}, f32[72,16,128]{2,1,0:T(8,128)S(1)}, u32[]{:S(2)}, u32[]{:S(2)}) collective-permute-start(f32[72,16,128]{2,1,0:T(8,128)S(1)} %get-tuple-element.18), channel_id=1, source_target_pairs={{0,8},{8,0},{16,24},{24,16},{32,40},{40,32},{48,56},{56,48},{64,72... | collective-permute-start | bytes 1769480 | tf_op jit(solution)/shard_map/ppermute | solution.py:583
  65.1 6.1 %collective-permute-start.5 = (f32[16,16,128]{2,1,0:T(8,128)S(1)}, f32[16,16,128]{2,1,0:T(8,128)S(1)}, u32[]{:S(2)}, u32[]{:S(2)}) collective-permute-start(f32[16,16,128]{2,1,0:T(8,128)S(1)} %get-tuple-element.22), channel_id=1, source_target_pairs={{0,128},{128,0},{1,129},{129,1},{2,130},{130,2},{3,131},{131,3},{4... | collective-permute-start | bytes 393224 | tf_op jit(solution)/shard_map/ppermute | solution.py:595

commit v10 on v9

--- a/solution.py
+++ b/solution.py
@@ -204,13 +204,13 @@
     return z * PARTS + entry, row, z * PARTS + last, ninth
 
 
-def pack_rows(near_ref, far_ref, cell, slot, z, even):
-    nx = cell.shape[0]
-    entry, row, last, ninth = place(slot, z)
-    near_ref[entry, row : row + 8] = jnp.where(even, cell[nx - 8 : nx], cell[0:8])
-    far_ref[entry, row : row + 8] = jnp.where(even, cell[0:8], cell[nx - 8 : nx])
-    near_ref[last, ninth : ninth + 1] = jnp.where(even, cell[nx - 9 : nx - 8], cell[8:9])
-    far_ref[last, ninth : ninth + 1] = jnp.where(even, cell[8:9], cell[nx - 9 : nx - 8])
+def put(tile, cell, at, start, lanes):
+    moved = pltpu.roll(cell, lax.rem(at + LANES - start, LANES), 1)
+    return jnp.where((lanes >= at) & (lanes < at + EDGE), moved, tile)
+
+
+def inner_start():
+    return jnp.where(left_half(), LANES // 2, LANES // 2 - EDGE)
 
 
 def own_kernel(held_ref, same_ref, cross_ref):
@@ -218,10 +218,6 @@
     lanes = lane_ids(nx)
     incoming = border_start()
     outgoing = LANES - EDGE - incoming
-
-    def put(tile, cell, at, start):
-        moved = pltpu.roll(cell, lax.rem(at + LANES - start, LANES), 1)
-        return jnp.where((lanes >= at) & (lanes < at + EDGE), moved, tile)
 
     for plane in range(nz // 2):
         same = jnp.zeros((nx, LANES), jnp.float32)
@@ -230,24 +226,46 @@
             z = part * (nz // 2) + plane
             for slot in range(5):
                 cell = held_ref[slot, z]
-                same = put(same, cell, part * 64 + ORDER[slot] * EDGE, incoming)
+                same = put(same, cell, part * 64 + ORDER[slot] * EDGE, incoming, lanes)
                 if slot < 2:
-                    cross = put(cross, cell, part * 64 + (2 + slot) * EDGE, outgoing)
+                    cross = put(cross, cell, part * 64 + (2 + slot) * EDGE, outgoing, lanes)
         same_ref[plane] = same
         cross_ref[plane] = cross
 
 
 def rows_kernel(held_ref, other_ref, same_ref, cross_ref, border_ref, near_ref, far_ref):
-    nz = other_ref.shape[1]
+    nz, nx = other_ref.shape[1], other_ref.shape[2]
     even = on_even_row()
-    for z in range(nz):
-        for slot in range(7):
-            pack_rows(near_ref, far_ref, held_ref[slot, z] if slot < 5 else other_ref[slot - 5, z], slot, z, even)
-    for plane in range(nz // 2):
+    inner = inner_start()
+    half = nz // 2
+    for plane in range(half):
+        inner_rows, inner_ninth = jnp.zeros((8, LANES), jnp.float32), jnp.zeros((1, LANES), jnp.float32)
+        for part in range(2):
+            z = part * half + plane
+            rows, ninths = [], []
+            for slot, f in enumerate(ORDER):
+                cell = held_ref[slot, z] if slot < 5 else other_ref[slot - 5, z]
+                entry, row, last, ninth = place(slot, z)
+                near_ref[entry, row : row + 8] = jnp.where(even, cell[nx - 8 : nx], cell[0:8])
+                near_ref[last, ninth : ninth + 1] = jnp.where(even, cell[nx - 9 : nx - 8], cell[8:9])
+                rows.append(jnp.where(even, cell[0:8], cell[nx - 8 : nx]))
+                ninths.append(jnp.where(even, cell[8:9], cell[nx - 9 : nx - 8]))
+                at = part * 64 + f * EDGE
+                inner_rows = put(inner_rows, rows[-1], at, inner, lane_ids(8))
+                inner_ninth = put(inner_ninth, ninths[-1], at, inner, lane_ids(1))
+            for pair in range(4):
+                first, second = 2 * pair, min(2 * pair + 1, 6)
+                top = 8 * (pair % 2)
+                far_ref[2 * z + pair // 2, top : top + 8] = jnp.where(half_mask(8), rows[first], turn(rows[second], LANES // 2))
+                row = 4 * part + pair
+                far_ref[2 * nz + plane, row : row + 1] = jnp.where(half_mask(1), ninths[first], turn(ninths[second], LANES // 2))
         border = same_ref[plane] + cross_ref[plane]
         border_ref[plane] = border
         near_ref[nz * PARTS + plane] = border
-        far_ref[nz * PARTS + plane] = border
+        far_ref[2 * nz + plane, 8:9] = jnp.where(even, border[8:9], border[nx - 9 : nx - 8])
+        far_ref[2 * nz + plane, 9:10] = inner_ninth
+        far_ref[2 * nz + half + plane, 0:8] = jnp.where(even, border[0:8], border[nx - 8 : nx])
+        far_ref[2 * nz + half + plane, 8:16] = inner_rows
 
 
 ROWS = 48
@@ -286,26 +304,43 @@
             for ref in (val, kap, ya, yb):
                 ref[f, at] = zero_plane
 
-    def both(entry, row, count):
-        near, far = near_ref[entry, row : row + count], far_ref[entry, row : row + count]
-        return jnp.where(even, far, near), jnp.where(even, near, far)
+    inner = inner_start()
+
+    def unpack(cells, window, second, at):
+        count = cells.shape[0]
+        ids = lane_ids(count)
+        cells = turn(cells, LANES // 2) if second else cells
+        window = pltpu.roll(window, lax.rem(inner + LANES - at, LANES), 1)
+        return jnp.where(half_mask(count), cells, jnp.where((ids >= inner) & (ids < inner + EDGE), window, 0.0))
 
     def assemble(plane):
-        at = nz * PARTS + plane
-        low = jnp.where(even, far_ref[at], near_ref[at])
-        high = jnp.where(even, near_ref[at], far_ref[at])
-        sides = jnp.concatenate([tile(low[nx - 9 : nx - 8]), low[nx - 8 : nx], border_ref[plane], high[0:8], tile(high[8:9])], 0)
+        near_side = near_ref[nz * PARTS + plane]
+        ends, window = 2 * nz + plane, 2 * nz + nz // 2 + plane
+        far_side, far_end = far_ref[window, 0:8], far_ref[ends, 8:9]
+        sides = jnp.concatenate(
+            [
+                tile(jnp.where(even, far_end, near_side[nx - 9 : nx - 8])), jnp.where(even, far_side, near_side[nx - 8 : nx]),
+                border_ref[plane],
+                jnp.where(even, near_side[0:8], far_side), tile(jnp.where(even, near_side[8:9], far_end)),
+            ],
+            0,
+        )
         for part in range(2):
             z = part * (nz // 2) + plane
 
             def column(f):
                 slot = ORDER.index(f)
                 mid = held_ref[slot, z] if slot < 5 else other_ref[slot - 5, z]
+                at = part * 64 + f * EDGE
                 entry, row, last, ninth = place(slot, z)
-                low, high = both(entry, row, 8)
-                low_end, high_end = both(last, ninth, 1)
+                near, near_end = near_ref[entry, row : row + 8], near_ref[last, ninth : ninth + 1]
+                pair, second = divmod(slot, 2)
+                top, end = 8 * (pair % 2), 4 * part + pair
+                far = unpack(far_ref[2 * z + pair // 2, top : top + 8], far_ref[window, 8:16], second, at)
+                far_end = unpack(far_ref[ends, end : end + 1], far_ref[ends, 9:10], second, at)
+                low, high = jnp.where(even, far, near), jnp.where(even, near, far)
+                low_end, high_end = jnp.where(even, far_end, near_end), jnp.where(even, near_end, far_end)
                 cells = jnp.concatenate([tile(low_end), low, mid, high, tile(high_end)], 0)
-                at = part * 64 + f * EDGE
                 return jnp.where(edge, pltpu.roll(sides, lax.rem(start + LANES - at, LANES), 1), cells)
 
             diff, prev, react = column(5), column(4), column(6)
@@ -573,12 +608,12 @@
     axes = ("section", "sx", "sy")
     partner = [(0, 1), (1, 0)]
     other = lax.ppermute(sections, "section", partner)
-    edge, line = (nz // 2, nx, ny), (nz * PARTS + nz // 2, TALL, ny)
+    edge, whole, thin = (nz // 2, nx, ny), (nz * PARTS + nz // 2, TALL, ny), (3 * nz, TALL, ny)
     held = jnp.concatenate([sections, previous[None], diffusivity[None], reaction[None]], 0)
     same, cross = call(own_kernel, [edge, edge], name="own")(held)
     same = lax.ppermute(same, ("section", "sy"), beside(columns, False))
     cross = lax.ppermute(cross, ("section", "sy"), beside(columns, True))
-    border, near, far = call(rows_kernel, [edge, line, line], name="rows")(held, other, same, cross)
+    border, near, far = call(rows_kernel, [edge, whole, thin], name="rows")(held, other, same, cross)
     far = lax.ppermute(far, "sx", swaps(rows, 1))
     near = lax.ppermute(near, "sx", swaps(rows, 0))
     peers = 2 * columns * rows

time: 72.1 us -> 70.8 us (0.982)
  waiting for transfers between devices: 13.4 us -> 11.5 us
    ppermute x1, waiting for transfers between devices: 7.45 us -> 5.63 us  [body(): far = lax.ppermute(far, 'sx', swaps(rows, 1))]
    ppermute x1, starting transfers between devices: 0.09 us -> 1.9 us  [body(): near = lax.ppermute(near, 'sx', swaps(rows, 0))]
    ppermute x1, starting transfers between devices: 5.24 us -> 3.44 us  [body(): far = lax.ppermute(far, 'sx', swaps(rows, 1))]
where the time goes in v10:
time: 70.8 us; the launch traced here: 70.6 us
  blocking collectives  31.9 us (45%)
  starting transfers between devices  13.5 us (19%)
  Pallas kernels  12.5 us (18%)
  waiting for transfers between devices  11.5 us (16%)
  other arithmetic  1.2 us (2%)
    all_to_all x1, blocking collectives, body(): lax.all_to_all(part.reshape(peers, 1, LANES), axes, 0, 0)  31.9 us
    pallas_call x6, Pallas kernels, run(): pl.pallas_call(kernel, out_shape=shapes if many else shapes[0], in_specs=...  12.5 us
    ppermute x1, waiting for transfers between devices, body(): far = lax.ppermute(far, 'sx', swaps(rows, 1))  5.63 us
    ppermute x1, waiting for transfers between devices, body(): got = lax.ppermute(half, 'section', partner)  5.27 us
    ppermute x1, starting transfers between devices, body(): other = lax.ppermute(sections, 'section', partner)  3.74 us
    ppermute x1, starting transfers between devices, body(): far = lax.ppermute(far, 'sx', swaps(rows, 1))  3.44 us
    ppermute x1, starting transfers between devices, body(): same = lax.ppermute(same, ('section', 'sy'), beside(columns, False))  3.12 us
    ppermute x1, starting transfers between devices, body(): near = lax.ppermute(near, 'sx', swaps(rows, 0))  1.9 us
  transfers between devices with their start and end apart: 6, of which 3 were waited for; matrix products, arithmetic and copies ran while one was open for 2% of the time, Pallas kernels for 1%

profile of v10, /device:TPU:1, one launch (start us, length us, event | category | flops | bytes accessed | tf_op | source)
XLA Modules:
  0.0 70.6 jit_solution(10491868578881830123)
XLA Ops:
  0.0 3.7 %collective-permute-start = (f32[2,16,16,128]{3,2,1,0:T(8,128)}, f32[2,16,16,128]{3,2,1,0:T(8,128)S(1)}, u32[]{:S(2)}, u32[]{:S(2)}) collective-permute-start(f32[2,16,16,128]{3,2,1,0:T(8,128)} %param.5), channel_id=1, source_target_pairs={{0,128},{128,0},{1,129},{129,1},{2,130},{130,2},{3,131},{131,3},{4... | collective-permute-start | bytes 786440 | tf_op jit(solution)/shard_map/ppermute | solution.py:610
  3.7 1.2 %pad_maximum_fusion.held_ref.own_ref = f32[5,16,16,128]{3,2,1,0:T(8,128)S(1)} fusion(f32[1,16,16,128]{3,2,1,0:T(8,128)} %bitcast.9, f32[1,16,16,128]{3,2,1,0:T(8,128)} %bitcast.10, f32[1,16,16,128]{3,2,1,0:T(8,128)} %bitcast.11, f32[2,16,16,128]{3,2,1,0:T(8,128)} %param.5), kind=kLoop, calls=%fused_computation | loop fusion | flops 491520 | bytes 1310720 | tf_op jit(solution)/shard_map/concatenate | solution.py:612
  5.0 0.3 own.1
  5.3 3.1 %collective-permute-start.1 = (f32[8,16,128]{2,1,0:T(8,128)S(1)}, f32[8,16,128]{2,1,0:T(8,128)S(1)}, u32[]{:S(2)}, u32[]{:S(2)}) collective-permute-start(f32[8,16,128]{2,1,0:T(8,128)S(1)} %get-tuple-element.14), channel_id=1, source_target_pairs={{0,1},{1,2},{2,3},{3,4},{4,5},{5,6},{6,7},{129,128},{130,129},{131... | collective-permute-start | bytes 196616 | tf_op jit(solution)/shard_map/ppermute | solution.py:614
  8.4 0.7 collective-permute-start.2
  9.1 0.6 collective-permute-done.1.same_ref
  9.7 0.0 collective-permute-done.2.cross_ref
  9.7 0.0 collective-permute-done.other_ref
  9.7 0.5 rows.1
  10.2 1.9 %collective-permute-start.4 = (f32[72,16,128]{2,1,0:T(8,128)S(1)}, f32[72,16,128]{2,1,0:T(8,128)S(1)}, u32[]{:S(2)}, u32[]{:S(2)}) collective-permute-start(f32[72,16,128]{2,1,0:T(8,128)S(1)} %get-tuple-element.18), channel_id=1, source_target_pairs={{0,8},{8,0},{16,24},{24,16},{32,40},{40,32},{48,56},{56,48},{64,72... | collective-permute-start | bytes 1769480 | tf_op jit(solution)/shard_map/ppermute | solution.py:618
  12.1 3.4 %collective-permute-start.3 = (f32[48,16,128]{2,1,0:T(8,128)S(1)}, f32[48,16,128]{2,1,0:T(8,128)S(1)}, u32[]{:S(2)}, u32[]{:S(2)}) collective-permute-start(f32[48,16,128]{2,1,0:T(8,128)S(1)} %get-tuple-element.17), channel_id=1, source_target_pairs={{8,16},{16,8},{24,32},{32,24},{40,48},{48,40},{56,64},{64,56},{72,... | collective-permute-start | bytes 1179656 | tf_op jit(solution)/shard_map/ppermute | solution.py:617
  15.5 5.6 %collective-permute-done.3.far_ref = f32[48,16,128]{2,1,0:T(8,128)S(1)} collective-permute-done((f32[48,16,128]{2,1,0:T(8,128)S(1)}, f32[48,16,128]{2,1,0:T(8,128)S(1)}, u32[]{:S(2)}, u32[]{:S(2)}) %collective-permute-start.3) | collective-permute-done | bytes 393248 | tf_op jit(solution)/shard_map/ppermute | solution.py:617
  21.2 0.0 collective-permute-done.4.near_ref
  21.2 10.0 %main.1 = (f32[256,128]{1,0:T(8,128)S(1)}, f32[4,4,16,16,128]{4,3,2,1,0:T(8,128)S(1)}) custom-call(f32[5,16,16,128]{3,2,1,0:T(8,128)S(1)} %pad_maximum_fusion.held_ref.own_ref, f32[2,16,16,128]{3,2,1,0:T(8,128)S(1)} %collective-permute-done.other_ref, f32[8,16,128]{2,1,0:T(8,128)S(1)} %get-tuple-element.16.border_ref, ...), custom_call_target="tpu_custom_call" | custom-call | flops 50000000 | bytes 4194304 | tf_op jit(solution)/shard_map/main/pallas_call | solution.py:575
  31.2 31.9 %all_to_all.5 = f32[256,1,128]{2,1,0:T(1,128)S(1)} all-to-all(f32[256,1,128]{2,1,0:T(1,128)S(1)} %bitcast.8), channel_id=1, replica_groups=mesh['section'=2,'sx'=16,'sy'=8] {'section','sx','sy'}, dimensions={0} | all-to-all | bytes 262144 | tf_op jit(solution)/shard_map/all_to_all | solution.py:628
  63.0 0.7 send.1
  63.7 0.6 collective-permute-start.5
  64.3 0.2 mine.1.mine_ref
  64.5 5.3 %collective-permute-done.5.other_ref = f32[16,16,128]{2,1,0:T(8,128)S(1)} collective-permute-done((f32[16,16,128]{2,1,0:T(8,128)S(1)}, f32[16,16,128]{2,1,0:T(8,128)S(1)}, u32[]{:S(2)}, u32[]{:S(2)}) %collective-permute-start.5) | collective-permute-done | bytes 131104 | tf_op jit(solution)/shard_map/ppermute | solution.py:630
  69.8 0.8 %join.1 = f32[2,16,16,128]{3,2,1,0:T(8,128)} custom-call(f32[2,16,16,128]{3,2,1,0:T(8,128)S(1)} %mine.1.mine_ref, f32[16,16,128]{2,1,0:T(8,128)S(1)} %collective-permute-done.5.other_ref), custom_call_target="tpu_custom_call" | custom-call | flops 1000000 | bytes 655360 | tf_op jit(solution)/shard_map/join/pallas_call | solution.py:575
Async XLA Ops:
  0.0 9.7 %collective-permute-start = (f32[2,16,16,128]{3,2,1,0:T(8,128)}, f32[2,16,16,128]{3,2,1,0:T(8,128)S(1)}, u32[]{:S(2)}, u32[]{:S(2)}) collective-permute-start(f32[2,16,16,128]{3,2,1,0:T(8,128)} %param.5), channel_id=1, source_target_pairs={{0,128},{128,0},{1,129},{129,1},{2,130},{130,2},{3,131},{131,3},{4... | collective-permute-start | bytes 786440 | tf_op jit(solution)/shard_map/ppermute | solution.py:610
  5.3 4.4 %collective-permute-start.1 = (f32[8,16,128]{2,1,0:T(8,128)S(1)}, f32[8,16,128]{2,1,0:T(8,128)S(1)}, u32[]{:S(2)}, u32[]{:S(2)}) collective-permute-start(f32[8,16,128]{2,1,0:T(8,128)S(1)} %get-tuple-element.14), channel_id=1, source_target_pairs={{0,1},{1,2},{2,3},{3,4},{4,5},{5,6},{6,7},{129,128},{130,129},{131... | collective-permute-start | bytes 196616 | tf_op jit(solution)/shard_map/ppermute | solution.py:614
  8.4 1.3 %collective-permute-start.2 = (f32[8,16,128]{2,1,0:T(8,128)S(1)}, f32[8,16,128]{2,1,0:T(8,128)S(1)}, u32[]{:S(2)}, u32[]{:S(2)}) collective-permute-start(f32[8,16,128]{2,1,0:T(8,128)S(1)} %get-tuple-element.15), channel_id=1, source_target_pairs={{1,128},{2,129},{3,130},{4,131},{5,132},{6,133},{7,134},{128,1},{1... | collective-permute-start | bytes 196616 | tf_op jit(solution)/shard_map/ppermute | solution.py:615
  10.2 11.0 %collective-permute-start.4 = (f32[72,16,128]{2,1,0:T(8,128)S(1)}, f32[72,16,128]{2,1,0:T(8,128)S(1)}, u32[]{:S(2)}, u32[]{:S(2)}) collective-permute-start(f32[72,16,128]{2,1,0:T(8,128)S(1)} %get-tuple-element.18), channel_id=1, source_target_pairs={{0,8},{8,0},{16,24},{24,16},{32,40},{40,32},{48,56},{56,48},{64,72... | collective-permute-start | bytes 1769480 | tf_op jit(solution)/shard_map/ppermute | solution.py:618
  12.1 9.1 %collective-permute-start.3 = (f32[48,16,128]{2,1,0:T(8,128)S(1)}, f32[48,16,128]{2,1,0:T(8,128)S(1)}, u32[]{:S(2)}, u32[]{:S(2)}) collective-permute-start(f32[48,16,128]{2,1,0:T(8,128)S(1)} %get-tuple-element.17), channel_id=1, source_target_pairs={{8,16},{16,8},{24,32},{32,24},{40,48},{48,40},{56,64},{64,56},{72,... | collective-permute-start | bytes 1179656 | tf_op jit(solution)/shard_map/ppermute | solution.py:617
  63.7 6.1 %collective-permute-start.5 = (f32[16,16,128]{2,1,0:T(8,128)S(1)}, f32[16,16,128]{2,1,0:T(8,128)S(1)}, u32[]{:S(2)}, u32[]{:S(2)}) collective-permute-start(f32[16,16,128]{2,1,0:T(8,128)S(1)} %get-tuple-element.22), channel_id=1, source_target_pairs={{0,128},{128,0},{1,129},{129,1},{2,130},{130,2},{3,131},{131,3},{4... | collective-permute-start | bytes 393224 | tf_op jit(solution)/shard_map/ppermute | solution.py:630

commit v11 on v10

--- a/solution.py
+++ b/solution.py
@@ -272,6 +272,7 @@
 FIRST, LAST = 8, 40
 OWN = slice(16, 32)
 WORK = slice(FIRST, LAST)
+NARROW = slice(12, 36)
 BEFORE = slice(FIRST - 1, LAST - 1)
 AFTER = slice(FIRST + 1, LAST + 1)
 
@@ -416,23 +417,29 @@
         in_z = fz[0, z, cut] * ref[m, z, lo:hi] + fz[1, z, cut] * ref[m, z + 2, lo:hi]
         return (in_x + in_z) + in_y
 
+    def window(done):
+        reach = 2 * ITERS - done
+        return OWN if reach == 0 else NARROW if reach <= 4 else WORK
+
     for j in range(ITERS):
 
         def odd(z, j=j):
+            rows = window(2 * j + 1)
+            cut = slice(rows.start - FIRST, rows.stop - FIRST)
             for b in range(2):
-                t0 = spread(ya, 2 * b, z)
-                t1 = spread(ya, 2 * b + 1, z)
-                al, be = alpha[b, z], beta[b, z]
-                y0 = al * t0 - be * t1
-                y1 = be * t0 + al * t1
-                yb[2 * b, z + 1, WORK] = y0
-                yb[2 * b + 1, z + 1, WORK] = y1
-                sums_ref[j, 2 * b, z] = ya[2 * b, z + 1, OWN] + y0[8:24]
-                sums_ref[j, 2 * b + 1, z] = ya[2 * b + 1, z + 1, OWN] + y1[8:24]
+                t0 = spread(ya, 2 * b, z, rows)
+                t1 = spread(ya, 2 * b + 1, z, rows)
+                al, be = alpha[b, z, cut], beta[b, z, cut]
+                for m, y in ((2 * b, al * t0 - be * t1), (2 * b + 1, be * t0 + al * t1)):
+                    yb[m, z + 1, rows] = y
+                    if rows == WORK:
+                        sums_ref[j, m, z, 4:20] = ya[m, z + 1, OWN] + y[8:24]
+                    else:
+                        sums_ref[j, m, z] = ya[m, z + 1, rows] + y
 
         def even(z, j=j):
             last = j == ITERS - 1
-            rows = OWN if last else WORK
+            rows = window(2 * j + 2)
             cut = slice(rows.start - FIRST, rows.stop - FIRST)
             for b in range(2):
                 new = []
@@ -443,9 +450,9 @@
                     vec[j + 1, m, z, cut] = v
                     new.append(v)
                 if not last:
-                    al, be = alpha[b, z], beta[b, z]
-                    ya[2 * b, z + 1, WORK] = al * new[0] - be * new[1]
-                    ya[2 * b + 1, z + 1, WORK] = be * new[0] + al * new[1]
+                    al, be = alpha[b, z, cut], beta[b, z, cut]
+                    ya[2 * b, z + 1, rows] = al * new[0] - be * new[1]
+                    ya[2 * b + 1, z + 1, rows] = be * new[0] + al * new[1]
 
         each_plane(nz, STEP_UNROLL, odd)
         each_plane(nz, STEP_UNROLL, even)
@@ -454,19 +461,18 @@
     mine = half_mask(8)
     for b in range(2):
 
-        def dots(z, carry):
+        def dots(i, carry):
             out = list(carry)
-            for m in (2 * b, 2 * b + 1):
-                for r in (8, 16):
-                    cells = [vec[i, m, z, r : r + 8] for i in range(SIZE)]
-                    for at, (i, j) in enumerate(PAIRS):
-                        out[at] = out[at] + cells[i] * cells[j]
+            for z, m in [(4 * i + u, m) for u in range(4) for m in (2 * b, 2 * b + 1)]:
+                cells = [jnp.where(mine, vec[k, m, z, 8:16], turn(vec[k, m, z, 16:24], LANES // 2)) for k in range(SIZE)]
+                for at, (k, j) in enumerate(PAIRS):
+                    out[at] = out[at] + cells[k] * cells[j]
             return tuple(out)
 
         zero = jnp.zeros((8, LANES), jnp.float32)
-        out = lax.fori_loop(0, nz, dots, tuple(zero for _ in PAIRS))
+        out = lax.fori_loop(0, nz // 4, dots, tuple(zero for _ in PAIRS))
         for at in range(len(PAIRS)):
-            row = jnp.sum(jnp.where(mine, out[at], 0.0), axis=0, keepdims=True)
+            row = jnp.sum(out[at], axis=0, keepdims=True)
             table[b * len(PAIRS) + at : b * len(PAIRS) + at + 1] = row
     total = jnp.sum(table[...].T, axis=0, keepdims=True)
     part_ref[...] = jnp.broadcast_to(total, part_ref.shape)
@@ -525,9 +531,9 @@
     def combine(z):
         outs = [other_ref[r, z] for r in range(2)]
         for m in range(4):
-            field = weights[m // 2][0] * sums_ref[0, m, z]
+            field = weights[m // 2][0] * sums_ref[0, m, z, 4:20]
             for j in range(1, ITERS):
-                field = field + weights[m // 2][j] * sums_ref[j, m, z]
+                field = field + weights[m // 2][j] * sums_ref[j, m, z, 4:20]
             outs = [outs[r] + basis[r][m] * field for r in range(2)]
         send_ref[z] = jnp.where(mine, outs[0], turn(outs[1], LANES // 2))
 
@@ -547,9 +553,9 @@
     def combine(z):
         outs = [own_ref[r, z] for r in range(2)]
         for m in range(4):
-            field = weights[m // 2][0] * sums_ref[0, m, z]
+            field = weights[m // 2][0] * sums_ref[0, m, z, 4:20]
             for j in range(1, ITERS):
-                field = field + weights[m // 2][j] * sums_ref[j, m, z]
+                field = field + weights[m // 2][j] * sums_ref[j, m, z, 4:20]
             outs = [outs[r] + basis[r][m] * field for r in range(2)]
         mine_ref[0, z] = outs[0]
         mine_ref[1, z] = outs[1]
@@ -623,7 +629,7 @@
         (SIZE, 4) + work, (4,) + padded, (4,) + padded, (LANES, LANES),
     ]
     part, sums = call(
-        functools.partial(main_kernel, consts), [(peers, LANES), (ITERS, 4, nz, nx, ny)], scratch, 50_000_000, "main", 26
+        functools.partial(main_kernel, consts), [(peers, LANES), (ITERS, 4, nz, nx + 8, ny)], scratch, 50_000_000, "main", 26
     )(held, other, border, far, near)
     total = lax.all_to_all(part.reshape(peers, 1, LANES), axes, 0, 0).reshape(peers, LANES)
     half, weight = call(functools.partial(send_kernel, consts), [previous.shape, (2 * ITERS, LANES)], name="send")(total, sums, other)

time: 70.8 us -> 70.4 us (level)
  no operation moved by 1% of the time
where the time goes in v11:
time: 70.4 us; the launch traced here: 70.3 us
  blocking collectives  31.9 us (45%)
  starting transfers between devices  13.5 us (19%)
  Pallas kernels  12.1 us (17%)
  waiting for transfers between devices  11.5 us (16%)
  other arithmetic  1.2 us (2%)
    all_to_all x1, blocking collectives, body(): lax.all_to_all(part.reshape(peers, 1, LANES), axes, 0, 0)  31.9 us
    pallas_call x6, Pallas kernels, run(): pl.pallas_call(kernel, out_shape=shapes if many else shapes[0], in_specs=...  12.1 us
    ppermute x1, waiting for transfers between devices, body(): far = lax.ppermute(far, 'sx', swaps(rows, 1))  5.63 us
    ppermute x1, waiting for transfers between devices, body(): got = lax.ppermute(half, 'section', partner)  5.26 us
    ppermute x1, starting transfers between devices, body(): other = lax.ppermute(sections, 'section', partner)  3.74 us
    ppermute x1, starting transfers between devices, body(): far = lax.ppermute(far, 'sx', swaps(rows, 1))  3.44 us
    ppermute x1, starting transfers between devices, body(): same = lax.ppermute(same, ('section', 'sy'), beside(columns, False))  3.12 us
    ppermute x1, starting transfers between devices, body(): near = lax.ppermute(near, 'sx', swaps(rows, 0))  1.9 us
  transfers between devices with their start and end apart: 6, of which 3 were waited for; matrix products, arithmetic and copies ran while one was open for 2% of the time, Pallas kernels for 1%

profile of v11, /device:TPU:1, one launch (start us, length us, event | category | flops | bytes accessed | tf_op | source)
XLA Modules:
  0.0 70.3 jit_solution(14545815849610264474)
XLA Ops:
  0.0 3.7 %collective-permute-start = (f32[2,16,16,128]{3,2,1,0:T(8,128)}, f32[2,16,16,128]{3,2,1,0:T(8,128)S(1)}, u32[]{:S(2)}, u32[]{:S(2)}) collective-permute-start(f32[2,16,16,128]{3,2,1,0:T(8,128)} %param.5), channel_id=1, source_target_pairs={{0,128},{128,0},{1,129},{129,1},{2,130},{130,2},{3,131},{131,3},{4... | collective-permute-start | bytes 786440 | tf_op jit(solution)/shard_map/ppermute | solution.py:616
  3.7 1.2 %pad_maximum_fusion.held_ref.own_ref = f32[5,16,16,128]{3,2,1,0:T(8,128)S(1)} fusion(f32[1,16,16,128]{3,2,1,0:T(8,128)} %bitcast.9, f32[1,16,16,128]{3,2,1,0:T(8,128)} %bitcast.10, f32[1,16,16,128]{3,2,1,0:T(8,128)} %bitcast.11, f32[2,16,16,128]{3,2,1,0:T(8,128)} %param.5), kind=kLoop, calls=%fused_computation | loop fusion | flops 491520 | bytes 1310720 | tf_op jit(solution)/shard_map/concatenate | solution.py:618
  5.0 0.3 own.1
  5.3 3.1 %collective-permute-start.1 = (f32[8,16,128]{2,1,0:T(8,128)S(1)}, f32[8,16,128]{2,1,0:T(8,128)S(1)}, u32[]{:S(2)}, u32[]{:S(2)}) collective-permute-start(f32[8,16,128]{2,1,0:T(8,128)S(1)} %get-tuple-element.14), channel_id=1, source_target_pairs={{0,1},{1,2},{2,3},{3,4},{4,5},{5,6},{6,7},{129,128},{130,129},{131... | collective-permute-start | bytes 196616 | tf_op jit(solution)/shard_map/ppermute | solution.py:620
  8.4 0.7 collective-permute-start.2
  9.1 0.6 collective-permute-done.1.same_ref
  9.7 0.0 collective-permute-done.2.cross_ref
  9.7 0.0 collective-permute-done.other_ref
  9.7 0.5 rows.1
  10.2 1.9 %collective-permute-start.4 = (f32[72,16,128]{2,1,0:T(8,128)S(1)}, f32[72,16,128]{2,1,0:T(8,128)S(1)}, u32[]{:S(2)}, u32[]{:S(2)}) collective-permute-start(f32[72,16,128]{2,1,0:T(8,128)S(1)} %get-tuple-element.18), channel_id=1, source_target_pairs={{0,8},{8,0},{16,24},{24,16},{32,40},{40,32},{48,56},{56,48},{64,72... | collective-permute-start | bytes 1769480 | tf_op jit(solution)/shard_map/ppermute | solution.py:624
  12.1 3.4 %collective-permute-start.3 = (f32[48,16,128]{2,1,0:T(8,128)S(1)}, f32[48,16,128]{2,1,0:T(8,128)S(1)}, u32[]{:S(2)}, u32[]{:S(2)}) collective-permute-start(f32[48,16,128]{2,1,0:T(8,128)S(1)} %get-tuple-element.17), channel_id=1, source_target_pairs={{8,16},{16,8},{24,32},{32,24},{40,48},{48,40},{56,64},{64,56},{72,... | collective-permute-start | bytes 1179656 | tf_op jit(solution)/shard_map/ppermute | solution.py:623
  15.5 5.6 %collective-permute-done.3.far_ref = f32[48,16,128]{2,1,0:T(8,128)S(1)} collective-permute-done((f32[48,16,128]{2,1,0:T(8,128)S(1)}, f32[48,16,128]{2,1,0:T(8,128)S(1)}, u32[]{:S(2)}, u32[]{:S(2)}) %collective-permute-start.3) | collective-permute-done | bytes 393248 | tf_op jit(solution)/shard_map/ppermute | solution.py:623
  21.2 0.0 collective-permute-done.4.near_ref
  21.2 9.7 %main.1 = (f32[256,128]{1,0:T(8,128)S(1)}, f32[4,4,16,24,128]{4,3,2,1,0:T(8,128)S(1)}) custom-call(f32[5,16,16,128]{3,2,1,0:T(8,128)S(1)} %pad_maximum_fusion.held_ref.own_ref, f32[2,16,16,128]{3,2,1,0:T(8,128)S(1)} %collective-permute-done.other_ref, f32[8,16,128]{2,1,0:T(8,128)S(1)} %get-tuple-element.16.border_ref, ...), custom_call_target="tpu_custom_call" | custom-call | flops 50000000 | bytes 5242880 | tf_op jit(solution)/shard_map/main/pallas_call | solution.py:581
  30.8 31.9 %all_to_all.5 = f32[256,1,128]{2,1,0:T(1,128)S(1)} all-to-all(f32[256,1,128]{2,1,0:T(1,128)S(1)} %bitcast.8), channel_id=1, replica_groups=mesh['section'=2,'sx'=16,'sy'=8] {'section','sx','sy'}, dimensions={0} | all-to-all | bytes 262144 | tf_op jit(solution)/shard_map/all_to_all | solution.py:634
  62.7 0.7 send.1
  63.4 0.6 collective-permute-start.5
  64.0 0.2 mine.1.mine_ref
  64.2 5.3 %collective-permute-done.5.other_ref = f32[16,16,128]{2,1,0:T(8,128)S(1)} collective-permute-done((f32[16,16,128]{2,1,0:T(8,128)S(1)}, f32[16,16,128]{2,1,0:T(8,128)S(1)}, u32[]{:S(2)}, u32[]{:S(2)}) %collective-permute-start.5) | collective-permute-done | bytes 131104 | tf_op jit(solution)/shard_map/ppermute | solution.py:636
  69.4 0.8 %join.1 = f32[2,16,16,128]{3,2,1,0:T(8,128)} custom-call(f32[2,16,16,128]{3,2,1,0:T(8,128)S(1)} %mine.1.mine_ref, f32[16,16,128]{2,1,0:T(8,128)S(1)} %collective-permute-done.5.other_ref), custom_call_target="tpu_custom_call" | custom-call | flops 1000000 | bytes 655360 | tf_op jit(solution)/shard_map/join/pallas_call | solution.py:581
Async XLA Ops:
  0.0 9.7 %collective-permute-start = (f32[2,16,16,128]{3,2,1,0:T(8,128)}, f32[2,16,16,128]{3,2,1,0:T(8,128)S(1)}, u32[]{:S(2)}, u32[]{:S(2)}) collective-permute-start(f32[2,16,16,128]{3,2,1,0:T(8,128)} %param.5), channel_id=1, source_target_pairs={{0,128},{128,0},{1,129},{129,1},{2,130},{130,2},{3,131},{131,3},{4... | collective-permute-start | bytes 786440 | tf_op jit(solution)/shard_map/ppermute | solution.py:616
  5.3 4.4 %collective-permute-start.1 = (f32[8,16,128]{2,1,0:T(8,128)S(1)}, f32[8,16,128]{2,1,0:T(8,128)S(1)}, u32[]{:S(2)}, u32[]{:S(2)}) collective-permute-start(f32[8,16,128]{2,1,0:T(8,128)S(1)} %get-tuple-element.14), channel_id=1, source_target_pairs={{0,1},{1,2},{2,3},{3,4},{4,5},{5,6},{6,7},{129,128},{130,129},{131... | collective-permute-start | bytes 196616 | tf_op jit(solution)/shard_map/ppermute | solution.py:620
  8.4 1.3 %collective-permute-start.2 = (f32[8,16,128]{2,1,0:T(8,128)S(1)}, f32[8,16,128]{2,1,0:T(8,128)S(1)}, u32[]{:S(2)}, u32[]{:S(2)}) collective-permute-start(f32[8,16,128]{2,1,0:T(8,128)S(1)} %get-tuple-element.15), channel_id=1, source_target_pairs={{1,128},{2,129},{3,130},{4,131},{5,132},{6,133},{7,134},{128,1},{1... | collective-permute-start | bytes 196616 | tf_op jit(solution)/shard_map/ppermute | solution.py:621
  10.2 11.0 %collective-permute-start.4 = (f32[72,16,128]{2,1,0:T(8,128)S(1)}, f32[72,16,128]{2,1,0:T(8,128)S(1)}, u32[]{:S(2)}, u32[]{:S(2)}) collective-permute-start(f32[72,16,128]{2,1,0:T(8,128)S(1)} %get-tuple-element.18), channel_id=1, source_target_pairs={{0,8},{8,0},{16,24},{24,16},{32,40},{40,32},{48,56},{56,48},{64,72... | collective-permute-start | bytes 1769480 | tf_op jit(solution)/shard_map/ppermute | solution.py:624
  12.1 9.1 %collective-permute-start.3 = (f32[48,16,128]{2,1,0:T(8,128)S(1)}, f32[48,16,128]{2,1,0:T(8,128)S(1)}, u32[]{:S(2)}, u32[]{:S(2)}) collective-permute-start(f32[48,16,128]{2,1,0:T(8,128)S(1)} %get-tuple-element.17), channel_id=1, source_target_pairs={{8,16},{16,8},{24,32},{32,24},{40,48},{48,40},{56,64},{64,56},{72,... | collective-permute-start | bytes 1179656 | tf_op jit(solution)/shard_map/ppermute | solution.py:623
  63.4 6.1 %collective-permute-start.5 = (f32[16,16,128]{2,1,0:T(8,128)S(1)}, f32[16,16,128]{2,1,0:T(8,128)S(1)}, u32[]{:S(2)}, u32[]{:S(2)}) collective-permute-start(f32[16,16,128]{2,1,0:T(8,128)S(1)} %get-tuple-element.22), channel_id=1, source_target_pairs={{0,128},{128,0},{1,129},{129,1},{2,130},{130,2},{3,131},{131,3},{4... | collective-permute-start | bytes 393224 | tf_op jit(solution)/shard_map/ppermute | solution.py:636

commit v12 on v11

--- a/solution.py
+++ b/solution.py
@@ -213,8 +213,36 @@
     return jnp.where(left_half(), LANES // 2, LANES // 2 - EDGE)
 
 
-def own_kernel(held_ref, same_ref, cross_ref):
+def pack_far(far_ref, load, fields, base, plane, nz):
+    even = on_even_row()
+    half = nz // 2
+    pairs = (len(fields) + 1) // 2
+    window, end = jnp.zeros((8, LANES), jnp.float32), jnp.zeros((1, LANES), jnp.float32)
+    for part in range(2):
+        z = part * half + plane
+        rows, ninths = [], []
+        for slot, f in enumerate(fields):
+            cell = load(slot, z)
+            nx = cell.shape[0]
+            rows.append(jnp.where(even, cell[0:8], cell[nx - 8 : nx]))
+            ninths.append(jnp.where(even, cell[8:9], cell[nx - 9 : nx - 8]))
+            at = part * 64 + f * EDGE
+            window = put(window, rows[-1], at, inner_start(), lane_ids(8))
+            end = put(end, ninths[-1], at, inner_start(), lane_ids(1))
+        for pair in range(pairs):
+            first, second = 2 * pair, min(2 * pair + 1, len(fields) - 1)
+            far_ref[pairs * z + pair] = jnp.where(half_mask(8), rows[first], turn(rows[second], LANES // 2))
+            row = part * pairs + pair
+            far_ref[base + plane, row : row + 1] = jnp.where(half_mask(1), ninths[first], turn(ninths[second], LANES // 2))
+    far_ref[base + plane, 7:8] = end
+    far_ref[base + half + plane] = window
+
+
+def own_kernel(held_ref, same_ref, cross_ref, far_ref):
     nz, nx = held_ref.shape[1], held_ref.shape[2]
+    load = lambda slot, z: held_ref[slot, z]
+    for plane in range(nz // 2):
+        pack_far(far_ref, load, ORDER[:5], 3 * nz, plane, nz)
     lanes = lane_ids(nx)
     incoming = border_start()
     outgoing = LANES - EDGE - incoming
@@ -236,36 +264,20 @@
 def rows_kernel(held_ref, other_ref, same_ref, cross_ref, border_ref, near_ref, far_ref):
     nz, nx = other_ref.shape[1], other_ref.shape[2]
     even = on_even_row()
-    inner = inner_start()
-    half = nz // 2
-    for plane in range(half):
-        inner_rows, inner_ninth = jnp.zeros((8, LANES), jnp.float32), jnp.zeros((1, LANES), jnp.float32)
-        for part in range(2):
-            z = part * half + plane
-            rows, ninths = [], []
-            for slot, f in enumerate(ORDER):
-                cell = held_ref[slot, z] if slot < 5 else other_ref[slot - 5, z]
-                entry, row, last, ninth = place(slot, z)
-                near_ref[entry, row : row + 8] = jnp.where(even, cell[nx - 8 : nx], cell[0:8])
-                near_ref[last, ninth : ninth + 1] = jnp.where(even, cell[nx - 9 : nx - 8], cell[8:9])
-                rows.append(jnp.where(even, cell[0:8], cell[nx - 8 : nx]))
-                ninths.append(jnp.where(even, cell[8:9], cell[nx - 9 : nx - 8]))
-                at = part * 64 + f * EDGE
-                inner_rows = put(inner_rows, rows[-1], at, inner, lane_ids(8))
-                inner_ninth = put(inner_ninth, ninths[-1], at, inner, lane_ids(1))
-            for pair in range(4):
-                first, second = 2 * pair, min(2 * pair + 1, 6)
-                top = 8 * (pair % 2)
-                far_ref[2 * z + pair // 2, top : top + 8] = jnp.where(half_mask(8), rows[first], turn(rows[second], LANES // 2))
-                row = 4 * part + pair
-                far_ref[2 * nz + plane, row : row + 1] = jnp.where(half_mask(1), ninths[first], turn(ninths[second], LANES // 2))
+    for z in range(nz):
+        for slot in range(7):
+            cell = held_ref[slot, z] if slot < 5 else other_ref[slot - 5, z]
+            entry, row, last, ninth = place(slot, z)
+            near_ref[entry, row : row + 8] = jnp.where(even, cell[nx - 8 : nx], cell[0:8])
+            near_ref[last, ninth : ninth + 1] = jnp.where(even, cell[nx - 9 : nx - 8], cell[8:9])
+    load = lambda slot, z: other_ref[slot, z]
+    for plane in range(nz // 2):
+        pack_far(far_ref, load, ORDER[5:], nz, plane, nz)
         border = same_ref[plane] + cross_ref[plane]
         border_ref[plane] = border
         near_ref[nz * PARTS + plane] = border
-        far_ref[2 * nz + plane, 8:9] = jnp.where(even, border[8:9], border[nx - 9 : nx - 8])
-        far_ref[2 * nz + plane, 9:10] = inner_ninth
-        far_ref[2 * nz + half + plane, 0:8] = jnp.where(even, border[0:8], border[nx - 8 : nx])
-        far_ref[2 * nz + half + plane, 8:16] = inner_rows
+        far_ref[nz + plane, 6:7] = jnp.where(even, border[8:9], border[nx - 9 : nx - 8])
+        far_ref[2 * nz + plane] = jnp.where(even, border[0:8], border[nx - 8 : nx])
 
 
 ROWS = 48
@@ -286,7 +298,7 @@
     lax.fori_loop(0, count // unroll, group, 0)
 
 
-def main_kernel(consts, held_ref, other_ref, border_ref, far_ref, near_ref, part_ref, sums_ref,
+def main_kernel(consts, held_ref, other_ref, border_ref, own_far_ref, far_ref, near_ref, part_ref, sums_ref,
                 val, kap, frozen, prv, rea, dif, fx, fy, fz, alpha, beta, vec, ya, yb, table):
     eigen_basis, basis_inverse, shift_rows, pairs = consts
     nz, nx = held_ref.shape[1], held_ref.shape[2]
@@ -316,8 +328,7 @@
 
     def assemble(plane):
         near_side = near_ref[nz * PARTS + plane]
-        ends, window = 2 * nz + plane, 2 * nz + nz // 2 + plane
-        far_side, far_end = far_ref[window, 0:8], far_ref[ends, 8:9]
+        far_side, far_end = far_ref[2 * nz + plane], far_ref[nz + plane, 6:7]
         sides = jnp.concatenate(
             [
                 tile(jnp.where(even, far_end, near_side[nx - 9 : nx - 8])), jnp.where(even, far_side, near_side[nx - 8 : nx]),
@@ -335,10 +346,13 @@
                 at = part * 64 + f * EDGE
                 entry, row, last, ninth = place(slot, z)
                 near, near_end = near_ref[entry, row : row + 8], near_ref[last, ninth : ninth + 1]
-                pair, second = divmod(slot, 2)
-                top, end = 8 * (pair % 2), 4 * part + pair
-                far = unpack(far_ref[2 * z + pair // 2, top : top + 8], far_ref[window, 8:16], second, at)
-                far_end = unpack(far_ref[ends, end : end + 1], far_ref[ends, 9:10], second, at)
+                if slot < 5:
+                    ref, pairs, base, (pair, second) = own_far_ref, 3, 3 * nz, divmod(slot, 2)
+                else:
+                    ref, pairs, base, pair, second = far_ref, 1, nz, 0, slot - 5
+                end = part * pairs + pair
+                far = unpack(ref[pairs * z + pair], ref[base + nz // 2 + plane], second, at)
+                far_end = unpack(ref[base + plane, end : end + 1], ref[base + plane, 7:8], second, at)
                 low, high = jnp.where(even, far, near), jnp.where(even, near, far)
                 low_end, high_end = jnp.where(even, far_end, near_end), jnp.where(even, near_end, far_end)
                 cells = jnp.concatenate([tile(low_end), low, mid, high, tile(high_end)], 0)
@@ -614,12 +628,14 @@
     axes = ("section", "sx", "sy")
     partner = [(0, 1), (1, 0)]
     other = lax.ppermute(sections, "section", partner)
-    edge, whole, thin = (nz // 2, nx, ny), (nz * PARTS + nz // 2, TALL, ny), (3 * nz, TALL, ny)
+    edge, whole, early, late = (nz // 2, nx, ny), (nz * PARTS + nz // 2, TALL, ny), (4 * nz, 8, ny), (2 * nz + nz // 2, 8, ny)
     held = jnp.concatenate([sections, previous[None], diffusivity[None], reaction[None]], 0)
-    same, cross = call(own_kernel, [edge, edge], name="own")(held)
+    same, cross, own_far = call(own_kernel, [edge, edge, early], name="own")(held)
+    own_far = lax.ppermute(own_far, "sx", swaps(rows, 1))
     same = lax.ppermute(same, ("section", "sy"), beside(columns, False))
     cross = lax.ppermute(cross, ("section", "sy"), beside(columns, True))
-    border, near, far = call(rows_kernel, [edge, whole, thin], name="rows")(held, other, same, cross)
+    cross, own_far = lax.optimization_barrier((cross, own_far))
+    border, near, far = call(rows_kernel, [edge, whole, late], name="rows")(held, other, same, cross)
     far = lax.ppermute(far, "sx", swaps(rows, 1))
     near = lax.ppermute(near, "sx", swaps(rows, 0))
     peers = 2 * columns * rows
@@ -630,7 +646,7 @@
     ]
     part, sums = call(
         functools.partial(main_kernel, consts), [(peers, LANES), (ITERS, 4, nz, nx + 8, ny)], scratch, 50_000_000, "main", 26
-    )(held, other, border, far, near)
+    )(held, other, border, own_far, far, near)
     total = lax.all_to_all(part.reshape(peers, 1, LANES), axes, 0, 0).reshape(peers, LANES)
     half, weight = call(functools.partial(send_kernel, consts), [previous.shape, (2 * ITERS, LANES)], name="send")(total, sums, other)
     got = lax.ppermute(half, "section", partner)

time: 70.4 us -> 70.6 us (level)
  starting transfers between devices: 13.5 us -> 17.4 us
  blocking collectives: 31.9 us -> 29.1 us
  waiting for transfers between devices: 11.5 us -> 10.4 us
    ppermute x0 -> x1, starting transfers between devices: none -> 4.94 us  [body(): own_far = lax.ppermute(own_far, 'sx', swaps(rows, 1))]
    all_to_all x1, blocking collectives: 31.9 us -> 29.1 us  [body(): lax.all_to_all(part.reshape(peers, 1, LANES), axes, 0, 0)]
    ppermute x1, waiting for transfers between devices: 5.63 us -> 3.24 us  [body(): far = lax.ppermute(far, 'sx', swaps(rows, 1))]
    ppermute x1, starting transfers between devices: 1.9 us -> 0.49 us  [body(): near = lax.ppermute(near, 'sx', swaps(rows, 0))]
    ppermute x1, starting transfers between devices: 3.12 us -> 4.39 us  [body(): same = lax.ppermute(same, ('section', 'sy'), beside(columns, False))]
    ppermute x1, waiting for transfers between devices: 0.64 us -> 1.86 us  [body(): same = lax.ppermute(same, ('section', 'sy'), beside(columns, False))]
    ppermute x1, starting transfers between devices: 3.74 us -> 3 us  [body(): other = lax.ppermute(sections, 'section', partner)]
  transfers between devices with their start and end apart: 6 -> 7, of which waited for: 3 -> 3; matrix products, arithmetic and copies ran while one was open for 2% -> 0% of each run, Pallas kernels for 1% -> 0%
where the time goes in v12:
time: 70.6 us; the launch traced here: 70.3 us
  blocking collectives  29.1 us (41%)
  starting transfers between devices  17.4 us (25%)
  Pallas kernels  12.2 us (17%)
  waiting for transfers between devices  10.4 us (15%)
  other arithmetic  1.2 us (2%)
    all_to_all x1, blocking collectives, body(): lax.all_to_all(part.reshape(peers, 1, LANES), axes, 0, 0)  29.1 us
    pallas_call x6, Pallas kernels, run(): pl.pallas_call(kernel, out_shape=shapes if many else shapes[0], in_specs=...  12.2 us
    ppermute x1, waiting for transfers between devices, body(): got = lax.ppermute(half, 'section', partner)  5.26 us
    ppermute x1, starting transfers between devices, body(): own_far = lax.ppermute(own_far, 'sx', swaps(rows, 1))  4.94 us
    ppermute x1, starting transfers between devices, body(): same = lax.ppermute(same, ('section', 'sy'), beside(columns, False))  4.39 us
    ppermute x1, starting transfers between devices, body(): far = lax.ppermute(far, 'sx', swaps(rows, 1))  3.37 us
    ppermute x1, waiting for transfers between devices, body(): far = lax.ppermute(far, 'sx', swaps(rows, 1))  3.24 us
    ppermute x1, starting transfers between devices, body(): other = lax.ppermute(sections, 'section', partner)  3 us
  transfers between devices with their start and end apart: 7, of which 3 were waited for; matrix products, arithmetic and copies ran while one was open for 0% of the time, Pallas kernels for 0%

profile of v12, /device:TPU:1, one launch (start us, length us, event | category | flops | bytes accessed | tf_op | source)
XLA Modules:
  0.0 70.3 jit_solution(11862510068904873978)
XLA Ops:
  0.0 1.2 %pad_maximum_fusion.held_ref.own_ref = f32[5,16,16,128]{3,2,1,0:T(8,128)S(1)} fusion(f32[1,16,16,128]{3,2,1,0:T(8,128)} %bitcast.9, f32[1,16,16,128]{3,2,1,0:T(8,128)} %bitcast.10, f32[1,16,16,128]{3,2,1,0:T(8,128)} %bitcast.11, f32[2,16,16,128]{3,2,1,0:T(8,128)} %param.5), kind=kLoop, calls=%fused_computation | loop fusion | flops 491520 | bytes 1310720 | tf_op jit(solution)/shard_map/concatenate | solution.py:632
  1.2 0.6 own.1
  1.8 4.9 %collective-permute-start.3 = (f32[64,8,128]{2,1,0:T(8,128)S(1)}, f32[64,8,128]{2,1,0:T(8,128)S(1)}, u32[]{:S(2)}, u32[]{:S(2)}) collective-permute-start(f32[64,8,128]{2,1,0:T(8,128)S(1)} %get-tuple-element.19), channel_id=1, source_target_pairs={{8,16},{16,8},{24,32},{32,24},{40,48},{48,40},{56,64},{64,56},{72,... | collective-permute-start | bytes 786440 | tf_op jit(solution)/shard_map/ppermute | solution.py:634
  6.7 3.0 %collective-permute-start = (f32[2,16,16,128]{3,2,1,0:T(8,128)}, f32[2,16,16,128]{3,2,1,0:T(8,128)S(1)}, u32[]{:S(2)}, u32[]{:S(2)}) collective-permute-start(f32[2,16,16,128]{3,2,1,0:T(8,128)} %param.5), channel_id=1, source_target_pairs={{0,128},{128,0},{1,129},{129,1},{2,130},{130,2},{3,131},{131,3},{4... | collective-permute-start | bytes 786440 | tf_op jit(solution)/shard_map/ppermute | solution.py:630
  9.7 0.7 collective-permute-start.2
  10.4 4.4 %collective-permute-start.1 = (f32[8,16,128]{2,1,0:T(8,128)S(1)}, f32[8,16,128]{2,1,0:T(8,128)S(1)}, u32[]{:S(2)}, u32[]{:S(2)}) collective-permute-start(f32[8,16,128]{2,1,0:T(8,128)S(1)} %get-tuple-element.17), channel_id=1, source_target_pairs={{0,1},{1,2},{2,3},{3,4},{4,5},{5,6},{6,7},{129,128},{130,129},{131... | collective-permute-start | bytes 196616 | tf_op jit(solution)/shard_map/ppermute | solution.py:635
  14.8 0.0 collective-permute-done.2.cross_ref
  14.8 0.0 collective-permute-done.3.own_far_ref
  14.8 1.9 %collective-permute-done.1.same_ref = f32[8,16,128]{2,1,0:T(8,128)S(1)} collective-permute-done((f32[8,16,128]{2,1,0:T(8,128)S(1)}, f32[8,16,128]{2,1,0:T(8,128)S(1)}, u32[]{:S(2)}, u32[]{:S(2)}) %collective-permute-start.1) | collective-permute-done | bytes 65568 | tf_op jit(solution)/shard_map/ppermute | solution.py:635
  16.7 0.0 collective-permute-done.other_ref
  16.7 0.2 rows.1
  16.9 0.5 collective-permute-start.5
  17.4 3.4 %collective-permute-start.4 = (f32[40,8,128]{2,1,0:T(8,128)S(1)}, f32[40,8,128]{2,1,0:T(8,128)S(1)}, u32[]{:S(2)}, u32[]{:S(2)}) collective-permute-start(f32[40,8,128]{2,1,0:T(8,128)S(1)} %get-tuple-element.23), channel_id=1, source_target_pairs={{8,16},{16,8},{24,32},{32,24},{40,48},{48,40},{56,64},{64,56},{72,... | collective-permute-start | bytes 491528 | tf_op jit(solution)/shard_map/ppermute | solution.py:639
  20.8 3.2 %collective-permute-done.4.far_ref = f32[40,8,128]{2,1,0:T(8,128)S(1)} collective-permute-done((f32[40,8,128]{2,1,0:T(8,128)S(1)}, f32[40,8,128]{2,1,0:T(8,128)S(1)}, u32[]{:S(2)}, u32[]{:S(2)}) %collective-permute-start.4) | collective-permute-done | bytes 163872 | tf_op jit(solution)/shard_map/ppermute | solution.py:639
  24.0 0.0 collective-permute-done.5.near_ref
  24.0 9.7 %main.1 = (f32[256,128]{1,0:T(8,128)S(1)}, f32[4,4,16,24,128]{4,3,2,1,0:T(8,128)S(1)}) custom-call(f32[5,16,16,128]{3,2,1,0:T(8,128)S(1)} %pad_maximum_fusion.held_ref.own_ref, f32[2,16,16,128]{3,2,1,0:T(8,128)S(1)} %collective-permute-done.other_ref, f32[8,16,128]{2,1,0:T(8,128)S(1)} %get-tuple-element.21.border_ref, ...), custom_call_target="tpu_custom_call" | custom-call | flops 50000000 | bytes 5275648 | tf_op jit(solution)/shard_map/main/pallas_call | solution.py:595
  33.7 29.1 %all_to_all.5 = f32[256,1,128]{2,1,0:T(1,128)S(1)} all-to-all(f32[256,1,128]{2,1,0:T(1,128)S(1)} %bitcast.8), channel_id=1, replica_groups=mesh['section'=2,'sx'=16,'sy'=8] {'section','sx','sy'}, dimensions={0} | all-to-all | bytes 262144 | tf_op jit(solution)/shard_map/all_to_all | solution.py:650
  62.8 0.7 send.1
  63.5 0.6 collective-permute-start.6
  64.1 0.2 mine.1.mine_ref
  64.3 5.3 %collective-permute-done.6.other_ref = f32[16,16,128]{2,1,0:T(8,128)S(1)} collective-permute-done((f32[16,16,128]{2,1,0:T(8,128)S(1)}, f32[16,16,128]{2,1,0:T(8,128)S(1)}, u32[]{:S(2)}, u32[]{:S(2)}) %collective-permute-start.6) | collective-permute-done | bytes 131104 | tf_op jit(solution)/shard_map/ppermute | solution.py:652
  69.5 0.8 %join.1 = f32[2,16,16,128]{3,2,1,0:T(8,128)} custom-call(f32[2,16,16,128]{3,2,1,0:T(8,128)S(1)} %mine.1.mine_ref, f32[16,16,128]{2,1,0:T(8,128)S(1)} %collective-permute-done.6.other_ref), custom_call_target="tpu_custom_call" | custom-call | flops 1000000 | bytes 655360 | tf_op jit(solution)/shard_map/join/pallas_call | solution.py:595
Async XLA Ops:
  1.8 13.0 %collective-permute-start.3 = (f32[64,8,128]{2,1,0:T(8,128)S(1)}, f32[64,8,128]{2,1,0:T(8,128)S(1)}, u32[]{:S(2)}, u32[]{:S(2)}) collective-permute-start(f32[64,8,128]{2,1,0:T(8,128)S(1)} %get-tuple-element.19), channel_id=1, source_target_pairs={{8,16},{16,8},{24,32},{32,24},{40,48},{48,40},{56,64},{64,56},{72,... | collective-permute-start | bytes 786440 | tf_op jit(solution)/shard_map/ppermute | solution.py:634
  6.7 9.9 %collective-permute-start = (f32[2,16,16,128]{3,2,1,0:T(8,128)}, f32[2,16,16,128]{3,2,1,0:T(8,128)S(1)}, u32[]{:S(2)}, u32[]{:S(2)}) collective-permute-start(f32[2,16,16,128]{3,2,1,0:T(8,128)} %param.5), channel_id=1, source_target_pairs={{0,128},{128,0},{1,129},{129,1},{2,130},{130,2},{3,131},{131,3},{4... | collective-permute-start | bytes 786440 | tf_op jit(solution)/shard_map/ppermute | solution.py:630
  9.7 5.1 %collective-permute-start.2 = (f32[8,16,128]{2,1,0:T(8,128)S(1)}, f32[8,16,128]{2,1,0:T(8,128)S(1)}, u32[]{:S(2)}, u32[]{:S(2)}) collective-permute-start(f32[8,16,128]{2,1,0:T(8,128)S(1)} %get-tuple-element.18), channel_id=1, source_target_pairs={{1,128},{2,129},{3,130},{4,131},{5,132},{6,133},{7,134},{128,1},{1... | collective-permute-start | bytes 196616 | tf_op jit(solution)/shard_map/ppermute | solution.py:636
  10.4 6.3 %collective-permute-start.1 = (f32[8,16,128]{2,1,0:T(8,128)S(1)}, f32[8,16,128]{2,1,0:T(8,128)S(1)}, u32[]{:S(2)}, u32[]{:S(2)}) collective-permute-start(f32[8,16,128]{2,1,0:T(8,128)S(1)} %get-tuple-element.17), channel_id=1, source_target_pairs={{0,1},{1,2},{2,3},{3,4},{4,5},{5,6},{6,7},{129,128},{130,129},{131... | collective-permute-start | bytes 196616 | tf_op jit(solution)/shard_map/ppermute | solution.py:635
  16.9 7.1 %collective-permute-start.5 = (f32[72,16,128]{2,1,0:T(8,128)S(1)}, f32[72,16,128]{2,1,0:T(8,128)S(1)}, u32[]{:S(2)}, u32[]{:S(2)}) collective-permute-start(f32[72,16,128]{2,1,0:T(8,128)S(1)} %get-tuple-element.24), channel_id=1, source_target_pairs={{0,8},{8,0},{16,24},{24,16},{32,40},{40,32},{48,56},{56,48},{64,72... | collective-permute-start | bytes 1769480 | tf_op jit(solution)/shard_map/ppermute | solution.py:640
  17.4 6.6 %collective-permute-start.4 = (f32[40,8,128]{2,1,0:T(8,128)S(1)}, f32[40,8,128]{2,1,0:T(8,128)S(1)}, u32[]{:S(2)}, u32[]{:S(2)}) collective-permute-start(f32[40,8,128]{2,1,0:T(8,128)S(1)} %get-tuple-element.23), channel_id=1, source_target_pairs={{8,16},{16,8},{24,32},{32,24},{40,48},{48,40},{56,64},{64,56},{72,... | collective-permute-start | bytes 491528 | tf_op jit(solution)/shard_map/ppermute | solution.py:639
  63.5 6.1 %collective-permute-start.6 = (f32[16,16,128]{2,1,0:T(8,128)S(1)}, f32[16,16,128]{2,1,0:T(8,128)S(1)}, u32[]{:S(2)}, u32[]{:S(2)}) collective-permute-start(f32[16,16,128]{2,1,0:T(8,128)S(1)} %get-tuple-element.28), channel_id=1, source_target_pairs={{0,128},{128,0},{1,129},{129,1},{2,130},{130,2},{3,131},{131,3},{4... | collective-permute-start | bytes 393224 | tf_op jit(solution)/shard_map/ppermute | solution.py:652

commit v13 on v12

--- a/solution.py
+++ b/solution.py
@@ -213,6 +213,15 @@
     return jnp.where(left_half(), LANES // 2, LANES // 2 - EDGE)
 
 
+def unpack(cells, window, second, at):
+    count = cells.shape[0]
+    inner = inner_start()
+    ids = lane_ids(count)
+    cells = turn(cells, LANES // 2) if second else cells
+    window = pltpu.roll(window, lax.rem(inner + LANES - at, LANES), 1)
+    return jnp.where(half_mask(count), cells, jnp.where((ids >= inner) & (ids < inner + EDGE), window, 0.0))
+
+
 def pack_far(far_ref, load, fields, base, plane, nz):
     even = on_even_row()
     half = nz // 2
@@ -238,11 +247,21 @@
     far_ref[base + half + plane] = window
 
 
-def own_kernel(held_ref, same_ref, cross_ref, far_ref):
+def own_kernel(held_ref, same_ref, cross_ref, far_ref, swap_ref):
     nz, nx = held_ref.shape[1], held_ref.shape[2]
     load = lambda slot, z: held_ref[slot, z]
     for plane in range(nz // 2):
         pack_far(far_ref, load, ORDER[:5], 3 * nz, plane, nz)
+    quarter = nz // 4
+    theirs = LANES - EDGE - inner_start()
+    for plane in range(quarter):
+        window = jnp.zeros((nx, LANES), jnp.float32)
+        for part in range(4):
+            z = part * quarter + plane
+            swap_ref[z] = jnp.where(half_mask(nx), turn(held_ref[1, z], LANES // 2), held_ref[0, z])
+            for slot in range(2):
+                window = put(window, held_ref[slot, z], part * 32 + slot * EDGE, theirs, lane_ids(nx))
+        swap_ref[nz + plane] = window
     lanes = lane_ids(nx)
     incoming = border_start()
     outgoing = LANES - EDGE - incoming
@@ -261,15 +280,22 @@
         cross_ref[plane] = cross
 
 
-def rows_kernel(held_ref, other_ref, same_ref, cross_ref, border_ref, near_ref, far_ref):
+def rows_kernel(held_ref, got_ref, same_ref, cross_ref, other_ref, border_ref, near_ref, far_ref):
     nz, nx = other_ref.shape[1], other_ref.shape[2]
     even = on_even_row()
+    quarter = nz // 4
     for z in range(nz):
+        part, plane = divmod(z, quarter)
+        fresh = [
+            unpack(got_ref[z], got_ref[nz + plane], slot == 1, part * 32 + slot * EDGE) for slot in range(2)
+        ]
         for slot in range(7):
-            cell = held_ref[slot, z] if slot < 5 else other_ref[slot - 5, z]
+            cell = held_ref[slot, z] if slot < 5 else fresh[slot - 5]
             entry, row, last, ninth = place(slot, z)
             near_ref[entry, row : row + 8] = jnp.where(even, cell[nx - 8 : nx], cell[0:8])
             near_ref[last, ninth : ninth + 1] = jnp.where(even, cell[nx - 9 : nx - 8], cell[8:9])
+        other_ref[0, z] = fresh[0]
+        other_ref[1, z] = fresh[1]
     load = lambda slot, z: other_ref[slot, z]
     for plane in range(nz // 2):
         pack_far(far_ref, load, ORDER[5:], nz, plane, nz)
@@ -316,15 +342,6 @@
         for f in range(4):
             for ref in (val, kap, ya, yb):
                 ref[f, at] = zero_plane
-
-    inner = inner_start()
-
-    def unpack(cells, window, second, at):
-        count = cells.shape[0]
-        ids = lane_ids(count)
-        cells = turn(cells, LANES // 2) if second else cells
-        window = pltpu.roll(window, lax.rem(inner + LANES - at, LANES), 1)
-        return jnp.where(half_mask(count), cells, jnp.where((ids >= inner) & (ids < inner + EDGE), window, 0.0))
 
     def assemble(plane):
         near_side = near_ref[nz * PARTS + plane]
@@ -627,15 +644,15 @@
     columns, rows = lax.axis_size("sy"), lax.axis_size("sx")
     axes = ("section", "sx", "sy")
     partner = [(0, 1), (1, 0)]
-    other = lax.ppermute(sections, "section", partner)
     edge, whole, early, late = (nz // 2, nx, ny), (nz * PARTS + nz // 2, TALL, ny), (4 * nz, 8, ny), (2 * nz + nz // 2, 8, ny)
     held = jnp.concatenate([sections, previous[None], diffusivity[None], reaction[None]], 0)
-    same, cross, own_far = call(own_kernel, [edge, edge, early], name="own")(held)
+    same, cross, own_far, half = call(own_kernel, [edge, edge, early, (nz + nz // 4, nx, ny)], name="own")(held)
+    half = lax.ppermute(half, "section", partner)
     own_far = lax.ppermute(own_far, "sx", swaps(rows, 1))
     same = lax.ppermute(same, ("section", "sy"), beside(columns, False))
     cross = lax.ppermute(cross, ("section", "sy"), beside(columns, True))
     cross, own_far = lax.optimization_barrier((cross, own_far))
-    border, near, far = call(rows_kernel, [edge, whole, late], name="rows")(held, other, same, cross)
+    other, border, near, far = call(rows_kernel, [sections.shape, edge, whole, late], name="rows")(held, half, same, cross)
     far = lax.ppermute(far, "sx", swaps(rows, 1))
     near = lax.ppermute(near, "sx", swaps(rows, 0))
     peers = 2 * columns * rows

time: 70.6 us -> 70.8 us (level)
  no operation moved by 1% of the time
where the time goes in v13:
time: 70.8 us; the launch traced here: 70.6 us
  blocking collectives  29.1 us (41%)
  starting transfers between devices  17.1 us (24%)
  Pallas kernels  12.4 us (18%)
  waiting for transfers between devices  10.7 us (15%)
  other arithmetic  1.2 us (2%)
    all_to_all x1, blocking collectives, body(): lax.all_to_all(part.reshape(peers, 1, LANES), axes, 0, 0)  29.1 us
    pallas_call x6, Pallas kernels, run(): pl.pallas_call(kernel, out_shape=shapes if many else shapes[0], in_specs=...  12.4 us
    ppermute x1, waiting for transfers between devices, body(): got = lax.ppermute(half, 'section', partner)  5.26 us
    ppermute x1, starting transfers between devices, body(): own_far = lax.ppermute(own_far, 'sx', swaps(rows, 1))  4.94 us
    ppermute x1, starting transfers between devices, body(): same = lax.ppermute(same, ('section', 'sy'), beside(columns, False))  4.39 us
    ppermute x1, waiting for transfers between devices, body(): far = lax.ppermute(far, 'sx', swaps(rows, 1))  3.57 us
    ppermute x1, starting transfers between devices, body(): far = lax.ppermute(far, 'sx', swaps(rows, 1))  3.04 us
    ppermute x1, starting transfers between devices, body(): half = lax.ppermute(half, 'section', partner)  3 us
  transfers between devices with their start and end apart: 7, of which 3 were waited for; matrix products, arithmetic and copies ran while one was open for 0% of the time, Pallas kernels for 0%

profile of v13, /device:TPU:1, one launch (start us, length us, event | category | flops | bytes accessed | tf_op | source)
XLA Modules:
  0.0 70.6 jit_solution(13313523780973462089)
XLA Ops:
  0.0 1.2 %pad_maximum_fusion.held_ref.own_ref = f32[5,16,16,128]{3,2,1,0:T(8,128)S(1)} fusion(f32[1,16,16,128]{3,2,1,0:T(8,128)} %bitcast.9, f32[1,16,16,128]{3,2,1,0:T(8,128)} %bitcast.10, f32[1,16,16,128]{3,2,1,0:T(8,128)} %bitcast.11, f32[2,16,16,128]{3,2,1,0:T(8,128)} %param.5), kind=kLoop, calls=%fused_computation | loop fusion | flops 491520 | bytes 1310720 | tf_op jit(solution)/shard_map/concatenate | solution.py:648
  1.2 0.7 own.1
  1.9 4.9 %collective-permute-start.3 = (f32[64,8,128]{2,1,0:T(8,128)S(1)}, f32[64,8,128]{2,1,0:T(8,128)S(1)}, u32[]{:S(2)}, u32[]{:S(2)}) collective-permute-start(f32[64,8,128]{2,1,0:T(8,128)S(1)} %get-tuple-element.22), channel_id=1, source_target_pairs={{8,16},{16,8},{24,32},{32,24},{40,48},{48,40},{56,64},{64,56},{72,... | collective-permute-start | bytes 786440 | tf_op jit(solution)/shard_map/ppermute | solution.py:651
  6.8 3.0 %collective-permute-start = (f32[20,16,128]{2,1,0:T(8,128)S(1)}, f32[20,16,128]{2,1,0:T(8,128)S(1)}, u32[]{:S(2)}, u32[]{:S(2)}) collective-permute-start(f32[20,16,128]{2,1,0:T(8,128)S(1)} %get-tuple-element.19), channel_id=1, source_target_pairs={{0,128},{128,0},{1,129},{129,1},{2,130},{130,2},{3,131},{131,3},{4... | collective-permute-start | bytes 491528 | tf_op jit(solution)/shard_map/ppermute | solution.py:650
  9.8 0.7 collective-permute-start.2
  10.5 4.4 %collective-permute-start.1 = (f32[8,16,128]{2,1,0:T(8,128)S(1)}, f32[8,16,128]{2,1,0:T(8,128)S(1)}, u32[]{:S(2)}, u32[]{:S(2)}) collective-permute-start(f32[8,16,128]{2,1,0:T(8,128)S(1)} %get-tuple-element.20), channel_id=1, source_target_pairs={{0,1},{1,2},{2,3},{3,4},{4,5},{5,6},{6,7},{129,128},{130,129},{131... | collective-permute-start | bytes 196616 | tf_op jit(solution)/shard_map/ppermute | solution.py:652
  14.9 0.0 collective-permute-done.2.cross_ref
  14.9 0.0 collective-permute-done.3.own_far_ref
  14.9 1.9 %collective-permute-done.1.same_ref = f32[8,16,128]{2,1,0:T(8,128)S(1)} collective-permute-done((f32[8,16,128]{2,1,0:T(8,128)S(1)}, f32[8,16,128]{2,1,0:T(8,128)S(1)}, u32[]{:S(2)}, u32[]{:S(2)}) %collective-permute-start.1) | collective-permute-done | bytes 65568 | tf_op jit(solution)/shard_map/ppermute | solution.py:652
  16.8 0.0 collective-permute-done.got_ref
  16.8 0.3 rows.1
  17.1 0.5 collective-permute-start.5
  17.6 3.0 %collective-permute-start.4 = (f32[40,8,128]{2,1,0:T(8,128)S(1)}, f32[40,8,128]{2,1,0:T(8,128)S(1)}, u32[]{:S(2)}, u32[]{:S(2)}) collective-permute-start(f32[40,8,128]{2,1,0:T(8,128)S(1)} %get-tuple-element.27), channel_id=1, source_target_pairs={{8,16},{16,8},{24,32},{32,24},{40,48},{48,40},{56,64},{64,56},{72,... | collective-permute-start | bytes 491528 | tf_op jit(solution)/shard_map/ppermute | solution.py:656
  20.6 3.6 %collective-permute-done.4.far_ref = f32[40,8,128]{2,1,0:T(8,128)S(1)} collective-permute-done((f32[40,8,128]{2,1,0:T(8,128)S(1)}, f32[40,8,128]{2,1,0:T(8,128)S(1)}, u32[]{:S(2)}, u32[]{:S(2)}) %collective-permute-start.4) | collective-permute-done | bytes 163872 | tf_op jit(solution)/shard_map/ppermute | solution.py:656
  24.2 0.0 collective-permute-done.5.near_ref
  24.2 9.7 %main.1 = (f32[256,128]{1,0:T(8,128)S(1)}, f32[4,4,16,24,128]{4,3,2,1,0:T(8,128)S(1)}) custom-call(f32[5,16,16,128]{3,2,1,0:T(8,128)S(1)} %pad_maximum_fusion.held_ref.own_ref, f32[2,16,16,128]{3,2,1,0:T(8,128)S(1)} %get-tuple-element.24.other_ref, f32[8,16,128]{2,1,0:T(8,128)S(1)} %get-tuple-element.25.border_ref, ...), custom_call_target="tpu_custom_call" | custom-call | flops 50000000 | bytes 5275648 | tf_op jit(solution)/shard_map/main/pallas_call | solution.py:612
  33.9 29.1 %all_to_all.5 = f32[256,1,128]{2,1,0:T(1,128)S(1)} all-to-all(f32[256,1,128]{2,1,0:T(1,128)S(1)} %bitcast.8), channel_id=1, replica_groups=mesh['section'=2,'sx'=16,'sy'=8] {'section','sx','sy'}, dimensions={0} | all-to-all | bytes 262144 | tf_op jit(solution)/shard_map/all_to_all | solution.py:667
  63.0 0.7 send.1
  63.7 0.6 collective-permute-start.6
  64.3 0.2 mine.1.mine_ref
  64.5 5.3 %collective-permute-done.6.other_ref = f32[16,16,128]{2,1,0:T(8,128)S(1)} collective-permute-done((f32[16,16,128]{2,1,0:T(8,128)S(1)}, f32[16,16,128]{2,1,0:T(8,128)S(1)}, u32[]{:S(2)}, u32[]{:S(2)}) %collective-permute-start.6) | collective-permute-done | bytes 131104 | tf_op jit(solution)/shard_map/ppermute | solution.py:669
  69.8 0.8 %join.1 = f32[2,16,16,128]{3,2,1,0:T(8,128)} custom-call(f32[2,16,16,128]{3,2,1,0:T(8,128)S(1)} %mine.1.mine_ref, f32[16,16,128]{2,1,0:T(8,128)S(1)} %collective-permute-done.6.other_ref), custom_call_target="tpu_custom_call" | custom-call | flops 1000000 | bytes 655360 | tf_op jit(solution)/shard_map/join/pallas_call | solution.py:612
Async XLA Ops:
  1.9 13.0 %collective-permute-start.3 = (f32[64,8,128]{2,1,0:T(8,128)S(1)}, f32[64,8,128]{2,1,0:T(8,128)S(1)}, u32[]{:S(2)}, u32[]{:S(2)}) collective-permute-start(f32[64,8,128]{2,1,0:T(8,128)S(1)} %get-tuple-element.22), channel_id=1, source_target_pairs={{8,16},{16,8},{24,32},{32,24},{40,48},{48,40},{56,64},{64,56},{72,... | collective-permute-start | bytes 786440 | tf_op jit(solution)/shard_map/ppermute | solution.py:651
  6.8 9.9 %collective-permute-start = (f32[20,16,128]{2,1,0:T(8,128)S(1)}, f32[20,16,128]{2,1,0:T(8,128)S(1)}, u32[]{:S(2)}, u32[]{:S(2)}) collective-permute-start(f32[20,16,128]{2,1,0:T(8,128)S(1)} %get-tuple-element.19), channel_id=1, source_target_pairs={{0,128},{128,0},{1,129},{129,1},{2,130},{130,2},{3,131},{131,3},{4... | collective-permute-start | bytes 491528 | tf_op jit(solution)/shard_map/ppermute | solution.py:650
  9.8 5.1 %collective-permute-start.2 = (f32[8,16,128]{2,1,0:T(8,128)S(1)}, f32[8,16,128]{2,1,0:T(8,128)S(1)}, u32[]{:S(2)}, u32[]{:S(2)}) collective-permute-start(f32[8,16,128]{2,1,0:T(8,128)S(1)} %get-tuple-element.21), channel_id=1, source_target_pairs={{1,128},{2,129},{3,130},{4,131},{5,132},{6,133},{7,134},{128,1},{1... | collective-permute-start | bytes 196616 | tf_op jit(solution)/shard_map/ppermute | solution.py:653
  10.5 6.3 %collective-permute-start.1 = (f32[8,16,128]{2,1,0:T(8,128)S(1)}, f32[8,16,128]{2,1,0:T(8,128)S(1)}, u32[]{:S(2)}, u32[]{:S(2)}) collective-permute-start(f32[8,16,128]{2,1,0:T(8,128)S(1)} %get-tuple-element.20), channel_id=1, source_target_pairs={{0,1},{1,2},{2,3},{3,4},{4,5},{5,6},{6,7},{129,128},{130,129},{131... | collective-permute-start | bytes 196616 | tf_op jit(solution)/shard_map/ppermute | solution.py:652
  17.1 7.1 %collective-permute-start.5 = (f32[72,16,128]{2,1,0:T(8,128)S(1)}, f32[72,16,128]{2,1,0:T(8,128)S(1)}, u32[]{:S(2)}, u32[]{:S(2)}) collective-permute-start(f32[72,16,128]{2,1,0:T(8,128)S(1)} %get-tuple-element.28), channel_id=1, source_target_pairs={{0,8},{8,0},{16,24},{24,16},{32,40},{40,32},{48,56},{56,48},{64,72... | collective-permute-start | bytes 1769480 | tf_op jit(solution)/shard_map/ppermute | solution.py:657
  17.6 6.6 %collective-permute-start.4 = (f32[40,8,128]{2,1,0:T(8,128)S(1)}, f32[40,8,128]{2,1,0:T(8,128)S(1)}, u32[]{:S(2)}, u32[]{:S(2)}) collective-permute-start(f32[40,8,128]{2,1,0:T(8,128)S(1)} %get-tuple-element.27), channel_id=1, source_target_pairs={{8,16},{16,8},{24,32},{32,24},{40,48},{48,40},{56,64},{64,56},{72,... | collective-permute-start | bytes 491528 | tf_op jit(solution)/shard_map/ppermute | solution.py:656
  63.7 6.1 %collective-permute-start.6 = (f32[16,16,128]{2,1,0:T(8,128)S(1)}, f32[16,16,128]{2,1,0:T(8,128)S(1)}, u32[]{:S(2)}, u32[]{:S(2)}) collective-permute-start(f32[16,16,128]{2,1,0:T(8,128)S(1)} %get-tuple-element.32), channel_id=1, source_target_pairs={{0,128},{128,0},{1,129},{129,1},{2,130},{130,2},{3,131},{131,3},{4... | collective-permute-start | bytes 393224 | tf_op jit(solution)/shard_map/ppermute | solution.py:669

commit v14 on v12

--- a/solution.py
+++ b/solution.py
@@ -13,8 +13,8 @@
 LANES = 128
 SIZE = ITERS + 1
 PAIRS = [(i, j) for i in range(SIZE) for j in range(i, SIZE)]
-PREPARE_UNROLL = 2
-STEP_UNROLL = 8
+PREPARE_UNROLL = 4
+STEP_UNROLL = 16
 
 
 step_size = 1.0

time: 70.6 us -> 69.4 us (0.983)
  Pallas kernels: 12.2 us -> 11 us
    pallas_call x6, Pallas kernels: 12.2 us -> 11 us  [run(): pl.pallas_call(kernel, out_shape=shapes if many else shapes[0], in_specs=...]
where the time goes in v14:
time: 69.4 us; the launch traced here: 69.2 us
  blocking collectives  29.1 us (42%)
  starting transfers between devices  17.4 us (25%)
  Pallas kernels  11 us (16%)
  waiting for transfers between devices  10.4 us (15%)
  other arithmetic  1.2 us (2%)
    all_to_all x1, blocking collectives, body(): lax.all_to_all(part.reshape(peers, 1, LANES), axes, 0, 0)  29.1 us
    pallas_call x6, Pallas kernels, run(): pl.pallas_call(kernel, out_shape=shapes if many else shapes[0], in_specs=...  11 us
    ppermute x1, waiting for transfers between devices, body(): got = lax.ppermute(half, 'section', partner)  5.26 us
    ppermute x1, starting transfers between devices, body(): own_far = lax.ppermute(own_far, 'sx', swaps(rows, 1))  4.94 us
    ppermute x1, starting transfers between devices, body(): same = lax.ppermute(same, ('section', 'sy'), beside(columns, False))  4.39 us
    ppermute x1, starting transfers between devices, body(): far = lax.ppermute(far, 'sx', swaps(rows, 1))  3.37 us
    ppermute x1, waiting for transfers between devices, body(): far = lax.ppermute(far, 'sx', swaps(rows, 1))  3.24 us
    ppermute x1, starting transfers between devices, body(): other = lax.ppermute(sections, 'section', partner)  3 us
  transfers between devices with their start and end apart: 7, of which 3 were waited for; matrix products, arithmetic and copies ran while one was open for 0% of the time, Pallas kernels for 0%

profile of v14, /device:TPU:1, one launch (start us, length us, event | category | flops | bytes accessed | tf_op | source)
XLA Modules:
  0.0 69.2 jit_solution(11262447995699280442)
XLA Ops:
  0.0 1.2 %pad_maximum_fusion.held_ref.own_ref = f32[5,16,16,128]{3,2,1,0:T(8,128)S(1)} fusion(f32[1,16,16,128]{3,2,1,0:T(8,128)} %bitcast.9, f32[1,16,16,128]{3,2,1,0:T(8,128)} %bitcast.10, f32[1,16,16,128]{3,2,1,0:T(8,128)} %bitcast.11, f32[2,16,16,128]{3,2,1,0:T(8,128)} %param.5), kind=kLoop, calls=%fused_computation | loop fusion | flops 491520 | bytes 1310720 | tf_op jit(solution)/shard_map/concatenate | solution.py:632
  1.2 0.6 own.1
  1.8 4.9 %collective-permute-start.3 = (f32[64,8,128]{2,1,0:T(8,128)S(1)}, f32[64,8,128]{2,1,0:T(8,128)S(1)}, u32[]{:S(2)}, u32[]{:S(2)}) collective-permute-start(f32[64,8,128]{2,1,0:T(8,128)S(1)} %get-tuple-element.19), channel_id=1, source_target_pairs={{8,16},{16,8},{24,32},{32,24},{40,48},{48,40},{56,64},{64,56},{72,... | collective-permute-start | bytes 786440 | tf_op jit(solution)/shard_map/ppermute | solution.py:634
  6.7 3.0 %collective-permute-start = (f32[2,16,16,128]{3,2,1,0:T(8,128)}, f32[2,16,16,128]{3,2,1,0:T(8,128)S(1)}, u32[]{:S(2)}, u32[]{:S(2)}) collective-permute-start(f32[2,16,16,128]{3,2,1,0:T(8,128)} %param.5), channel_id=1, source_target_pairs={{0,128},{128,0},{1,129},{129,1},{2,130},{130,2},{3,131},{131,3},{4... | collective-permute-start | bytes 786440 | tf_op jit(solution)/shard_map/ppermute | solution.py:630
  9.7 0.7 collective-permute-start.2
  10.4 4.4 %collective-permute-start.1 = (f32[8,16,128]{2,1,0:T(8,128)S(1)}, f32[8,16,128]{2,1,0:T(8,128)S(1)}, u32[]{:S(2)}, u32[]{:S(2)}) collective-permute-start(f32[8,16,128]{2,1,0:T(8,128)S(1)} %get-tuple-element.17), channel_id=1, source_target_pairs={{0,1},{1,2},{2,3},{3,4},{4,5},{5,6},{6,7},{129,128},{130,129},{131... | collective-permute-start | bytes 196616 | tf_op jit(solution)/shard_map/ppermute | solution.py:635
  14.8 0.0 collective-permute-done.2.cross_ref
  14.8 0.0 collective-permute-done.3.own_far_ref
  14.8 1.9 %collective-permute-done.1.same_ref = f32[8,16,128]{2,1,0:T(8,128)S(1)} collective-permute-done((f32[8,16,128]{2,1,0:T(8,128)S(1)}, f32[8,16,128]{2,1,0:T(8,128)S(1)}, u32[]{:S(2)}, u32[]{:S(2)}) %collective-permute-start.1) | collective-permute-done | bytes 65568 | tf_op jit(solution)/shard_map/ppermute | solution.py:635
  16.7 0.0 collective-permute-done.other_ref
  16.7 0.2 rows.1
  16.9 0.5 collective-permute-start.5
  17.4 3.4 %collective-permute-start.4 = (f32[40,8,128]{2,1,0:T(8,128)S(1)}, f32[40,8,128]{2,1,0:T(8,128)S(1)}, u32[]{:S(2)}, u32[]{:S(2)}) collective-permute-start(f32[40,8,128]{2,1,0:T(8,128)S(1)} %get-tuple-element.23), channel_id=1, source_target_pairs={{8,16},{16,8},{24,32},{32,24},{40,48},{48,40},{56,64},{64,56},{72,... | collective-permute-start | bytes 491528 | tf_op jit(solution)/shard_map/ppermute | solution.py:639
  20.8 3.2 %collective-permute-done.4.far_ref = f32[40,8,128]{2,1,0:T(8,128)S(1)} collective-permute-done((f32[40,8,128]{2,1,0:T(8,128)S(1)}, f32[40,8,128]{2,1,0:T(8,128)S(1)}, u32[]{:S(2)}, u32[]{:S(2)}) %collective-permute-start.4) | collective-permute-done | bytes 163872 | tf_op jit(solution)/shard_map/ppermute | solution.py:639
  24.0 0.0 collective-permute-done.5.near_ref
  24.0 8.5 %main.1 = (f32[256,128]{1,0:T(8,128)S(1)}, f32[4,4,16,24,128]{4,3,2,1,0:T(8,128)S(1)}) custom-call(f32[5,16,16,128]{3,2,1,0:T(8,128)S(1)} %pad_maximum_fusion.held_ref.own_ref, f32[2,16,16,128]{3,2,1,0:T(8,128)S(1)} %collective-permute-done.other_ref, f32[8,16,128]{2,1,0:T(8,128)S(1)} %get-tuple-element.21.border_ref, ...), custom_call_target="tpu_custom_call" | custom-call | flops 50000000 | bytes 5275648 | tf_op jit(solution)/shard_map/main/pallas_call | solution.py:595
  32.5 29.1 %all_to_all.5 = f32[256,1,128]{2,1,0:T(1,128)S(1)} all-to-all(f32[256,1,128]{2,1,0:T(1,128)S(1)} %bitcast.8), channel_id=1, replica_groups=mesh['section'=2,'sx'=16,'sy'=8] {'section','sx','sy'}, dimensions={0} | all-to-all | bytes 262144 | tf_op jit(solution)/shard_map/all_to_all | solution.py:650
  61.6 0.7 %send.1 = (f32[16,16,128]{2,1,0:T(8,128)S(1)}, f32[8,128]{1,0:T(8,128)S(1)}) custom-call(f32[256,128]{1,0:T(8,128)S(1)} %bitcast.7, f32[4,4,16,24,128]{4,3,2,1,0:T(8,128)S(1)} %get-tuple-element.26.sums_ref, f32[2,16,16,128]{3,2,1,0:T(8,128)S(1)} %collective-permute-done.other_ref), custom_call_target="tpu_custom_call" | custom-call | flops 1000000 | bytes 3674112 | tf_op jit(solution)/shard_map/send/pallas_call | solution.py:595
  62.3 0.6 collective-permute-start.6
  62.9 0.2 mine.1.mine_ref
  63.1 5.3 %collective-permute-done.6.other_ref = f32[16,16,128]{2,1,0:T(8,128)S(1)} collective-permute-done((f32[16,16,128]{2,1,0:T(8,128)S(1)}, f32[16,16,128]{2,1,0:T(8,128)S(1)}, u32[]{:S(2)}, u32[]{:S(2)}) %collective-permute-start.6) | collective-permute-done | bytes 131104 | tf_op jit(solution)/shard_map/ppermute | solution.py:652
  68.3 0.8 %join.1 = f32[2,16,16,128]{3,2,1,0:T(8,128)} custom-call(f32[2,16,16,128]{3,2,1,0:T(8,128)S(1)} %mine.1.mine_ref, f32[16,16,128]{2,1,0:T(8,128)S(1)} %collective-permute-done.6.other_ref), custom_call_target="tpu_custom_call" | custom-call | flops 1000000 | bytes 655360 | tf_op jit(solution)/shard_map/join/pallas_call | solution.py:595
Async XLA Ops:
  1.8 13.0 %collective-permute-start.3 = (f32[64,8,128]{2,1,0:T(8,128)S(1)}, f32[64,8,128]{2,1,0:T(8,128)S(1)}, u32[]{:S(2)}, u32[]{:S(2)}) collective-permute-start(f32[64,8,128]{2,1,0:T(8,128)S(1)} %get-tuple-element.19), channel_id=1, source_target_pairs={{8,16},{16,8},{24,32},{32,24},{40,48},{48,40},{56,64},{64,56},{72,... | collective-permute-start | bytes 786440 | tf_op jit(solution)/shard_map/ppermute | solution.py:634
  6.7 9.9 %collective-permute-start = (f32[2,16,16,128]{3,2,1,0:T(8,128)}, f32[2,16,16,128]{3,2,1,0:T(8,128)S(1)}, u32[]{:S(2)}, u32[]{:S(2)}) collective-permute-start(f32[2,16,16,128]{3,2,1,0:T(8,128)} %param.5), channel_id=1, source_target_pairs={{0,128},{128,0},{1,129},{129,1},{2,130},{130,2},{3,131},{131,3},{4... | collective-permute-start | bytes 786440 | tf_op jit(solution)/shard_map/ppermute | solution.py:630
  9.7 5.1 %collective-permute-start.2 = (f32[8,16,128]{2,1,0:T(8,128)S(1)}, f32[8,16,128]{2,1,0:T(8,128)S(1)}, u32[]{:S(2)}, u32[]{:S(2)}) collective-permute-start(f32[8,16,128]{2,1,0:T(8,128)S(1)} %get-tuple-element.18), channel_id=1, source_target_pairs={{1,128},{2,129},{3,130},{4,131},{5,132},{6,133},{7,134},{128,1},{1... | collective-permute-start | bytes 196616 | tf_op jit(solution)/shard_map/ppermute | solution.py:636
  10.4 6.3 %collective-permute-start.1 = (f32[8,16,128]{2,1,0:T(8,128)S(1)}, f32[8,16,128]{2,1,0:T(8,128)S(1)}, u32[]{:S(2)}, u32[]{:S(2)}) collective-permute-start(f32[8,16,128]{2,1,0:T(8,128)S(1)} %get-tuple-element.17), channel_id=1, source_target_pairs={{0,1},{1,2},{2,3},{3,4},{4,5},{5,6},{6,7},{129,128},{130,129},{131... | collective-permute-start | bytes 196616 | tf_op jit(solution)/shard_map/ppermute | solution.py:635
  16.9 7.1 %collective-permute-start.5 = (f32[72,16,128]{2,1,0:T(8,128)S(1)}, f32[72,16,128]{2,1,0:T(8,128)S(1)}, u32[]{:S(2)}, u32[]{:S(2)}) collective-permute-start(f32[72,16,128]{2,1,0:T(8,128)S(1)} %get-tuple-element.24), channel_id=1, source_target_pairs={{0,8},{8,0},{16,24},{24,16},{32,40},{40,32},{48,56},{56,48},{64,72... | collective-permute-start | bytes 1769480 | tf_op jit(solution)/shard_map/ppermute | solution.py:640
  17.4 6.6 %collective-permute-start.4 = (f32[40,8,128]{2,1,0:T(8,128)S(1)}, f32[40,8,128]{2,1,0:T(8,128)S(1)}, u32[]{:S(2)}, u32[]{:S(2)}) collective-permute-start(f32[40,8,128]{2,1,0:T(8,128)S(1)} %get-tuple-element.23), channel_id=1, source_target_pairs={{8,16},{16,8},{24,32},{32,24},{40,48},{48,40},{56,64},{64,56},{72,... | collective-permute-start | bytes 491528 | tf_op jit(solution)/shard_map/ppermute | solution.py:639
  62.3 6.1 %collective-permute-start.6 = (f32[16,16,128]{2,1,0:T(8,128)S(1)}, f32[16,16,128]{2,1,0:T(8,128)S(1)}, u32[]{:S(2)}, u32[]{:S(2)}) collective-permute-start(f32[16,16,128]{2,1,0:T(8,128)S(1)} %get-tuple-element.28), channel_id=1, source_target_pairs={{0,128},{128,0},{1,129},{129,1},{2,130},{130,2},{3,131},{131,3},{4... | collective-permute-start | bytes 393224 | tf_op jit(solution)/shard_map/ppermute | solution.py:652

commit v15 on v14

--- a/solution.py
+++ b/solution.py
@@ -371,7 +371,7 @@
                     ref[f, z + 1, 0:FIRST] = zero_rows
                     ref[f, z + 1, LAST:ROWS] = zero_rows
 
-    each_plane(nz // 2, 1, assemble)
+    each_plane(nz // 2, 2, assemble)
 
     def pick(matrix, m, j):
         return jnp.where(section == 0, jnp.float32(matrix[m][j]), jnp.float32(matrix[m][(j + 2) % 4]))

time: 69.4 us -> 69.1 us (level)
  no operation moved by 1% of the time
where the time goes in v15:
time: 69.1 us; the launch traced here: 68.8 us
  blocking collectives  29.1 us (42%)
  starting transfers between devices  17.4 us (25%)
  Pallas kernels  10.7 us (15%)
  waiting for transfers between devices  10.4 us (15%)
  other arithmetic  1.2 us (2%)
    all_to_all x1, blocking collectives, body(): lax.all_to_all(part.reshape(peers, 1, LANES), axes, 0, 0)  29.1 us
    pallas_call x6, Pallas kernels, run(): pl.pallas_call(kernel, out_shape=shapes if many else shapes[0], in_specs=...  10.7 us
    ppermute x1, waiting for transfers between devices, body(): got = lax.ppermute(half, 'section', partner)  5.26 us
    ppermute x1, starting transfers between devices, body(): own_far = lax.ppermute(own_far, 'sx', swaps(rows, 1))  4.94 us
    ppermute x1, starting transfers between devices, body(): same = lax.ppermute(same, ('section', 'sy'), beside(columns, False))  4.39 us
    ppermute x1, starting transfers between devices, body(): far = lax.ppermute(far, 'sx', swaps(rows, 1))  3.37 us
    ppermute x1, waiting for transfers between devices, body(): far = lax.ppermute(far, 'sx', swaps(rows, 1))  3.24 us
    ppermute x1, starting transfers between devices, body(): other = lax.ppermute(sections, 'section', partner)  3 us
  transfers between devices with their start and end apart: 7, of which 3 were waited for; matrix products, arithmetic and copies ran while one was open for 0% of the time, Pallas kernels for 0%

profile of v15, /device:TPU:1, one launch (start us, length us, event | category | flops | bytes accessed | tf_op | source)
XLA Modules:
  0.0 68.8 jit_solution(17109436843551774912)
XLA Ops:
  0.0 1.2 %pad_maximum_fusion.held_ref.own_ref = f32[5,16,16,128]{3,2,1,0:T(8,128)S(1)} fusion(f32[1,16,16,128]{3,2,1,0:T(8,128)} %bitcast.9, f32[1,16,16,128]{3,2,1,0:T(8,128)} %bitcast.10, f32[1,16,16,128]{3,2,1,0:T(8,128)} %bitcast.11, f32[2,16,16,128]{3,2,1,0:T(8,128)} %param.5), kind=kLoop, calls=%fused_computation | loop fusion | flops 491520 | bytes 1310720 | tf_op jit(solution)/shard_map/concatenate | solution.py:632
  1.2 0.6 own.1
  1.8 4.9 %collective-permute-start.3 = (f32[64,8,128]{2,1,0:T(8,128)S(1)}, f32[64,8,128]{2,1,0:T(8,128)S(1)}, u32[]{:S(2)}, u32[]{:S(2)}) collective-permute-start(f32[64,8,128]{2,1,0:T(8,128)S(1)} %get-tuple-element.19), channel_id=1, source_target_pairs={{8,16},{16,8},{24,32},{32,24},{40,48},{48,40},{56,64},{64,56},{72,... | collective-permute-start | bytes 786440 | tf_op jit(solution)/shard_map/ppermute | solution.py:634
  6.7 3.0 %collective-permute-start = (f32[2,16,16,128]{3,2,1,0:T(8,128)}, f32[2,16,16,128]{3,2,1,0:T(8,128)S(1)}, u32[]{:S(2)}, u32[]{:S(2)}) collective-permute-start(f32[2,16,16,128]{3,2,1,0:T(8,128)} %param.5), channel_id=1, source_target_pairs={{0,128},{128,0},{1,129},{129,1},{2,130},{130,2},{3,131},{131,3},{4... | collective-permute-start | bytes 786440 | tf_op jit(solution)/shard_map/ppermute | solution.py:630
  9.7 0.7 collective-permute-start.2
  10.4 4.4 %collective-permute-start.1 = (f32[8,16,128]{2,1,0:T(8,128)S(1)}, f32[8,16,128]{2,1,0:T(8,128)S(1)}, u32[]{:S(2)}, u32[]{:S(2)}) collective-permute-start(f32[8,16,128]{2,1,0:T(8,128)S(1)} %get-tuple-element.17), channel_id=1, source_target_pairs={{0,1},{1,2},{2,3},{3,4},{4,5},{5,6},{6,7},{129,128},{130,129},{131... | collective-permute-start | bytes 196616 | tf_op jit(solution)/shard_map/ppermute | solution.py:635
  14.8 0.0 collective-permute-done.2.cross_ref
  14.8 0.0 collective-permute-done.3.own_far_ref
  14.8 1.9 %collective-permute-done.1.same_ref = f32[8,16,128]{2,1,0:T(8,128)S(1)} collective-permute-done((f32[8,16,128]{2,1,0:T(8,128)S(1)}, f32[8,16,128]{2,1,0:T(8,128)S(1)}, u32[]{:S(2)}, u32[]{:S(2)}) %collective-permute-start.1) | collective-permute-done | bytes 65568 | tf_op jit(solution)/shard_map/ppermute | solution.py:635
  16.7 0.0 collective-permute-done.other_ref
  16.7 0.2 rows.1
  16.9 0.5 collective-permute-start.5
  17.4 3.4 %collective-permute-start.4 = (f32[40,8,128]{2,1,0:T(8,128)S(1)}, f32[40,8,128]{2,1,0:T(8,128)S(1)}, u32[]{:S(2)}, u32[]{:S(2)}) collective-permute-start(f32[40,8,128]{2,1,0:T(8,128)S(1)} %get-tuple-element.23), channel_id=1, source_target_pairs={{8,16},{16,8},{24,32},{32,24},{40,48},{48,40},{56,64},{64,56},{72,... | collective-permute-start | bytes 491528 | tf_op jit(solution)/shard_map/ppermute | solution.py:639
  20.8 3.2 %collective-permute-done.4.far_ref = f32[40,8,128]{2,1,0:T(8,128)S(1)} collective-permute-done((f32[40,8,128]{2,1,0:T(8,128)S(1)}, f32[40,8,128]{2,1,0:T(8,128)S(1)}, u32[]{:S(2)}, u32[]{:S(2)}) %collective-permute-start.4) | collective-permute-done | bytes 163872 | tf_op jit(solution)/shard_map/ppermute | solution.py:639
  24.0 0.0 collective-permute-done.5.near_ref
  24.0 8.2 %main.1 = (f32[256,128]{1,0:T(8,128)S(1)}, f32[4,4,16,24,128]{4,3,2,1,0:T(8,128)S(1)}) custom-call(f32[5,16,16,128]{3,2,1,0:T(8,128)S(1)} %pad_maximum_fusion.held_ref.own_ref, f32[2,16,16,128]{3,2,1,0:T(8,128)S(1)} %collective-permute-done.other_ref, f32[8,16,128]{2,1,0:T(8,128)S(1)} %get-tuple-element.21.border_ref, ...), custom_call_target="tpu_custom_call" | custom-call | flops 50000000 | bytes 5275648 | tf_op jit(solution)/shard_map/main/pallas_call | solution.py:595
  32.2 29.1 %all_to_all.5 = f32[256,1,128]{2,1,0:T(1,128)S(1)} all-to-all(f32[256,1,128]{2,1,0:T(1,128)S(1)} %bitcast.8), channel_id=1, replica_groups=mesh['section'=2,'sx'=16,'sy'=8] {'section','sx','sy'}, dimensions={0} | all-to-all | bytes 262144 | tf_op jit(solution)/shard_map/all_to_all | solution.py:650
  61.3 0.7 %send.1 = (f32[16,16,128]{2,1,0:T(8,128)S(1)}, f32[8,128]{1,0:T(8,128)S(1)}) custom-call(f32[256,128]{1,0:T(8,128)S(1)} %bitcast.7, f32[4,4,16,24,128]{4,3,2,1,0:T(8,128)S(1)} %get-tuple-element.26.sums_ref, f32[2,16,16,128]{3,2,1,0:T(8,128)S(1)} %collective-permute-done.other_ref), custom_call_target="tpu_custom_call" | custom-call | flops 1000000 | bytes 3674112 | tf_op jit(solution)/shard_map/send/pallas_call | solution.py:595
  62.0 0.6 collective-permute-start.6
  62.5 0.2 mine.1.mine_ref
  62.8 5.3 %collective-permute-done.6.other_ref = f32[16,16,128]{2,1,0:T(8,128)S(1)} collective-permute-done((f32[16,16,128]{2,1,0:T(8,128)S(1)}, f32[16,16,128]{2,1,0:T(8,128)S(1)}, u32[]{:S(2)}, u32[]{:S(2)}) %collective-permute-start.6) | collective-permute-done | bytes 131104 | tf_op jit(solution)/shard_map/ppermute | solution.py:652
  68.0 0.8 %join.1 = f32[2,16,16,128]{3,2,1,0:T(8,128)} custom-call(f32[2,16,16,128]{3,2,1,0:T(8,128)S(1)} %mine.1.mine_ref, f32[16,16,128]{2,1,0:T(8,128)S(1)} %collective-permute-done.6.other_ref), custom_call_target="tpu_custom_call" | custom-call | flops 1000000 | bytes 655360 | tf_op jit(solution)/shard_map/join/pallas_call | solution.py:595
Async XLA Ops:
  1.8 13.0 %collective-permute-start.3 = (f32[64,8,128]{2,1,0:T(8,128)S(1)}, f32[64,8,128]{2,1,0:T(8,128)S(1)}, u32[]{:S(2)}, u32[]{:S(2)}) collective-permute-start(f32[64,8,128]{2,1,0:T(8,128)S(1)} %get-tuple-element.19), channel_id=1, source_target_pairs={{8,16},{16,8},{24,32},{32,24},{40,48},{48,40},{56,64},{64,56},{72,... | collective-permute-start | bytes 786440 | tf_op jit(solution)/shard_map/ppermute | solution.py:634
  6.7 9.9 %collective-permute-start = (f32[2,16,16,128]{3,2,1,0:T(8,128)}, f32[2,16,16,128]{3,2,1,0:T(8,128)S(1)}, u32[]{:S(2)}, u32[]{:S(2)}) collective-permute-start(f32[2,16,16,128]{3,2,1,0:T(8,128)} %param.5), channel_id=1, source_target_pairs={{0,128},{128,0},{1,129},{129,1},{2,130},{130,2},{3,131},{131,3},{4... | collective-permute-start | bytes 786440 | tf_op jit(solution)/shard_map/ppermute | solution.py:630
  9.7 5.1 %collective-permute-start.2 = (f32[8,16,128]{2,1,0:T(8,128)S(1)}, f32[8,16,128]{2,1,0:T(8,128)S(1)}, u32[]{:S(2)}, u32[]{:S(2)}) collective-permute-start(f32[8,16,128]{2,1,0:T(8,128)S(1)} %get-tuple-element.18), channel_id=1, source_target_pairs={{1,128},{2,129},{3,130},{4,131},{5,132},{6,133},{7,134},{128,1},{1... | collective-permute-start | bytes 196616 | tf_op jit(solution)/shard_map/ppermute | solution.py:636
  10.4 6.3 %collective-permute-start.1 = (f32[8,16,128]{2,1,0:T(8,128)S(1)}, f32[8,16,128]{2,1,0:T(8,128)S(1)}, u32[]{:S(2)}, u32[]{:S(2)}) collective-permute-start(f32[8,16,128]{2,1,0:T(8,128)S(1)} %get-tuple-element.17), channel_id=1, source_target_pairs={{0,1},{1,2},{2,3},{3,4},{4,5},{5,6},{6,7},{129,128},{130,129},{131... | collective-permute-start | bytes 196616 | tf_op jit(solution)/shard_map/ppermute | solution.py:635
  16.9 7.1 %collective-permute-start.5 = (f32[72,16,128]{2,1,0:T(8,128)S(1)}, f32[72,16,128]{2,1,0:T(8,128)S(1)}, u32[]{:S(2)}, u32[]{:S(2)}) collective-permute-start(f32[72,16,128]{2,1,0:T(8,128)S(1)} %get-tuple-element.24), channel_id=1, source_target_pairs={{0,8},{8,0},{16,24},{24,16},{32,40},{40,32},{48,56},{56,48},{64,72... | collective-permute-start | bytes 1769480 | tf_op jit(solution)/shard_map/ppermute | solution.py:640
  17.4 6.6 %collective-permute-start.4 = (f32[40,8,128]{2,1,0:T(8,128)S(1)}, f32[40,8,128]{2,1,0:T(8,128)S(1)}, u32[]{:S(2)}, u32[]{:S(2)}) collective-permute-start(f32[40,8,128]{2,1,0:T(8,128)S(1)} %get-tuple-element.23), channel_id=1, source_target_pairs={{8,16},{16,8},{24,32},{32,24},{40,48},{48,40},{56,64},{64,56},{72,... | collective-permute-start | bytes 491528 | tf_op jit(solution)/shard_map/ppermute | solution.py:639
  62.0 6.1 %collective-permute-start.6 = (f32[16,16,128]{2,1,0:T(8,128)S(1)}, f32[16,16,128]{2,1,0:T(8,128)S(1)}, u32[]{:S(2)}, u32[]{:S(2)}) collective-permute-start(f32[16,16,128]{2,1,0:T(8,128)S(1)} %get-tuple-element.28), channel_id=1, source_target_pairs={{0,128},{128,0},{1,129},{129,1},{2,130},{130,2},{3,131},{131,3},{4... | collective-permute-start | bytes 393224 | tf_op jit(solution)/shard_map/ppermute | solution.py:652
